TPU v7x, 512 devices: a whole 4x4x16 slice. The times are simulated.
512 devices in a mesh: clu: 64 (over z, y), col: 8 (over x, core).
Axes of the slice: x: 4, y: 4, z: 16, core: 2. Of those that a mesh axis runs over, the one named last changes fastest.
Arguments:
- near_blocks: float32 [64, 16, 512, 512], P('clu', 'col'), may hold values from -0.25 to 0.25
- diag_block: float32 [64, 512, 512], P('clu', 'col'), as said below
- bases: float32 [64, 512, 512], P('clu', 'col'), as said below
- near_index: int32 [64, 16], replicated, may hold values from 0 to 63, as said below
- near_mask: int32 [64, 16], P('clu'), may hold values from 0 to 1
- parent_map: int32 [64], replicated, may hold values from 0 to 31, as said below
Outputs:
- coupling: float32 [64, 16, 256, 256], P('clu', 'col')
- parent_rows: float32 [64, 256, 512], P('clu', 'col')
- redundant_factor: float32 [64, 256, 256], P('clu', 'col')
Inputs may be any that keep to these rules, and one draw needn't show every extreme that they name: `parent_map`: every parent has exactly two children. `near_index`: the slots of cluster i name the clusters (i + d) mod 64 for d = 1 to 7, d = 32 and d = -1 to -8, each offset in exactly one slot, in an order drawn per row; live slots name distinct clusters; exactly one live slot names the cluster's sibling. `diag_block`: each block is symmetric and positive definite. `bases`: each basis change is invertible.
All inputs are finite; a program needn't handle non-finite values.
Results may differ from a plain program's by a relative error of at most 0.0003.
Values sent between devices are 32-bit elements; how exact they have to be, the bound alone decides.
No kernel may reach another device: no remote copies, remote signals or barrier semaphores. Data moves between devices by JAX's collectives and lax.ppermute only.
A program may use at most 64 MiB of HBM per device.

v0:
```python
import jax
import jax.numpy as jnp
from jax import lax
from jax.experimental import pallas as pl
from jax.experimental.pallas import tpu as pltpu
from jax.sharding import PartitionSpec as P


RANK = 256
HALF = 128
F32 = jnp.float32
BF16 = jnp.bfloat16
VMEM = pl.BlockSpec(memory_space=pltpu.VMEM)
SMEM = pl.BlockSpec(memory_space=pltpu.SMEM)
ANY = pl.BlockSpec(memory_space=pl.ANY)
HBM = pl.BlockSpec(memory_space=pltpu.HBM)


def dot_full(a, b, dims=((1,), (0,))):
    return lax.dot_general(
        a, b, (dims, ((), ())), precision=lax.Precision.HIGHEST, preferred_element_type=F32
    )


def split2(x):
    high = x.astype(BF16)
    return high, (x - high.astype(F32)).astype(BF16)


def dot3(a, b, dims=((1,), (0,))):
    def one(x, y):
        return lax.dot_general(x, y, (dims, ((), ())), preferred_element_type=F32)

    return one(a[0], b[0]) + (one(a[0], b[1]) + one(a[1], b[0]))


def split3(x):
    high = x.astype(BF16)
    rest = x - high.astype(F32)
    mid = rest.astype(BF16)
    return high, mid, (rest - mid.astype(F32)).astype(BF16)


def factor_half(work, upper):
    sub = lax.broadcasted_iota(jnp.int32, (8, HALF), 0)

    def spread_lane(x, j):
        return jnp.broadcast_to(x[:, j : j + 1], (8, HALF))

    def spread_row(x, m):
        return jnp.broadcast_to(x[m : m + 1, :], (8, HALF))

    rows_a, rows_w = work[0:8, :HALF], work[0:8, HALF:]
    for group in range(HALF // 8):
        base = 8 * group
        columns = [spread_lane(rows_a, base + j) for j in range(8)]
        cell = {(m, j): spread_row(columns[j], m) for j in range(8) for m in range(j, 8)}
        inv = [None] * 8
        ratio = {}
        for k in range(8):
            inv[k] = 1.0 / cell[k, k]
            for m in range(k + 1, 8):
                ratio[m, k] = cell[m, k] * inv[k]
            for j in range(k + 1, 8):
                for m in range(j, 8):
                    cell[m, j] = cell[m, j] - ratio[m, k] * cell[j, k]
        ra = [spread_row(rows_a, m) for m in range(8)]
        rw = [spread_row(rows_w, m) for m in range(8)]
        for m in range(8):
            for k in range(m):
                ra[m] = ra[m] - ratio[m, k] * ra[k]
                rw[m] = rw[m] - ratio[m, k] * rw[k]
        ua = uw = None
        for m in range(8):
            scale = lax.rsqrt(cell[m, m])
            a, w = ra[m] * scale, rw[m] * scale
            ua = a if ua is None else jnp.where(sub == m, a, ua)
            uw = w if uw is None else jnp.where(sub == m, w, uw)
        upper[base : base + 8, :HALF] = ua
        upper[base : base + 8, HALF:] = uw
        after = base + 8
        if after == HALF:
            break
        next_a, next_w = work[after : after + 8, :HALF], work[after : after + 8, HALF:]
        lead = [spread_lane(next_a, base + k) for k in range(8)]
        for k in range(8):
            for j in range(k):
                lead[k] = lead[k] - lead[j] * ratio[k, j]
        for k in range(8):
            factor = lead[k] * inv[k]
            next_a = next_a - factor * ra[k]
            next_w = next_w - factor * rw[k]
        rows_a, rows_w = next_a, next_w
        low = after + 8
        if low < HALF:
            h, m, l = (x.astype(F32) for x in split3(jnp.concatenate([ua, uw], axis=1)))
            ha, ma, la = h[:, :HALF], m[:, :HALF], l[:, :HALF]
            left = jnp.concatenate([ha, ha, ma, ha, la, ma], axis=0).astype(BF16)
            right = jnp.concatenate([h, m, h, l, h, m], axis=0).astype(BF16)
            step = lax.dot_general(left, right, (((0,), (0,)), ((), ())), preferred_element_type=F32)
            work[low:, :] = work[low:, :] - step[low:, :]


def params(mib):
    return pltpu.CompilerParams(vmem_limit_bytes=mib * 2**20)


def slice_kernel(bases_ref, skeleton_ref, sem):
    source = bases_ref.at[:, pl.ds(bases_ref.shape[1] - RANK, RANK)]
    run_copies([pltpu.make_async_copy(source, skeleton_ref, sem)])


def run_copies(copies):
    for copy in copies:
        copy.start()
    for copy in copies:
        copy.wait()


def spread_kernel(diag_ref, bases_ref, out_ref, sem):
    rows = diag_ref.shape[0]
    copies = []
    for p in range(out_ref.shape[0]):
        for q, ref in enumerate((diag_ref, bases_ref)):
            target = out_ref.at[p, pl.ds(q * rows, rows)]
            copies.append(pltpu.make_async_copy(ref, target, sem.at[p, q]))
    run_copies(copies)


def order_kernel(own_ref, index_ref, near0, near1, near2, near3, far, out_ref, slot_of, sem):
    own = own_ref[0]
    clusters, slots = index_ref.shape
    for k in range(slots):
        offset = (index_ref[own, k] - own + clusters + slots // 2) % clusters
        slot_of[jnp.where(offset < slots, offset, slots // 2)] = k
    copies = []
    for d in range(slots):
        stack = (near0, near1, near2, near3)[d % 4]
        source = far if d == slots // 2 else stack.at[(0, 2, 1, 3)[d // 4]]
        slot = slot_of[d]
        copies.append(pltpu.make_async_copy(source, out_ref.at[slot // 2, slot % 2], sem.at[d]))
    run_copies(copies)


def factor_kernel(column_ref, db_ref, solve_ref, schur_ref, factor_ref, work, upper1, upper2, full):
    rows = db_ref.shape[1] // 2
    size = db_ref.shape[0] * rows
    diag = db_ref[:, :rows, :].reshape(size, size)
    basis = db_ref[:, rows:, :].reshape(size, size)
    half = dot_full(diag, basis)
    first = ((0,), (0,))
    reduced = dot_full(half, basis, first)
    red = size - RANK
    ri = lax.broadcasted_iota(jnp.int32, (HALF, HALF), 0)
    ci = lax.broadcasted_iota(jnp.int32, (HALF, HALF), 1)
    eye = (ri == ci).astype(F32)
    work[:, :HALF] = reduced[:HALF, :HALF]
    work[:, HALF:] = eye
    factor_half(work, upper1)
    inv1 = upper1[:, HALF:]
    top = dot_full(inv1, reduced[:HALF, HALF:])
    low_t = top[:, :HALF]
    rest = reduced[HALF:red, HALF:] - dot_full(low_t, top, first)
    work[:, :HALF] = rest[:, :HALF]
    work[:, HALF:] = eye
    factor_half(work, upper2)
    inv2 = upper2[:, HALF:]
    couple1 = top[:, HALF:]
    joint = dot_full(inv2, jnp.concatenate([rest[:, HALF:], dot_full(low_t, inv1, first)], axis=1))
    couple2, cross = joint[:, :RANK], joint[:, RANK:]
    solve_ref[:HALF, :] = dot_full(inv1, couple1, first) - dot_full(cross, couple2, first)
    solve_ref[HALF:, :] = dot_full(inv2, couple2, first)
    column = column_ref[0]
    count = schur_ref.shape[0]
    start = pl.multiple_of(column * count, count)
    full[...] = reduced[red:, red:] - (
        dot_full(couple1, couple1, first) + dot_full(couple2, couple2, first)
    )
    schur_ref[...] = full[pl.ds(start, count), :]
    full[:HALF, :HALF] = jnp.where(ri >= ci, upper1[:, :HALF].T, 0.0)
    full[HALF:, :HALF] = low_t.T
    full[:HALF, HALF:] = jnp.zeros((HALF, HALF), F32)
    full[HALF:, HALF:] = jnp.where(ri >= ci, upper2[:, :HALF].T, 0.0)
    factor_ref[...] = full[pl.ds(start, count), :]


def find_sibling(own, parent_ref):
    parent = parent_ref[own]

    def step(i, found):
        return jnp.where((parent_ref[i] == parent) & (i != own), i, found)

    return lax.fori_loop(0, parent_ref.shape[0], step, jnp.int32(0), unroll=True)


def couple_kernel(
    place_ref, index_ref, mask_ref, parent_ref, near_ref, routed_ref, db_ref, solve_ref, out_ref, side_ref, block, sem
):
    loads = [pltpu.make_async_copy(near_ref.at[k], block.at[k], sem.at[k]) for k in range(near_ref.shape[0])]
    for load in loads:
        load.start()
    own, column = place_ref[0], place_ref[1]
    sibling = find_sibling(own, parent_ref)
    rows = db_ref.shape[1] // 2
    size = db_ref.shape[0] * rows
    red = size - RANK
    basis = db_ref[:, rows:, :].reshape(size, size)
    lift = basis[:, red:] - dot_full(basis[:, :red], solve_ref[...])
    lift2 = split2(lift)
    side = jnp.zeros((RANK, RANK), F32)
    for k in range(near_ref.shape[0]):
        slot = column * near_ref.shape[0] + k
        partner = routed_ref[:, k].reshape(size, RANK)
        loads[k].wait()
        middle = dot3(split2(block[k]), split2(partner))
        live = mask_ref[0, slot].astype(F32)
        coupling = dot3(lift2, split2(middle), ((0,), (0,))) * live
        out_ref[k] = coupling
        match = jnp.where(index_ref[own, slot] == sibling, live, 0.0)
        side = side + match * coupling
    side_ref[...] = side.reshape(side_ref.shape)


def merge_kernel(place_ref, parent_ref, parts_ref, schur_ref, out_ref):
    own = place_ref[0]
    first = own < find_sibling(own, parent_ref)
    side = parts_ref[0]
    for p in range(1, parts_ref.shape[0]):
        side = side + parts_ref[p]
    schur = schur_ref[...]
    out_ref[:, :RANK] = jnp.where(first, schur, side)
    out_ref[:, RANK:] = jnp.where(first, side, schur)


def shards(near_blocks, diag_block, bases, near_index, near_mask, parent_map):
    columns = lax.axis_size("col")
    clusters = lax.axis_size("clu")
    column = lax.axis_index("col").astype(jnp.int32)
    own = lax.axis_index("clu").astype(jnp.int32)
    place = jnp.stack([own, column])
    rows, size = bases.shape[1:]
    per_device = near_blocks.shape[1]
    shape = jax.ShapeDtypeStruct

    def shift(x, d):
        return lax.ppermute(x, "clu", [((i + d) % clusters, i) for i in range(clusters)])

    skeleton = pl.pallas_call(
        slice_kernel,
        out_shape=shape((rows, RANK), F32),
        in_specs=[HBM],
        out_specs=VMEM,
        scratch_shapes=[pltpu.SemaphoreType.DMA],
        compiler_params=params(4),
        name="skeleton",
    )(pltpu.with_memory_space_constraint(bases[0], pltpu.HBM))
    down8 = shift(skeleton, -8)
    far = shift(skeleton, clusters // 2)
    pair = jnp.stack([down8, skeleton])
    up4 = shift(pair, 4)
    spread = pl.pallas_call(
        spread_kernel,
        out_shape=pltpu.HBM((columns, 2 * rows, size), F32),
        in_specs=[VMEM] * 2,
        out_specs=HBM,
        scratch_shapes=[pltpu.SemaphoreType.DMA((columns, 2))],
        compiler_params=params(4),
        name="spread",
    )(diag_block[0], bases[0])
    db = lax.all_to_all(spread, "col", split_axis=0, concat_axis=0, tiled=False)
    near0 = jnp.concatenate([pair, up4], axis=0)
    near1 = shift(near0, 1)
    near2 = shift(near0, 2)
    near3 = shift(near0, 3)
    ordered = pl.pallas_call(
        order_kernel,
        out_shape=pltpu.HBM((columns, per_device, rows, RANK), F32),
        in_specs=[SMEM] * 2 + [ANY] * 5,
        out_specs=HBM,
        compiler_params=params(2),
        scratch_shapes=[
            pltpu.SMEM((near_index.shape[1],), jnp.int32),
            pltpu.SemaphoreType.DMA((near_index.shape[1],)),
        ],
        name="order",
    )(own[None], near_index, near0, near1, near2, near3, far)
    routed = lax.all_to_all(ordered, "col", split_axis=0, concat_axis=0, tiled=False)
    count = RANK // columns
    solve, schur, factor = pl.pallas_call(
        factor_kernel,
        out_shape=(
            shape((size - RANK, RANK), F32),
            shape((count, RANK), F32),
            shape(((size - RANK) // columns, size - RANK), F32),
        ),
        in_specs=[SMEM, VMEM],
        out_specs=(VMEM,) * 3,
        scratch_shapes=[pltpu.VMEM((HALF, 2 * HALF), F32)] * 3 + [pltpu.VMEM((RANK, RANK), F32)],
        cost_estimate=pl.CostEstimate(flops=6_000_000_000, bytes_accessed=4_000_000, transcendentals=0),
        compiler_params=params(24),
        name="factor",
    )(column[None], db)
    coupling, side = pl.pallas_call(
        couple_kernel,
        out_shape=(shape((per_device, RANK, RANK), F32), shape((columns, count, RANK), F32)),
        in_specs=[SMEM] * 4 + [HBM] + [VMEM] * 3,
        out_specs=(VMEM,) * 2,
        scratch_shapes=[
            pltpu.VMEM(near_blocks.shape[1:], F32),
            pltpu.SemaphoreType.DMA((per_device,)),
        ],
        compiler_params=params(24),
        name="couple",
    )(
        place,
        near_index,
        near_mask,
        parent_map,
        pltpu.with_memory_space_constraint(near_blocks[0], pltpu.HBM),
        routed,
        db,
        solve,
    )
    parts = lax.all_to_all(side, "col", split_axis=0, concat_axis=0, tiled=False)
    parent_rows = pl.pallas_call(
        merge_kernel,
        out_shape=shape((count, 2 * RANK), F32),
        in_specs=[SMEM] * 2 + [VMEM] * 2,
        out_specs=VMEM,
        compiler_params=params(4),
        name="merge",
    )(place, parent_map, parts, schur)
    return coupling[None], parent_rows[None], factor[None]


def solution(mesh):
    in_specs = (
        P("clu", "col", None, None),
        P("clu", "col", None),
        P("clu", "col", None),
        P(),
        P("clu", None),
        P(),
    )
    out_specs = (P("clu", "col", None, None), P("clu", "col", None), P("clu", "col", None))
    return jax.shard_map(shards, mesh=mesh, in_specs=in_specs, out_specs=out_specs, check_vma=False)
```

profile of v0, /device:TPU:32, one launch (start us, length us, event | category | flops | bytes accessed | tf_op | source)
XLA Modules:
  0.0 105.5 jit_solution(6981555476942268605)
XLA Ops:
  0.6 0.0 copy-start
  0.6 0.9 copy-done
  1.5 0.0 copy-start.1
  1.5 0.9 copy-done.1
  2.4 1.5 %spread.1 = f32[8,128,512]{2,1,0:T(8,128)} custom-call(f32[64,512]{1,0:T(8,128)S(1)} %bitcast.14, f32[64,512]{1,0:T(8,128)S(1)} %bitcast.13), custom_call_target="tpu_custom_call" | custom-call | tf_op jit(solution)/shard_map/spread/pallas_call | solution.py:261
  3.9 0.0 copy-start.4
  3.9 4.3 %all-to-all-start.1 = ((f32[8,128,512]{2,1,0:T(8,128)}), f32[8,128,512]{2,1,0:T(8,128)S(1)}, u32[]{:S(2)}, u32[]{:S(2)}) async-start(f32[8,128,512]{2,1,0:T(8,128)} %spread.1), calls=%async_computation.1 | async-start | bytes 4194304 | tf_op jit(solution)/shard_map/all_to_all | solution.py:270
  8.2 0.8 skeleton.1
  9.1 5.2 %collective-permute-start = (f32[64,256]{1,0:T(8,128)S(1)}, f32[64,256]{1,0:T(8,128)S(1)}, u32[]{:S(2)}, u32[]{:S(2)}) collective-permute-start(f32[64,256]{1,0:T(8,128)S(1)} %skeleton.1), channel_id=1, source_target_pairs={{448,0},{456,8},{464,16},{472,24},{480,32},{488,40},{496,48},{504,... | collective-permute-start | bytes 196616 | tf_op jit(solution)/shard_map/ppermute | solution.py:246
  14.3 9.9 %collective-permute-done = f32[64,256]{1,0:T(8,128)S(1)} collective-permute-done((f32[64,256]{1,0:T(8,128)S(1)}, f32[64,256]{1,0:T(8,128)S(1)}, u32[]{:S(2)}, u32[]{:S(2)}) %collective-permute-start) | collective-permute-done | bytes 65568 | tf_op jit(solution)/shard_map/ppermute | solution.py:246
  24.2 1.9 %collective-permute-start.1 = (f32[2,64,256]{2,1,0:T(8,128)S(1)}, f32[2,64,256]{2,1,0:T(8,128)S(1)}, u32[]{:S(2)}, u32[]{:S(2)}) collective-permute-start(f32[2,64,256]{2,1,0:T(8,128)S(1)} %pad_maximum_fusion.1), channel_id=1, source_target_pairs={{32,0},{40,8},{48,16},{56,24},{64,32},{72,40},{80,48},{88,56},{96,... | collective-permute-start | bytes 393224 | tf_op jit(solution)/shard_map/ppermute | solution.py:246
  26.1 5.3 %collective-permute-done.1 = f32[2,64,256]{2,1,0:T(8,128)S(1)} collective-permute-done((f32[2,64,256]{2,1,0:T(8,128)S(1)}, f32[2,64,256]{2,1,0:T(8,128)S(1)}, u32[]{:S(2)}, u32[]{:S(2)}) %collective-permute-start.1) | collective-permute-done | bytes 131104 | tf_op jit(solution)/shard_map/ppermute | solution.py:246
  31.5 3.4 %collective-permute-start.4 = (f32[4,64,256]{2,1,0:T(8,128)S(1)}, f32[4,64,256]{2,1,0:T(8,128)S(1)}, u32[]{:S(2)}, u32[]{:S(2)}) collective-permute-start(f32[4,64,256]{2,1,0:T(8,128)S(1)} %pad_maximum_fusion.near0), channel_id=1, source_target_pairs={{24,0},{32,8},{40,16},{48,24},{56,32},{64,40},{72,48},{80,56},{88,... | collective-permute-start | bytes 786440 | tf_op jit(solution)/shard_map/ppermute | solution.py:246
  34.8 7.9 %collective-permute-start.3 = (f32[4,64,256]{2,1,0:T(8,128)S(1)}, f32[4,64,256]{2,1,0:T(8,128)S(1)}, u32[]{:S(2)}, u32[]{:S(2)}) collective-permute-start(f32[4,64,256]{2,1,0:T(8,128)S(1)} %pad_maximum_fusion.near0), channel_id=1, source_target_pairs={{16,0},{24,8},{32,16},{40,24},{48,32},{56,40},{64,48},{72,56},{80,... | collective-permute-start | bytes 786440 | tf_op jit(solution)/shard_map/ppermute | solution.py:246
  42.8 3.3 %collective-permute-start.2 = (f32[4,64,256]{2,1,0:T(8,128)S(1)}, f32[4,64,256]{2,1,0:T(8,128)S(1)}, u32[]{:S(2)}, u32[]{:S(2)}) collective-permute-start(f32[4,64,256]{2,1,0:T(8,128)S(1)} %pad_maximum_fusion.near0), channel_id=1, source_target_pairs={{8,0},{16,8},{24,16},{32,24},{40,32},{48,40},{56,48},{64,56},{72,6... | collective-permute-start | bytes 786440 | tf_op jit(solution)/shard_map/ppermute | solution.py:246
  46.1 7.5 %collective-permute-start.5 = (f32[64,256]{1,0:T(8,128)S(1)}, f32[64,256]{1,0:T(8,128)S(1)}, u32[]{:S(2)}, u32[]{:S(2)}) collective-permute-start(f32[64,256]{1,0:T(8,128)S(1)} %skeleton.1), channel_id=1, source_target_pairs={{256,0},{264,8},{272,16},{280,24},{288,32},{296,40},{304,48},{312,... | collective-permute-start | bytes 196616 | tf_op jit(solution)/shard_map/ppermute | solution.py:246
  53.5 0.0 copy-done.4
  53.5 0.1 copy.10.index_ref
  53.6 11.4 %collective-permute-done.5.far = f32[64,256]{1,0:T(8,128)S(1)} collective-permute-done((f32[64,256]{1,0:T(8,128)S(1)}, f32[64,256]{1,0:T(8,128)S(1)}, u32[]{:S(2)}, u32[]{:S(2)}) %collective-permute-start.5) | collective-permute-done | bytes 65568 | tf_op jit(solution)/shard_map/ppermute | solution.py:246
  65.0 0.0 collective-permute-done.4.near3
  65.0 0.0 collective-permute-done.3.near2
  65.0 0.0 collective-permute-done.2.near1
  65.0 2.3 %order.1 = f32[8,2,64,256]{3,2,1,0:T(8,128)} custom-call(s32[1]{0:T(128)} %bitcast.own_ref, s32[64,16]{1,0:T(8,128)S(1)} %copy.10.index_ref, f32[4,64,256]{2,1,0:T(8,128)S(1)} %pad_maximum_fusion.near0, f32[4,64,256]{2,1,0:T(8,128)S(1)} %collective-permute-done.2.near1, f32[4,64,256]{2,1,0:T(8,128)S(1)} %collective-permute-done.3.near2, ...), custom_call_target="tpu_custom_call" | custom-call | tf_op jit(solution)/shard_map/order/pallas_call | solution.py:275
  67.3 0.0 all-to-all-done.1.db_ref
  67.3 4.2 %all-to-all-start = ((f32[8,2,64,256]{3,2,1,0:T(8,128)}), f32[8,2,64,256]{3,2,1,0:T(8,128)S(1)}, u32[]{:S(2)}, u32[]{:S(2)}) async-start(f32[8,2,64,256]{3,2,1,0:T(8,128)} %order.1), calls=%async_computation | async-start | bytes 2097152 | tf_op jit(solution)/shard_map/all_to_all | solution.py:287
  71.5 0.1 pad_add_fusion.place_ref
  71.6 0.0 copy-start.2
  71.6 0.0 copy-start.3
  71.6 14.4 %factor.1 = (f32[256,256]{1,0:T(8,128)S(1)}, f32[32,256]{1,0:T(8,128)S(1)}, f32[32,256]{1,0:T(8,128)}) custom-call(s32[1]{0:T(128)} %bitcast.1.column_ref, f32[8,128,512]{2,1,0:T(8,128)S(1)} %all-to-all-done.1.db_ref), custom_call_target="tpu_custom_call" | custom-call | flops 6000000000 | bytes 4000000 | tf_op jit(solution)/shard_map/factor/pallas_call | solution.py:289
  86.0 1.5 %all-to-all-done.routed_ref = f32[8,2,64,256]{3,2,1,0:T(8,128)S(1)} async-done(((f32[8,2,64,256]{3,2,1,0:T(8,128)}), f32[8,2,64,256]{3,2,1,0:T(8,128)S(1)}, u32[]{:S(2)}, u32[]{:S(2)}) %all-to-all-start) | async-done | bytes 1048608 | tf_op jit(solution)/shard_map/all_to_all | solution.py:287
  87.5 0.0 copy-done.2
  87.5 0.0 copy-done.3
  87.5 6.1 %couple.1 = (f32[2,256,256]{2,1,0:T(8,128)}, f32[8,32,256]{2,1,0:T(8,128)S(1)}) custom-call(s32[2]{0:T(128)S(1)} %pad_add_fusion.place_ref, s32[64,16]{1,0:T(8,128)S(1)} %copy.10.index_ref, s32[1,16]{1,0:T(1,128)S(1)} %copy-done.3, s32[64]{0:T(128)S(1)} %copy-done.2, f32[2,512,512]{2,1,0:T(8,128)} %bitcast.15, ...), custom_call_target="tpu_custom_call" | custom-call | tf_op jit(solution)/shard_map/couple/pallas_call | solution.py:303
  93.6 10.7 %all_to_all.15.parts_ref = f32[8,32,256]{2,1,0:T(8,128)S(1)} all-to-all(f32[8,32,256]{2,1,0:T(8,128)S(1)} %get-tuple-element.10), channel_id=1, replica_groups=mesh['clu'=64,'col'=8] {'col'}, dimensions={0} | all-to-all | bytes 524288 | tf_op jit(solution)/shard_map/all_to_all | solution.py:324
  104.2 1.3 %merge.1 = f32[32,512]{1,0:T(8,128)} custom-call(s32[2]{0:T(128)S(1)} %pad_add_fusion.place_ref, s32[64]{0:T(128)S(1)} %copy-done.2, f32[8,32,256]{2,1,0:T(8,128)S(1)} %all_to_all.15.parts_ref, f32[32,256]{1,0:T(8,128)S(1)} %get-tuple-element.11.schur_ref), custom_call_target="tpu_custom_call" | custom-call | tf_op jit(solution)/shard_map/merge/pallas_call | solution.py:325
  (2 shorter events, 0.0 us)
Async XLA Ops:
  0.6 0.9 copy-start
  1.5 0.9 copy-start.1
  3.9 49.6 %copy-start.4 = (s32[64,16]{0,1:T(8,128)S(1)}, s32[64,16]{0,1:T(8,128)}, u32[]{:S(2)}) copy-start(s32[64,16]{0,1:T(8,128)} %param.9) | copy-start | bytes 12292
  3.9 63.4 %all-to-all-start.1 = ((f32[8,128,512]{2,1,0:T(8,128)}), f32[8,128,512]{2,1,0:T(8,128)S(1)}, u32[]{:S(2)}, u32[]{:S(2)}) async-start(f32[8,128,512]{2,1,0:T(8,128)} %spread.1), calls=%async_computation.1 | async-start | bytes 4194304 | tf_op jit(solution)/shard_map/all_to_all | solution.py:270
  9.1 15.1 %collective-permute-start = (f32[64,256]{1,0:T(8,128)S(1)}, f32[64,256]{1,0:T(8,128)S(1)}, u32[]{:S(2)}, u32[]{:S(2)}) collective-permute-start(f32[64,256]{1,0:T(8,128)S(1)} %skeleton.1), channel_id=1, source_target_pairs={{448,0},{456,8},{464,16},{472,24},{480,32},{488,40},{496,48},{504,... | collective-permute-start | bytes 196616 | tf_op jit(solution)/shard_map/ppermute | solution.py:246
  24.2 7.2 %collective-permute-start.1 = (f32[2,64,256]{2,1,0:T(8,128)S(1)}, f32[2,64,256]{2,1,0:T(8,128)S(1)}, u32[]{:S(2)}, u32[]{:S(2)}) collective-permute-start(f32[2,64,256]{2,1,0:T(8,128)S(1)} %pad_maximum_fusion.1), channel_id=1, source_target_pairs={{32,0},{40,8},{48,16},{56,24},{64,32},{72,40},{80,48},{88,56},{96,... | collective-permute-start | bytes 393224 | tf_op jit(solution)/shard_map/ppermute | solution.py:246
  31.5 33.5 %collective-permute-start.4 = (f32[4,64,256]{2,1,0:T(8,128)S(1)}, f32[4,64,256]{2,1,0:T(8,128)S(1)}, u32[]{:S(2)}, u32[]{:S(2)}) collective-permute-start(f32[4,64,256]{2,1,0:T(8,128)S(1)} %pad_maximum_fusion.near0), channel_id=1, source_target_pairs={{24,0},{32,8},{40,16},{48,24},{56,32},{64,40},{72,48},{80,56},{88,... | collective-permute-start | bytes 786440 | tf_op jit(solution)/shard_map/ppermute | solution.py:246
  34.8 30.2 %collective-permute-start.3 = (f32[4,64,256]{2,1,0:T(8,128)S(1)}, f32[4,64,256]{2,1,0:T(8,128)S(1)}, u32[]{:S(2)}, u32[]{:S(2)}) collective-permute-start(f32[4,64,256]{2,1,0:T(8,128)S(1)} %pad_maximum_fusion.near0), channel_id=1, source_target_pairs={{16,0},{24,8},{32,16},{40,24},{48,32},{56,40},{64,48},{72,56},{80,... | collective-permute-start | bytes 786440 | tf_op jit(solution)/shard_map/ppermute | solution.py:246
  42.8 22.2 %collective-permute-start.2 = (f32[4,64,256]{2,1,0:T(8,128)S(1)}, f32[4,64,256]{2,1,0:T(8,128)S(1)}, u32[]{:S(2)}, u32[]{:S(2)}) collective-permute-start(f32[4,64,256]{2,1,0:T(8,128)S(1)} %pad_maximum_fusion.near0), channel_id=1, source_target_pairs={{8,0},{16,8},{24,16},{32,24},{40,32},{48,40},{56,48},{64,56},{72,6... | collective-permute-start | bytes 786440 | tf_op jit(solution)/shard_map/ppermute | solution.py:246
  46.1 18.9 %collective-permute-start.5 = (f32[64,256]{1,0:T(8,128)S(1)}, f32[64,256]{1,0:T(8,128)S(1)}, u32[]{:S(2)}, u32[]{:S(2)}) collective-permute-start(f32[64,256]{1,0:T(8,128)S(1)} %skeleton.1), channel_id=1, source_target_pairs={{256,0},{264,8},{272,16},{280,24},{288,32},{296,40},{304,48},{312,... | collective-permute-start | bytes 196616 | tf_op jit(solution)/shard_map/ppermute | solution.py:246
  67.3 20.2 %all-to-all-start = ((f32[8,2,64,256]{3,2,1,0:T(8,128)}), f32[8,2,64,256]{3,2,1,0:T(8,128)S(1)}, u32[]{:S(2)}, u32[]{:S(2)}) async-start(f32[8,2,64,256]{3,2,1,0:T(8,128)} %order.1), calls=%async_computation | async-start | bytes 2097152 | tf_op jit(solution)/shard_map/all_to_all | solution.py:287
  71.6 15.9 %copy-start.2 = (s32[64]{0:T(128)S(1)}, s32[64]{0:T(128)}, u32[]{:S(2)}) copy-start(s32[64]{0:T(128)} %parent_ref.3) | copy-start | bytes 772
  71.6 15.9 %copy-start.3 = (s32[1,16]{1,0:T(1,128)S(1)}, s32[1,16]{1,0:T(1,128)}, u32[]{:S(2)}) copy-start(s32[1,16]{1,0:T(1,128)} %mask_ref.1) | copy-start | bytes 196
where the time goes:
time: 106 us; the launch traced here: 105 us
  starting transfers between devices  37.7 us (36%)
  waiting for transfers between devices  28 us (26%)
  Pallas kernels  26.3 us (25%)
  blocking collectives  10.7 us (10%)
  local copies, waits for them, and re-layouts  1.9 us (2%)
    ppermute x6, starting transfers between devices, shift(): lax.ppermute(x, 'clu', [((i + d) % clusters, i) for i in range(clusters)])  29.1 us
    ppermute x6, waiting for transfers between devices, shift(): lax.ppermute(x, 'clu', [((i + d) % clusters, i) for i in range(clusters)])  26.6 us
    pallas_call x1, Pallas kernels, shards(): pl.pallas_call(factor_kernel, out_shape=(shape((size - RANK, RANK), F32),...  14.4 us
    all_to_all x1, blocking collectives, shards(): lax.all_to_all(side, 'col', split_axis=0, concat_axis=0, tiled=False)  10.7 us
    pallas_call x1, Pallas kernels, shards(): pl.pallas_call(couple_kernel, out_shape=(shape((per_device, RANK, RANK),...  6.07 us
    all_to_all x1, starting transfers between devices, shards(): db = lax.all_to_all(spread, 'col', split_axis=0, concat_axis=0, tiled=False)  4.31 us
    all_to_all x1, starting transfers between devices, shards(): lax.all_to_all(ordered, 'col', split_axis=0, concat_axis=0, tiled=False)  4.23 us
    pallas_call x1, Pallas kernels, shards(): pl.pallas_call(order_kernel, out_shape=pltpu.HBM((columns, per_device, ro...  2.29 us
  transfers between devices with their start and end apart: 8, of which 4 were waited for; matrix products, arithmetic and copies ran while one was open for 0% of the time, Pallas kernels for 17%

commit v1 on v0

--- a/solution.py
+++ b/solution.py
@@ -105,6 +105,10 @@
     return pltpu.CompilerParams(vmem_limit_bytes=mib * 2**20)
 
 
+def keep_out(x):
+    return pltpu.with_memory_space_constraint(x, pltpu.HBM)
+
+
 def slice_kernel(bases_ref, skeleton_ref, sem):
     source = bases_ref.at[:, pl.ds(bases_ref.shape[1] - RANK, RANK)]
     run_copies([pltpu.make_async_copy(source, skeleton_ref, sem)])
@@ -117,14 +121,13 @@
         copy.wait()
 
 
-def spread_kernel(diag_ref, bases_ref, out_ref, sem):
+def spread_kernel(diag_ref, bases_ref, out_ref, both, sem):
     rows = diag_ref.shape[0]
-    copies = []
-    for p in range(out_ref.shape[0]):
-        for q, ref in enumerate((diag_ref, bases_ref)):
-            target = out_ref.at[p, pl.ds(q * rows, rows)]
-            copies.append(pltpu.make_async_copy(ref, target, sem.at[p, q]))
-    run_copies(copies)
+    pair = (diag_ref, bases_ref)
+    run_copies(
+        [pltpu.make_async_copy(ref, both.at[pl.ds(q * rows, rows)], sem.at[q]) for q, ref in enumerate(pair)]
+    )
+    run_copies([pltpu.make_async_copy(both, out_ref.at[p], sem.at[p]) for p in range(out_ref.shape[0])])
 
 
 def order_kernel(own_ref, index_ref, near0, near1, near2, near3, far, out_ref, slot_of, sem):
@@ -142,15 +145,18 @@
     run_copies(copies)
 
 
-def factor_kernel(column_ref, db_ref, solve_ref, schur_ref, factor_ref, work, upper1, upper2, full):
+def factor_kernel(
+    column_ref, db_ref, high_ref, low_ref, schur_ref, factor_ref, work, upper1, upper2, full, solve_ref
+):
     rows = db_ref.shape[1] // 2
     size = db_ref.shape[0] * rows
     diag = db_ref[:, :rows, :].reshape(size, size)
     basis = db_ref[:, rows:, :].reshape(size, size)
-    half = dot_full(diag, basis)
     first = ((0,), (0,))
-    reduced = dot_full(half, basis, first)
     red = size - RANK
+    reduced = dot_full(dot_full(diag, basis[:, :red]), basis, first)
+    skeleton = split2(basis[:, red:])
+    corner = dot3(skeleton, split2(dot3(split2(diag), skeleton)), first)
     ri = lax.broadcasted_iota(jnp.int32, (HALF, HALF), 0)
     ci = lax.broadcasted_iota(jnp.int32, (HALF, HALF), 1)
     eye = (ri == ci).astype(F32)
@@ -170,10 +176,12 @@
     couple2, cross = joint[:, :RANK], joint[:, RANK:]
     solve_ref[:HALF, :] = dot_full(inv1, couple1, first) - dot_full(cross, couple2, first)
     solve_ref[HALF:, :] = dot_full(inv2, couple2, first)
+    lift = basis[:, red:] - dot3(split2(basis[:, :red]), split2(solve_ref[...]))
+    high_ref[...], low_ref[...] = split2(lift)
     column = column_ref[0]
     count = schur_ref.shape[0]
     start = pl.multiple_of(column * count, count)
-    full[...] = reduced[red:, red:] - (
+    full[...] = corner - (
         dot_full(couple1, couple1, first) + dot_full(couple2, couple2, first)
     )
     schur_ref[...] = full[pl.ds(start, count), :]
@@ -193,32 +201,41 @@
     return lax.fori_loop(0, parent_ref.shape[0], step, jnp.int32(0), unroll=True)
 
 
-def couple_kernel(
-    place_ref, index_ref, mask_ref, parent_ref, near_ref, routed_ref, db_ref, solve_ref, out_ref, side_ref, block, sem
-):
-    loads = [pltpu.make_async_copy(near_ref.at[k], block.at[k], sem.at[k]) for k in range(near_ref.shape[0])]
+def project_kernel(near_ref, high_ref, low_ref, out_high, out_low, block, sem):
+    count = near_ref.shape[0]
+    loads = [pltpu.make_async_copy(near_ref.at[k], block.at[k], sem.at[k]) for k in range(count)]
     for load in loads:
         load.start()
+    lift = high_ref[...], low_ref[...]
+    for k in range(count):
+        loads[k].wait()
+        out_high[k], out_low[k] = split2(dot3(lift, split2(block[k]), ((0,), (0,))))
+
+
+def slot_product(high_ref, low_ref, routed_ref, k):
+    size = high_ref.shape[2]
+    partner = routed_ref[:, k].reshape(size, RANK)
+    return dot3((high_ref[k], low_ref[k]), split2(partner))
+
+
+def side_kernel(place_ref, index_ref, mask_ref, parent_ref, high_ref, low_ref, routed_ref, side_ref):
     own, column = place_ref[0], place_ref[1]
     sibling = find_sibling(own, parent_ref)
-    rows = db_ref.shape[1] // 2
-    size = db_ref.shape[0] * rows
-    red = size - RANK
-    basis = db_ref[:, rows:, :].reshape(size, size)
-    lift = basis[:, red:] - dot_full(basis[:, :red], solve_ref[...])
-    lift2 = split2(lift)
-    side = jnp.zeros((RANK, RANK), F32)
-    for k in range(near_ref.shape[0]):
-        slot = column * near_ref.shape[0] + k
-        partner = routed_ref[:, k].reshape(size, RANK)
-        loads[k].wait()
-        middle = dot3(split2(block[k]), split2(partner))
-        live = mask_ref[0, slot].astype(F32)
-        coupling = dot3(lift2, split2(middle), ((0,), (0,))) * live
-        out_ref[k] = coupling
-        match = jnp.where(index_ref[own, slot] == sibling, live, 0.0)
-        side = side + match * coupling
-    side_ref[...] = side.reshape(side_ref.shape)
+    side_ref[...] = jnp.zeros_like(side_ref)
+    count = high_ref.shape[0]
+    for k in range(count):
+        slot = column * count + k
+
+        @pl.when((mask_ref[0, slot] != 0) & (index_ref[own, slot] == sibling))
+        def _():
+            side_ref[...] = slot_product(high_ref, low_ref, routed_ref, k).reshape(side_ref.shape)
+
+
+def couple_kernel(place_ref, mask_ref, high_ref, low_ref, routed_ref, out_ref):
+    count = high_ref.shape[0]
+    for k in range(count):
+        live = mask_ref[0, place_ref[1] * count + k].astype(F32)
+        out_ref[k] = slot_product(high_ref, low_ref, routed_ref, k) * live
 
 
 def merge_kernel(place_ref, parent_ref, parts_ref, schur_ref, out_ref):
@@ -253,7 +270,7 @@
         scratch_shapes=[pltpu.SemaphoreType.DMA],
         compiler_params=params(4),
         name="skeleton",
-    )(pltpu.with_memory_space_constraint(bases[0], pltpu.HBM))
+    )(keep_out(bases[0]))
     down8 = shift(skeleton, -8)
     far = shift(skeleton, clusters // 2)
     pair = jnp.stack([down8, skeleton])
@@ -261,12 +278,12 @@
     spread = pl.pallas_call(
         spread_kernel,
         out_shape=pltpu.HBM((columns, 2 * rows, size), F32),
-        in_specs=[VMEM] * 2,
+        in_specs=[HBM] * 2,
         out_specs=HBM,
-        scratch_shapes=[pltpu.SemaphoreType.DMA((columns, 2))],
+        scratch_shapes=[pltpu.VMEM((2 * rows, size), F32), pltpu.SemaphoreType.DMA((columns,))],
         compiler_params=params(4),
         name="spread",
-    )(diag_block[0], bases[0])
+    )(keep_out(diag_block[0]), keep_out(bases[0]))
     db = lax.all_to_all(spread, "col", split_axis=0, concat_axis=0, tiled=False)
     near0 = jnp.concatenate([pair, up4], axis=0)
     near1 = shift(near0, 1)
@@ -286,42 +303,54 @@
     )(own[None], near_index, near0, near1, near2, near3, far)
     routed = lax.all_to_all(ordered, "col", split_axis=0, concat_axis=0, tiled=False)
     count = RANK // columns
-    solve, schur, factor = pl.pallas_call(
+    high, low, schur, factor = pl.pallas_call(
         factor_kernel,
         out_shape=(
-            shape((size - RANK, RANK), F32),
+            shape((size, RANK), BF16),
+            shape((size, RANK), BF16),
             shape((count, RANK), F32),
             shape(((size - RANK) // columns, size - RANK), F32),
         ),
         in_specs=[SMEM, VMEM],
-        out_specs=(VMEM,) * 3,
-        scratch_shapes=[pltpu.VMEM((HALF, 2 * HALF), F32)] * 3 + [pltpu.VMEM((RANK, RANK), F32)],
+        out_specs=(VMEM,) * 4,
+        scratch_shapes=[pltpu.VMEM((HALF, 2 * HALF), F32)] * 3 + [pltpu.VMEM((RANK, RANK), F32)] * 2,
         cost_estimate=pl.CostEstimate(flops=6_000_000_000, bytes_accessed=4_000_000, transcendentals=0),
         compiler_params=params(24),
         name="factor",
     )(column[None], db)
-    coupling, side = pl.pallas_call(
-        couple_kernel,
-        out_shape=(shape((per_device, RANK, RANK), F32), shape((columns, count, RANK), F32)),
-        in_specs=[SMEM] * 4 + [HBM] + [VMEM] * 3,
+    projected = (per_device, RANK, size)
+    rows_high, rows_low = pl.pallas_call(
+        project_kernel,
+        out_shape=(shape(projected, BF16),) * 2,
+        in_specs=[HBM] + [VMEM] * 2,
         out_specs=(VMEM,) * 2,
         scratch_shapes=[
             pltpu.VMEM(near_blocks.shape[1:], F32),
             pltpu.SemaphoreType.DMA((per_device,)),
         ],
-        compiler_params=params(24),
+        cost_estimate=pl.CostEstimate(flops=1_000_000_000, bytes_accessed=4_000_000, transcendentals=0),
+        compiler_params=params(16),
+        name="project",
+    )(keep_out(near_blocks[0]), high, low)
+    side = pl.pallas_call(
+        side_kernel,
+        out_shape=shape((columns, count, RANK), F32),
+        in_specs=[SMEM] * 4 + [VMEM] * 3,
+        out_specs=VMEM,
+        cost_estimate=pl.CostEstimate(flops=200_000_000, bytes_accessed=2_000_000, transcendentals=0),
+        compiler_params=params(8),
+        name="side",
+    )(place, near_index, near_mask, parent_map, rows_high, rows_low, routed)
+    parts = lax.all_to_all(side, "col", split_axis=0, concat_axis=0, tiled=False)
+    coupling = pl.pallas_call(
+        couple_kernel,
+        out_shape=shape((per_device, RANK, RANK), F32),
+        in_specs=[SMEM] * 2 + [VMEM] * 3,
+        out_specs=VMEM,
+        cost_estimate=pl.CostEstimate(flops=400_000_000, bytes_accessed=4_000_000, transcendentals=0),
+        compiler_params=params(8),
         name="couple",
-    )(
-        place,
-        near_index,
-        near_mask,
-        parent_map,
-        pltpu.with_memory_space_constraint(near_blocks[0], pltpu.HBM),
-        routed,
-        db,
-        solve,
-    )
-    parts = lax.all_to_all(side, "col", split_axis=0, concat_axis=0, tiled=False)
+    )(place, near_mask, rows_high, rows_low, routed)
     parent_rows = pl.pallas_call(
         merge_kernel,
         out_shape=shape((count, 2 * RANK), F32),

time: 106 us -> 105 us (level)
  blocking collectives: 10.7 us -> 0 us
  waiting for transfers between devices: 28 us -> 35.4 us
  starting transfers between devices: 37.7 us -> 40.9 us
  local copies, waits for them, and re-layouts: 1.9 us -> 0.1 us
    all_to_all x1 -> x0, blocking collectives: 10.7 us -> none  [shards(): lax.all_to_all(side, 'col', split_axis=0, concat_axis=0, tiled=False)]
    all_to_all x0 -> x1, waiting for transfers between devices: none -> 5.58 us  [shards(): lax.all_to_all(side, 'col', split_axis=0, concat_axis=0, tiled=False)]
    all_to_all x0 -> x1, starting transfers between devices: none -> 4.8 us  [shards(): lax.all_to_all(side, 'col', split_axis=0, concat_axis=0, tiled=False)]
    ppermute x6, waiting for transfers between devices: 26.6 us -> 29.8 us  [shift(): lax.ppermute(x, 'clu', [((i + d) % clusters, i) for i in range(clusters)])]
    unnamed x11 -> x7, local copies, waits for them, and re-layouts: 1.9 us -> 0.1 us
    all_to_all x1, waiting for transfers between devices: 1.46 us -> 0.01 us  [shards(): lax.all_to_all(ordered, 'col', split_axis=0, concat_axis=0, tiled=False)]
    ppermute x6, starting transfers between devices: 29.1 us -> 27.9 us  [shift(): lax.ppermute(x, 'clu', [((i + d) % clusters, i) for i in range(clusters)])]
    pallas_call x2 -> x4, Pallas kernels: 20.5 us -> 20.2 us  [the longest x1 13.9 us: shards(): pl.pallas_call(factor_kernel, out_shape=(shape((size, RANK), BF16), shape...]
  transfers between devices with their start and end apart: 8 -> 9, of which waited for: 4 -> 4; matrix products, arithmetic and copies ran while one was open for 0% -> 0% of each run, Pallas kernels for 17% -> 21%
where the time goes in v1:
time: 105 us; the launch traced here: 104 us
  starting transfers between devices  40.9 us (39%)
  waiting for transfers between devices  35.4 us (34%)
  Pallas kernels  27 us (26%)
    ppermute x6, waiting for transfers between devices, shift(): lax.ppermute(x, 'clu', [((i + d) % clusters, i) for i in range(clusters)])  29.8 us
    ppermute x6, starting transfers between devices, shift(): lax.ppermute(x, 'clu', [((i + d) % clusters, i) for i in range(clusters)])  27.9 us
    pallas_call x1, Pallas kernels, shards(): pl.pallas_call(factor_kernel, out_shape=(shape((size, RANK), BF16), shape...  13.9 us
    all_to_all x1, waiting for transfers between devices, shards(): lax.all_to_all(side, 'col', split_axis=0, concat_axis=0, tiled=False)  5.58 us
    all_to_all x1, starting transfers between devices, shards(): lax.all_to_all(side, 'col', split_axis=0, concat_axis=0, tiled=False)  4.8 us
    all_to_all x1, starting transfers between devices, shards(): db = lax.all_to_all(spread, 'col', split_axis=0, concat_axis=0, tiled=False)  4.31 us
    all_to_all x1, starting transfers between devices, shards(): lax.all_to_all(ordered, 'col', split_axis=0, concat_axis=0, tiled=False)  3.82 us
    pallas_call x1, Pallas kernels, shards(): pl.pallas_call(project_kernel, out_shape=(shape(projected, BF16),) * 2, i...  2.47 us
  transfers between devices with their start and end apart: 9, of which 4 were waited for; matrix products, arithmetic and copies ran while one was open for 0% of the time, Pallas kernels for 21%

profile of v1, /device:TPU:32, one launch (start us, length us, event | category | flops | bytes accessed | tf_op | source)
XLA Modules:
  0.0 104.2 jit_solution(11397317737625162320)
XLA Ops:
  0.6 2.4 %spread.1 = f32[8,128,512]{2,1,0:T(8,128)} custom-call(f32[64,512]{1,0:T(8,128)} %bitcast.17, f32[64,512]{1,0:T(8,128)} %bitcast.13), custom_call_target="tpu_custom_call" | custom-call | tf_op jit(solution)/shard_map/spread/pallas_call | solution.py:278
  3.0 0.0 copy-start.2
  3.0 4.3 %all-to-all-start = ((f32[8,128,512]{2,1,0:T(8,128)}), f32[8,128,512]{2,1,0:T(8,128)S(1)}, u32[]{:S(2)}, u32[]{:S(2)}) async-start(f32[8,128,512]{2,1,0:T(8,128)} %spread.1), calls=%async_computation | async-start | bytes 4194304 | tf_op jit(solution)/shard_map/all_to_all | solution.py:287
  7.3 0.8 skeleton.1
  8.2 5.2 %collective-permute-start = (f32[64,256]{1,0:T(8,128)S(1)}, f32[64,256]{1,0:T(8,128)S(1)}, u32[]{:S(2)}, u32[]{:S(2)}) collective-permute-start(f32[64,256]{1,0:T(8,128)S(1)} %skeleton.1), channel_id=1, source_target_pairs={{448,0},{456,8},{464,16},{472,24},{480,32},{488,40},{496,48},{504,... | collective-permute-start | bytes 196616 | tf_op jit(solution)/shard_map/ppermute | solution.py:263
  13.4 9.9 %collective-permute-done = f32[64,256]{1,0:T(8,128)S(1)} collective-permute-done((f32[64,256]{1,0:T(8,128)S(1)}, f32[64,256]{1,0:T(8,128)S(1)}, u32[]{:S(2)}, u32[]{:S(2)}) %collective-permute-start) | collective-permute-done | bytes 65568 | tf_op jit(solution)/shard_map/ppermute | solution.py:263
  23.3 1.9 %collective-permute-start.1 = (f32[2,64,256]{2,1,0:T(8,128)S(1)}, f32[2,64,256]{2,1,0:T(8,128)S(1)}, u32[]{:S(2)}, u32[]{:S(2)}) collective-permute-start(f32[2,64,256]{2,1,0:T(8,128)S(1)} %pad_maximum_fusion.1), channel_id=1, source_target_pairs={{32,0},{40,8},{48,16},{56,24},{64,32},{72,40},{80,48},{88,56},{96,... | collective-permute-start | bytes 393224 | tf_op jit(solution)/shard_map/ppermute | solution.py:263
  25.2 5.3 %collective-permute-done.1 = f32[2,64,256]{2,1,0:T(8,128)S(1)} collective-permute-done((f32[2,64,256]{2,1,0:T(8,128)S(1)}, f32[2,64,256]{2,1,0:T(8,128)S(1)}, u32[]{:S(2)}, u32[]{:S(2)}) %collective-permute-start.1) | collective-permute-done | bytes 131104 | tf_op jit(solution)/shard_map/ppermute | solution.py:263
  30.6 4.8 %collective-permute-start.2 = (f32[4,64,256]{2,1,0:T(8,128)S(1)}, f32[4,64,256]{2,1,0:T(8,128)S(1)}, u32[]{:S(2)}, u32[]{:S(2)}) collective-permute-start(f32[4,64,256]{2,1,0:T(8,128)S(1)} %pad_maximum_fusion.near0), channel_id=1, source_target_pairs={{8,0},{16,8},{24,16},{32,24},{40,32},{48,40},{56,48},{64,56},{72,6... | collective-permute-start | bytes 786440 | tf_op jit(solution)/shard_map/ppermute | solution.py:263
  35.4 2.5 %collective-permute-start.3 = (f32[4,64,256]{2,1,0:T(8,128)S(1)}, f32[4,64,256]{2,1,0:T(8,128)S(1)}, u32[]{:S(2)}, u32[]{:S(2)}) collective-permute-start(f32[4,64,256]{2,1,0:T(8,128)S(1)} %pad_maximum_fusion.near0), channel_id=1, source_target_pairs={{16,0},{24,8},{32,16},{40,24},{48,32},{56,40},{64,48},{72,56},{80,... | collective-permute-start | bytes 786440 | tf_op jit(solution)/shard_map/ppermute | solution.py:263
  37.9 6.0 %collective-permute-start.4 = (f32[4,64,256]{2,1,0:T(8,128)S(1)}, f32[4,64,256]{2,1,0:T(8,128)S(1)}, u32[]{:S(2)}, u32[]{:S(2)}) collective-permute-start(f32[4,64,256]{2,1,0:T(8,128)S(1)} %pad_maximum_fusion.near0), channel_id=1, source_target_pairs={{24,0},{32,8},{40,16},{48,24},{56,32},{64,40},{72,48},{80,56},{88,... | collective-permute-start | bytes 786440 | tf_op jit(solution)/shard_map/ppermute | solution.py:263
  43.9 7.5 %collective-permute-start.5 = (f32[64,256]{1,0:T(8,128)S(1)}, f32[64,256]{1,0:T(8,128)S(1)}, u32[]{:S(2)}, u32[]{:S(2)}) collective-permute-start(f32[64,256]{1,0:T(8,128)S(1)} %skeleton.1), channel_id=1, source_target_pairs={{256,0},{264,8},{272,16},{280,24},{288,32},{296,40},{304,48},{312,... | collective-permute-start | bytes 196616 | tf_op jit(solution)/shard_map/ppermute | solution.py:263
  51.4 0.0 copy-done.2
  51.4 0.1 copy.9.index_ref
  51.5 14.6 %collective-permute-done.5.far = f32[64,256]{1,0:T(8,128)S(1)} collective-permute-done((f32[64,256]{1,0:T(8,128)S(1)}, f32[64,256]{1,0:T(8,128)S(1)}, u32[]{:S(2)}, u32[]{:S(2)}) %collective-permute-start.5) | collective-permute-done | bytes 65568 | tf_op jit(solution)/shard_map/ppermute | solution.py:263
  66.1 0.0 collective-permute-done.2.near1
  66.1 0.0 collective-permute-done.3.near2
  66.1 0.0 collective-permute-done.4.near3
  66.1 2.3 %order.1 = f32[8,2,64,256]{3,2,1,0:T(8,128)} custom-call(s32[1]{0:T(128)} %bitcast.own_ref, s32[64,16]{1,0:T(8,128)S(1)} %copy.9.index_ref, f32[4,64,256]{2,1,0:T(8,128)S(1)} %pad_maximum_fusion.near0, f32[4,64,256]{2,1,0:T(8,128)S(1)} %collective-permute-done.2.near1, f32[4,64,256]{2,1,0:T(8,128)S(1)} %collective-permute-done.3.near2, ...), custom_call_target="tpu_custom_call" | custom-call | tf_op jit(solution)/shard_map/order/pallas_call | solution.py:292
  68.4 0.0 all-to-all-done.db_ref
  68.4 3.8 %all-to-all-start.1 = ((f32[8,2,64,256]{3,2,1,0:T(8,128)}), f32[8,2,64,256]{3,2,1,0:T(8,128)S(1)}, u32[]{:S(2)}, u32[]{:S(2)}) async-start(f32[8,2,64,256]{3,2,1,0:T(8,128)} %order.1), calls=%async_computation.1 | async-start | bytes 2097152 | tf_op jit(solution)/shard_map/all_to_all | solution.py:304
  72.2 0.1 pad_add_fusion.place_ref
  72.3 13.9 %factor.1 = (bf16[512,256]{1,0:T(8,128)(2,1)S(1)}, bf16[512,256]{1,0:T(8,128)(2,1)S(1)}, f32[32,256]{1,0:T(8,128)S(1)}, f32[32,256]{1,0:T(8,128)}) custom-call(s32[1]{0:T(128)} %bitcast.1.column_ref, f32[8,128,512]{2,1,0:T(8,128)S(1)} %all-to-all-done.db_ref), custom_call_target="tpu_custom_call" | custom-call | flops 6000000000 | bytes 4000000 | tf_op jit(solution)/shard_map/factor/pallas_call | solution.py:306
  86.2 0.0 copy-start
  86.2 0.0 copy-start.1
  86.2 2.5 %project.1 = (bf16[2,256,512]{2,1,0:T(8,128)(2,1)S(1)}, bf16[2,256,512]{2,1,0:T(8,128)(2,1)S(1)}) custom-call(f32[2,512,512]{2,1,0:T(8,128)} %bitcast.19, bf16[512,256]{1,0:T(8,128)(2,1)S(1)} %get-tuple-element.9.high_ref, bf16[512,256]{1,0:T(8,128)(2,1)S(1)} %get-tuple-element.10.low_ref), custom_call_target="tpu_custom_call" | custom-call | flops 1000000000 | bytes 4000000 | tf_op jit(solution)/shard_map/project/pallas_call | solution.py:322
  88.7 0.0 all-to-all-done.1.routed_ref
  88.7 0.0 copy-done
  88.7 0.0 copy-done.1
  88.7 1.9 %side.1 = f32[8,32,256]{2,1,0:T(8,128)} custom-call(s32[2]{0:T(128)S(1)} %pad_add_fusion.place_ref, s32[64,16]{1,0:T(8,128)S(1)} %copy.9.index_ref, s32[1,16]{1,0:T(1,128)S(1)} %copy-done, s32[64]{0:T(128)S(1)} %copy-done.1, bf16[2,256,512]{2,1,0:T(8,128)(2,1)S(1)} %get-tuple-element.11.high_ref, bf16[2,256,512]{2,1,0:T(8,128)(2,1)S(1)} %get-tuple-element.12.low_ref, ...), custom_call_target="tpu_custom_call" | custom-call | flops 200000000 | bytes 2000000 | tf_op jit(solution)/shard_map/side/pallas_call | solution.py:335
  90.6 4.8 %all-to-all-start.2 = ((f32[8,32,256]{2,1,0:T(8,128)}), f32[8,32,256]{2,1,0:T(8,128)S(1)}, u32[]{:S(2)}, u32[]{:S(2)}) async-start(f32[8,32,256]{2,1,0:T(8,128)} %side.1), calls=%async_computation.2 | async-start | bytes 524288 | tf_op jit(solution)/shard_map/all_to_all | solution.py:344
  95.4 1.9 %couple.1 = f32[2,256,256]{2,1,0:T(8,128)} custom-call(s32[2]{0:T(128)S(1)} %pad_add_fusion.place_ref, s32[1,16]{1,0:T(1,128)S(1)} %copy-done, bf16[2,256,512]{2,1,0:T(8,128)(2,1)S(1)} %get-tuple-element.11.high_ref, bf16[2,256,512]{2,1,0:T(8,128)(2,1)S(1)} %get-tuple-element.12.low_ref, f32[8,2,64,256]{3,2,1,0:T(8,128)S(1)} %all-to-all-done.1.routed_ref), custom_call_target="tpu_custom_call" | custom-call | flops 400000000 | bytes 4000000 | tf_op jit(solution)/shard_map/couple/pallas_call | solution.py:345
  97.3 5.6 %all-to-all-done.2.parts_ref = f32[8,32,256]{2,1,0:T(8,128)S(1)} async-done(((f32[8,32,256]{2,1,0:T(8,128)}), f32[8,32,256]{2,1,0:T(8,128)S(1)}, u32[]{:S(2)}, u32[]{:S(2)}) %all-to-all-start.2) | async-done | bytes 262176 | tf_op jit(solution)/shard_map/all_to_all | solution.py:344
  102.9 1.3 %merge.1 = f32[32,512]{1,0:T(8,128)} custom-call(s32[2]{0:T(128)S(1)} %pad_add_fusion.place_ref, s32[64]{0:T(128)S(1)} %copy-done.1, f32[8,32,256]{2,1,0:T(8,128)S(1)} %all-to-all-done.2.parts_ref, f32[32,256]{1,0:T(8,128)S(1)} %get-tuple-element.13.schur_ref), custom_call_target="tpu_custom_call" | custom-call | tf_op jit(solution)/shard_map/merge/pallas_call | solution.py:354
  (2 shorter events, 0.0 us)
Async XLA Ops:
  3.0 48.4 %copy-start.2 = (s32[64,16]{0,1:T(8,128)S(1)}, s32[64,16]{0,1:T(8,128)}, u32[]{:S(2)}) copy-start(s32[64,16]{0,1:T(8,128)} %param.9) | copy-start | bytes 12292
  3.0 65.4 %all-to-all-start = ((f32[8,128,512]{2,1,0:T(8,128)}), f32[8,128,512]{2,1,0:T(8,128)S(1)}, u32[]{:S(2)}, u32[]{:S(2)}) async-start(f32[8,128,512]{2,1,0:T(8,128)} %spread.1), calls=%async_computation | async-start | bytes 4194304 | tf_op jit(solution)/shard_map/all_to_all | solution.py:287
  8.2 15.1 %collective-permute-start = (f32[64,256]{1,0:T(8,128)S(1)}, f32[64,256]{1,0:T(8,128)S(1)}, u32[]{:S(2)}, u32[]{:S(2)}) collective-permute-start(f32[64,256]{1,0:T(8,128)S(1)} %skeleton.1), channel_id=1, source_target_pairs={{448,0},{456,8},{464,16},{472,24},{480,32},{488,40},{496,48},{504,... | collective-permute-start | bytes 196616 | tf_op jit(solution)/shard_map/ppermute | solution.py:263
  23.3 7.2 %collective-permute-start.1 = (f32[2,64,256]{2,1,0:T(8,128)S(1)}, f32[2,64,256]{2,1,0:T(8,128)S(1)}, u32[]{:S(2)}, u32[]{:S(2)}) collective-permute-start(f32[2,64,256]{2,1,0:T(8,128)S(1)} %pad_maximum_fusion.1), channel_id=1, source_target_pairs={{32,0},{40,8},{48,16},{56,24},{64,32},{72,40},{80,48},{88,56},{96,... | collective-permute-start | bytes 393224 | tf_op jit(solution)/shard_map/ppermute | solution.py:263
  30.6 35.5 %collective-permute-start.2 = (f32[4,64,256]{2,1,0:T(8,128)S(1)}, f32[4,64,256]{2,1,0:T(8,128)S(1)}, u32[]{:S(2)}, u32[]{:S(2)}) collective-permute-start(f32[4,64,256]{2,1,0:T(8,128)S(1)} %pad_maximum_fusion.near0), channel_id=1, source_target_pairs={{8,0},{16,8},{24,16},{32,24},{40,32},{48,40},{56,48},{64,56},{72,6... | collective-permute-start | bytes 786440 | tf_op jit(solution)/shard_map/ppermute | solution.py:263
  35.4 30.7 %collective-permute-start.3 = (f32[4,64,256]{2,1,0:T(8,128)S(1)}, f32[4,64,256]{2,1,0:T(8,128)S(1)}, u32[]{:S(2)}, u32[]{:S(2)}) collective-permute-start(f32[4,64,256]{2,1,0:T(8,128)S(1)} %pad_maximum_fusion.near0), channel_id=1, source_target_pairs={{16,0},{24,8},{32,16},{40,24},{48,32},{56,40},{64,48},{72,56},{80,... | collective-permute-start | bytes 786440 | tf_op jit(solution)/shard_map/ppermute | solution.py:263
  37.9 28.2 %collective-permute-start.4 = (f32[4,64,256]{2,1,0:T(8,128)S(1)}, f32[4,64,256]{2,1,0:T(8,128)S(1)}, u32[]{:S(2)}, u32[]{:S(2)}) collective-permute-start(f32[4,64,256]{2,1,0:T(8,128)S(1)} %pad_maximum_fusion.near0), channel_id=1, source_target_pairs={{24,0},{32,8},{40,16},{48,24},{56,32},{64,40},{72,48},{80,56},{88,... | collective-permute-start | bytes 786440 | tf_op jit(solution)/shard_map/ppermute | solution.py:263
  43.9 22.1 %collective-permute-start.5 = (f32[64,256]{1,0:T(8,128)S(1)}, f32[64,256]{1,0:T(8,128)S(1)}, u32[]{:S(2)}, u32[]{:S(2)}) collective-permute-start(f32[64,256]{1,0:T(8,128)S(1)} %skeleton.1), channel_id=1, source_target_pairs={{256,0},{264,8},{272,16},{280,24},{288,32},{296,40},{304,48},{312,... | collective-permute-start | bytes 196616 | tf_op jit(solution)/shard_map/ppermute | solution.py:263
  68.4 20.3 %all-to-all-start.1 = ((f32[8,2,64,256]{3,2,1,0:T(8,128)}), f32[8,2,64,256]{3,2,1,0:T(8,128)S(1)}, u32[]{:S(2)}, u32[]{:S(2)}) async-start(f32[8,2,64,256]{3,2,1,0:T(8,128)} %order.1), calls=%async_computation.1 | async-start | bytes 2097152 | tf_op jit(solution)/shard_map/all_to_all | solution.py:304
  86.2 2.5 %copy-start = (s32[1,16]{1,0:T(1,128)S(1)}, s32[1,16]{1,0:T(1,128)}, u32[]{:S(2)}) copy-start(s32[1,16]{1,0:T(1,128)} %mask_ref.3) | copy-start | bytes 196
  86.2 2.5 %copy-start.1 = (s32[64]{0:T(128)S(1)}, s32[64]{0:T(128)}, u32[]{:S(2)}) copy-start(s32[64]{0:T(128)} %parent_ref.3) | copy-start | bytes 772
  90.6 12.3 %all-to-all-start.2 = ((f32[8,32,256]{2,1,0:T(8,128)}), f32[8,32,256]{2,1,0:T(8,128)S(1)}, u32[]{:S(2)}, u32[]{:S(2)}) async-start(f32[8,32,256]{2,1,0:T(8,128)} %side.1), calls=%async_computation.2 | async-start | bytes 524288 | tf_op jit(solution)/shard_map/all_to_all | solution.py:344

commit v2 on v1

--- a/solution.py
+++ b/solution.py
@@ -121,27 +121,61 @@
         copy.wait()
 
 
-def spread_kernel(diag_ref, bases_ref, out_ref, both, sem):
+def find_sibling(own, parent_ref):
+    parent = parent_ref[own]
+
+    def step(i, found):
+        return jnp.where((parent_ref[i] == parent) & (i != own), i, found)
+
+    return lax.fori_loop(0, parent_ref.shape[0], step, jnp.int32(0), unroll=True)
+
+
+FIRST, LIVE = 32, 33
+
+
+def spread_kernel(
+    place_ref, index_ref, mask_ref, parent_ref, diag_ref, bases_ref, out_ref, facts_ref, both, sem
+):
     rows = diag_ref.shape[0]
     pair = (diag_ref, bases_ref)
-    run_copies(
-        [pltpu.make_async_copy(ref, both.at[pl.ds(q * rows, rows)], sem.at[q]) for q, ref in enumerate(pair)]
+    loads = [pltpu.make_async_copy(ref, both.at[pl.ds(q * rows, rows)], sem.at[q]) for q, ref in enumerate(pair)]
+    for load in loads:
+        load.start()
+    own, column = place_ref[0], place_ref[1]
+    slots, clusters = index_ref.shape
+    half = slots // 2
+    for k in range(slots):
+        offset = (index_ref[k, own] - own + clusters + half) % clusters
+        facts_ref[jnp.where(offset < slots, offset, half)] = k
+    for load in loads:
+        load.wait()
+    stores = [pltpu.make_async_copy(both, out_ref.at[p], sem.at[p]) for p in range(out_ref.shape[0])]
+    for store in stores:
+        store.start()
+    sibling = find_sibling(own, parent_ref)
+    facts_ref[FIRST] = (own < sibling).astype(jnp.int32)
+    count = slots // out_ref.shape[0]
+    for k in range(count):
+        slot = column * count + k
+        live = mask_ref[0, slot]
+        facts_ref[LIVE + 2 * k] = live
+        facts_ref[LIVE + 2 * k + 1] = jnp.where(index_ref[slot, own] == sibling, live, 0)
+    for store in stores:
+        store.wait()
+
+
+def order_kernel(facts_ref, near0, near1, near3, relay1, relay3, far, out_ref, sem):
+    sources = (
+        [near0.at[0], near0.at[2], far, near0.at[3]],
+        [near1.at[0], near1.at[2], near1.at[1], near1.at[3]],
+        [relay1.at[0], relay3.at[0], relay1.at[1], relay3.at[1]],
+        [near3.at[0], near3.at[2], near3.at[1], near3.at[3]],
     )
-    run_copies([pltpu.make_async_copy(both, out_ref.at[p], sem.at[p]) for p in range(out_ref.shape[0])])
-
-
-def order_kernel(own_ref, index_ref, near0, near1, near2, near3, far, out_ref, slot_of, sem):
-    own = own_ref[0]
-    clusters, slots = index_ref.shape
-    for k in range(slots):
-        offset = (index_ref[own, k] - own + clusters + slots // 2) % clusters
-        slot_of[jnp.where(offset < slots, offset, slots // 2)] = k
     copies = []
-    for d in range(slots):
-        stack = (near0, near1, near2, near3)[d % 4]
-        source = far if d == slots // 2 else stack.at[(0, 2, 1, 3)[d // 4]]
-        slot = slot_of[d]
-        copies.append(pltpu.make_async_copy(source, out_ref.at[slot // 2, slot % 2], sem.at[d]))
+    for d in range(16):
+        slot = facts_ref[d]
+        target = out_ref.at[slot // 2, slot % 2]
+        copies.append(pltpu.make_async_copy(sources[d % 4][d // 4], target, sem.at[d]))
     run_copies(copies)
 
 
@@ -192,15 +226,6 @@
     factor_ref[...] = full[pl.ds(start, count), :]
 
 
-def find_sibling(own, parent_ref):
-    parent = parent_ref[own]
-
-    def step(i, found):
-        return jnp.where((parent_ref[i] == parent) & (i != own), i, found)
-
-    return lax.fori_loop(0, parent_ref.shape[0], step, jnp.int32(0), unroll=True)
-
-
 def project_kernel(near_ref, high_ref, low_ref, out_high, out_low, block, sem):
     count = near_ref.shape[0]
     loads = [pltpu.make_async_copy(near_ref.at[k], block.at[k], sem.at[k]) for k in range(count)]
@@ -218,29 +243,23 @@
     return dot3((high_ref[k], low_ref[k]), split2(partner))
 
 
-def side_kernel(place_ref, index_ref, mask_ref, parent_ref, high_ref, low_ref, routed_ref, side_ref):
-    own, column = place_ref[0], place_ref[1]
-    sibling = find_sibling(own, parent_ref)
+def side_kernel(facts_ref, high_ref, low_ref, routed_ref, side_ref):
     side_ref[...] = jnp.zeros_like(side_ref)
-    count = high_ref.shape[0]
-    for k in range(count):
-        slot = column * count + k
-
-        @pl.when((mask_ref[0, slot] != 0) & (index_ref[own, slot] == sibling))
+    for k in range(high_ref.shape[0]):
+
+        @pl.when(facts_ref[LIVE + 2 * k + 1] != 0)
         def _():
             side_ref[...] = slot_product(high_ref, low_ref, routed_ref, k).reshape(side_ref.shape)
 
 
-def couple_kernel(place_ref, mask_ref, high_ref, low_ref, routed_ref, out_ref):
-    count = high_ref.shape[0]
-    for k in range(count):
-        live = mask_ref[0, place_ref[1] * count + k].astype(F32)
+def couple_kernel(facts_ref, high_ref, low_ref, routed_ref, out_ref):
+    for k in range(high_ref.shape[0]):
+        live = facts_ref[LIVE + 2 * k].astype(F32)
         out_ref[k] = slot_product(high_ref, low_ref, routed_ref, k) * live
 
 
-def merge_kernel(place_ref, parent_ref, parts_ref, schur_ref, out_ref):
-    own = place_ref[0]
-    first = own < find_sibling(own, parent_ref)
+def merge_kernel(facts_ref, parts_ref, schur_ref, out_ref):
+    first = facts_ref[FIRST] != 0
     side = parts_ref[0]
     for p in range(1, parts_ref.shape[0]):
         side = side + parts_ref[p]
@@ -275,32 +294,30 @@
     far = shift(skeleton, clusters // 2)
     pair = jnp.stack([down8, skeleton])
     up4 = shift(pair, 4)
-    spread = pl.pallas_call(
+    spread, facts = pl.pallas_call(
         spread_kernel,
-        out_shape=pltpu.HBM((columns, 2 * rows, size), F32),
-        in_specs=[HBM] * 2,
-        out_specs=HBM,
+        out_shape=(pltpu.HBM((columns, 2 * rows, size), F32), shape((64,), jnp.int32)),
+        in_specs=[SMEM] * 4 + [HBM] * 2,
+        out_specs=(HBM, SMEM),
         scratch_shapes=[pltpu.VMEM((2 * rows, size), F32), pltpu.SemaphoreType.DMA((columns,))],
         compiler_params=params(4),
         name="spread",
-    )(keep_out(diag_block[0]), keep_out(bases[0]))
+    )(place, near_index.T, near_mask, parent_map, keep_out(diag_block[0]), keep_out(bases[0]))
     db = lax.all_to_all(spread, "col", split_axis=0, concat_axis=0, tiled=False)
     near0 = jnp.concatenate([pair, up4], axis=0)
     near1 = shift(near0, 1)
-    near2 = shift(near0, 2)
     near3 = shift(near0, 3)
+    relay1 = shift(near1[:2], 1)
+    relay3 = shift(near3[:2], 3)
     ordered = pl.pallas_call(
         order_kernel,
         out_shape=pltpu.HBM((columns, per_device, rows, RANK), F32),
-        in_specs=[SMEM] * 2 + [ANY] * 5,
+        in_specs=[SMEM] + [ANY] * 6,
         out_specs=HBM,
         compiler_params=params(2),
-        scratch_shapes=[
-            pltpu.SMEM((near_index.shape[1],), jnp.int32),
-            pltpu.SemaphoreType.DMA((near_index.shape[1],)),
-        ],
+        scratch_shapes=[pltpu.SemaphoreType.DMA((near_index.shape[1],))],
         name="order",
-    )(own[None], near_index, near0, near1, near2, near3, far)
+    )(facts, near0, near1, near3, relay1, relay3, far)
     routed = lax.all_to_all(ordered, "col", split_axis=0, concat_axis=0, tiled=False)
     count = RANK // columns
     high, low, schur, factor = pl.pallas_call(
@@ -335,30 +352,30 @@
     side = pl.pallas_call(
         side_kernel,
         out_shape=shape((columns, count, RANK), F32),
-        in_specs=[SMEM] * 4 + [VMEM] * 3,
+        in_specs=[SMEM] + [VMEM] * 3,
         out_specs=VMEM,
         cost_estimate=pl.CostEstimate(flops=200_000_000, bytes_accessed=2_000_000, transcendentals=0),
         compiler_params=params(8),
         name="side",
-    )(place, near_index, near_mask, parent_map, rows_high, rows_low, routed)
+    )(facts, rows_high, rows_low, routed)
     parts = lax.all_to_all(side, "col", split_axis=0, concat_axis=0, tiled=False)
     coupling = pl.pallas_call(
         couple_kernel,
         out_shape=shape((per_device, RANK, RANK), F32),
-        in_specs=[SMEM] * 2 + [VMEM] * 3,
+        in_specs=[SMEM] + [VMEM] * 3,
         out_specs=VMEM,
         cost_estimate=pl.CostEstimate(flops=400_000_000, bytes_accessed=4_000_000, transcendentals=0),
         compiler_params=params(8),
         name="couple",
-    )(place, near_mask, rows_high, rows_low, routed)
+    )(facts, rows_high, rows_low, routed)
     parent_rows = pl.pallas_call(
         merge_kernel,
         out_shape=shape((count, 2 * RANK), F32),
-        in_specs=[SMEM] * 2 + [VMEM] * 2,
+        in_specs=[SMEM] + [VMEM] * 2,
         out_specs=VMEM,
         compiler_params=params(4),
         name="merge",
-    )(place, parent_map, parts, schur)
+    )(facts, parts, schur)
     return coupling[None], parent_rows[None], factor[None]
 
 

time: 105 us -> 113 us (1.076)
  the two profiles are of different devices: /device:TPU:32 before, /device:TPU:24 now
where the time goes in v2:
time: 113 us; the launch traced here: 111 us
  starting transfers between devices  53.2 us (47%)
  waiting for transfers between devices  28.1 us (25%)
  Pallas kernels  27 us (24%)
  local copies, waits for them, and re-layouts  2.03 us (2%)
    ppermute x7, starting transfers between devices, shift(): lax.ppermute(x, 'clu', [((i + d) % clusters, i) for i in range(clusters)])  39.6 us
    ppermute x7, waiting for transfers between devices, shift(): lax.ppermute(x, 'clu', [((i + d) % clusters, i) for i in range(clusters)])  22.5 us
    pallas_call x1, Pallas kernels, shards(): pl.pallas_call(factor_kernel, out_shape=(shape((size, RANK), BF16), shape...  14 us
    all_to_all x1, waiting for transfers between devices, shards(): lax.all_to_all(side, 'col', split_axis=0, concat_axis=0, tiled=False)  5.56 us
    all_to_all x1, starting transfers between devices, shards(): lax.all_to_all(side, 'col', split_axis=0, concat_axis=0, tiled=False)  4.9 us
    all_to_all x1, starting transfers between devices, shards(): lax.all_to_all(ordered, 'col', split_axis=0, concat_axis=0, tiled=False)  4.34 us
    all_to_all x1, starting transfers between devices, shards(): db = lax.all_to_all(spread, 'col', split_axis=0, concat_axis=0, tiled=False)  4.31 us
    pallas_call x1, Pallas kernels, shards(): pl.pallas_call(spread_kernel, out_shape=(pltpu.HBM((columns, 2 * rows, si...  3.65 us
  transfers between devices with their start and end apart: 10, of which 5 were waited for; matrix products, arithmetic and copies ran while one was open for 0% of the time, Pallas kernels for 19%

profile of v2, /device:TPU:24, one launch (start us, length us, event | category | flops | bytes accessed | tf_op | source)
XLA Modules:
  0.0 111.2 jit_solution(9551514789663253849)
XLA Ops:
  0.6 0.1 pad_add_fusion.place_ref
  0.7 0.0 copy-start
  0.7 0.7 copy-done
  1.4 0.0 copy-start.1
  1.4 0.7 copy-done.1
  2.1 0.0 copy-start.2
  2.1 0.7 copy-done.2
  2.7 3.7 %spread.1 = (f32[8,128,512]{2,1,0:T(8,128)}, s32[64]{0:T(128)S(1)}) custom-call(s32[2]{0:T(128)S(1)} %pad_add_fusion.place_ref, s32[16,64]{1,0:T(8,128)S(1)} %bitcast.13, s32[1,16]{1,0:T(1,128)S(1)} %copy-done.1, s32[64]{0:T(128)S(1)} %copy-done.2, f32[64,512]{1,0:T(8,128)} %bitcast.19, f32[64,512]{1,0:T(8,128)} %bitcast.14), custom_call_target="tpu_custom_call" | custom-call | tf_op jit(solution)/shard_map/spread/pallas_call | solution.py:297
  6.4 4.3 %all-to-all-start = ((f32[8,128,512]{2,1,0:T(8,128)}), f32[8,128,512]{2,1,0:T(8,128)S(1)}, u32[]{:S(2)}, u32[]{:S(2)}) async-start(f32[8,128,512]{2,1,0:T(8,128)} %get-tuple-element.12), calls=%async_computation | async-start | bytes 4194304 | tf_op jit(solution)/shard_map/all_to_all | solution.py:306
  10.7 0.8 skeleton.1
  11.5 5.2 %collective-permute-start = (f32[64,256]{1,0:T(8,128)S(1)}, f32[64,256]{1,0:T(8,128)S(1)}, u32[]{:S(2)}, u32[]{:S(2)}) collective-permute-start(f32[64,256]{1,0:T(8,128)S(1)} %skeleton.1), channel_id=1, source_target_pairs={{448,0},{456,8},{464,16},{472,24},{480,32},{488,40},{496,48},{504,... | collective-permute-start | bytes 196616 | tf_op jit(solution)/shard_map/ppermute | solution.py:282
  16.7 9.5 %collective-permute-done = f32[64,256]{1,0:T(8,128)S(1)} collective-permute-done((f32[64,256]{1,0:T(8,128)S(1)}, f32[64,256]{1,0:T(8,128)S(1)}, u32[]{:S(2)}, u32[]{:S(2)}) %collective-permute-start) | collective-permute-done | bytes 65568 | tf_op jit(solution)/shard_map/ppermute | solution.py:282
  26.3 5.4 %collective-permute-start.1 = (f32[2,64,256]{2,1,0:T(8,128)S(1)}, f32[2,64,256]{2,1,0:T(8,128)S(1)}, u32[]{:S(2)}, u32[]{:S(2)}) collective-permute-start(f32[2,64,256]{2,1,0:T(8,128)S(1)} %pad_maximum_fusion.1), channel_id=1, source_target_pairs={{32,0},{40,8},{48,16},{56,24},{64,32},{72,40},{80,48},{88,56},{96,... | collective-permute-start | bytes 393224 | tf_op jit(solution)/shard_map/ppermute | solution.py:282
  31.7 2.6 %collective-permute-done.1 = f32[2,64,256]{2,1,0:T(8,128)S(1)} collective-permute-done((f32[2,64,256]{2,1,0:T(8,128)S(1)}, f32[2,64,256]{2,1,0:T(8,128)S(1)}, u32[]{:S(2)}, u32[]{:S(2)}) %collective-permute-start.1) | collective-permute-done | bytes 131104 | tf_op jit(solution)/shard_map/ppermute | solution.py:282
  34.3 2.7 %collective-permute-start.2 = (f32[4,64,256]{2,1,0:T(8,128)S(1)}, f32[4,64,256]{2,1,0:T(8,128)S(1)}, u32[]{:S(2)}, u32[]{:S(2)}) collective-permute-start(f32[4,64,256]{2,1,0:T(8,128)S(1)} %pad_maximum_fusion.near0), channel_id=1, source_target_pairs={{8,0},{16,8},{24,16},{32,24},{40,32},{48,40},{56,48},{64,56},{72,6... | collective-permute-start | bytes 786440 | tf_op jit(solution)/shard_map/ppermute | solution.py:282
  36.9 7.5 %collective-permute-start.3 = (f32[4,64,256]{2,1,0:T(8,128)S(1)}, f32[4,64,256]{2,1,0:T(8,128)S(1)}, u32[]{:S(2)}, u32[]{:S(2)}) collective-permute-start(f32[4,64,256]{2,1,0:T(8,128)S(1)} %pad_maximum_fusion.near0), channel_id=1, source_target_pairs={{24,0},{32,8},{40,16},{48,24},{56,32},{64,40},{72,48},{80,56},{88,... | collective-permute-start | bytes 786440 | tf_op jit(solution)/shard_map/ppermute | solution.py:282
  44.4 3.0 %collective-permute-done.2.near1 = f32[4,64,256]{2,1,0:T(8,128)S(1)} collective-permute-done((f32[4,64,256]{2,1,0:T(8,128)S(1)}, f32[4,64,256]{2,1,0:T(8,128)S(1)}, u32[]{:S(2)}, u32[]{:S(2)}) %collective-permute-start.2) | collective-permute-done | bytes 262176 | tf_op jit(solution)/shard_map/ppermute | solution.py:282
  47.4 1.9 %collective-permute-start.4 = (f32[2,64,256]{2,1,0:T(8,128)S(1)}, f32[2,64,256]{2,1,0:T(8,128)S(1)}, u32[]{:S(2)}, u32[]{:S(2)}) collective-permute-start(f32[2,64,256]{2,1,0:T(8,128)S(1)} %slice.8), channel_id=1, source_target_pairs={{8,0},{16,8},{24,16},{32,24},{40,32},{48,40},{56,48},{64,56},{72,6... | collective-permute-start | bytes 393224 | tf_op jit(solution)/shard_map/ppermute | solution.py:282
  49.4 0.0 collective-permute-done.3.near3
  49.4 9.5 %collective-permute-start.5 = (f32[2,64,256]{2,1,0:T(8,128)S(1)}, f32[2,64,256]{2,1,0:T(8,128)S(1)}, u32[]{:S(2)}, u32[]{:S(2)}) collective-permute-start(f32[2,64,256]{2,1,0:T(8,128)S(1)} %slice.9), channel_id=1, source_target_pairs={{24,0},{32,8},{40,16},{48,24},{56,32},{64,40},{72,48},{80,56},{88,... | collective-permute-start | bytes 393224 | tf_op jit(solution)/shard_map/ppermute | solution.py:282
  58.9 7.5 %collective-permute-start.6 = (f32[64,256]{1,0:T(8,128)S(1)}, f32[64,256]{1,0:T(8,128)S(1)}, u32[]{:S(2)}, u32[]{:S(2)}) collective-permute-start(f32[64,256]{1,0:T(8,128)S(1)} %skeleton.1), channel_id=1, source_target_pairs={{256,0},{264,8},{272,16},{280,24},{288,32},{296,40},{304,48},{312,... | collective-permute-start | bytes 196616 | tf_op jit(solution)/shard_map/ppermute | solution.py:282
  66.4 7.5 %collective-permute-done.6.far = f32[64,256]{1,0:T(8,128)S(1)} collective-permute-done((f32[64,256]{1,0:T(8,128)S(1)}, f32[64,256]{1,0:T(8,128)S(1)}, u32[]{:S(2)}, u32[]{:S(2)}) %collective-permute-start.6) | collective-permute-done | bytes 65568 | tf_op jit(solution)/shard_map/ppermute | solution.py:282
  73.8 0.0 collective-permute-done.4.relay1
  73.8 0.0 collective-permute-done.5.relay3
  73.8 1.7 %order.1 = f32[8,2,64,256]{3,2,1,0:T(8,128)} custom-call(s32[64]{0:T(128)S(1)} %get-tuple-element.11.facts_ref, f32[4,64,256]{2,1,0:T(8,128)S(1)} %pad_maximum_fusion.near0, f32[4,64,256]{2,1,0:T(8,128)S(1)} %collective-permute-done.2.near1, f32[4,64,256]{2,1,0:T(8,128)S(1)} %collective-permute-done.3.near3, ...), custom_call_target="tpu_custom_call" | custom-call | tf_op jit(solution)/shard_map/order/pallas_call | solution.py:312
  75.5 0.0 all-to-all-done.db_ref
  75.5 4.3 %all-to-all-start.1 = ((f32[8,2,64,256]{3,2,1,0:T(8,128)}), f32[8,2,64,256]{3,2,1,0:T(8,128)S(1)}, u32[]{:S(2)}, u32[]{:S(2)}) async-start(f32[8,2,64,256]{3,2,1,0:T(8,128)} %order.1), calls=%async_computation.1 | async-start | bytes 2097152 | tf_op jit(solution)/shard_map/all_to_all | solution.py:321
  79.9 14.0 %factor.1 = (bf16[512,256]{1,0:T(8,128)(2,1)S(1)}, bf16[512,256]{1,0:T(8,128)(2,1)S(1)}, f32[32,256]{1,0:T(8,128)S(1)}, f32[32,256]{1,0:T(8,128)}) custom-call(s32[1]{0:T(128)} %bitcast.1.column_ref, f32[8,128,512]{2,1,0:T(8,128)S(1)} %all-to-all-done.db_ref), custom_call_target="tpu_custom_call" | custom-call | flops 6000000000 | bytes 4000000 | tf_op jit(solution)/shard_map/factor/pallas_call | solution.py:323
  93.8 2.4 %project.1 = (bf16[2,256,512]{2,1,0:T(8,128)(2,1)S(1)}, bf16[2,256,512]{2,1,0:T(8,128)(2,1)S(1)}) custom-call(f32[2,512,512]{2,1,0:T(8,128)} %bitcast.21, bf16[512,256]{1,0:T(8,128)(2,1)S(1)} %get-tuple-element.13.high_ref, bf16[512,256]{1,0:T(8,128)(2,1)S(1)} %get-tuple-element.14.low_ref), custom_call_target="tpu_custom_call" | custom-call | flops 1000000000 | bytes 4000000 | tf_op jit(solution)/shard_map/project/pallas_call | solution.py:339
  96.3 0.0 all-to-all-done.1.routed_ref
  96.3 1.3 %side.1 = f32[8,32,256]{2,1,0:T(8,128)} custom-call(s32[64]{0:T(128)S(1)} %get-tuple-element.11.facts_ref, bf16[2,256,512]{2,1,0:T(8,128)(2,1)S(1)} %get-tuple-element.15.high_ref, bf16[2,256,512]{2,1,0:T(8,128)(2,1)S(1)} %get-tuple-element.16.low_ref, f32[8,2,64,256]{3,2,1,0:T(8,128)S(1)} %all-to-all-done.1.routed_ref), custom_call_target="tpu_custom_call" | custom-call | flops 200000000 | bytes 2000000 | tf_op jit(solution)/shard_map/side/pallas_call | solution.py:352
  97.6 4.9 %all-to-all-start.2 = ((f32[8,32,256]{2,1,0:T(8,128)}), f32[8,32,256]{2,1,0:T(8,128)S(1)}, u32[]{:S(2)}, u32[]{:S(2)}) async-start(f32[8,32,256]{2,1,0:T(8,128)} %side.1), calls=%async_computation.2 | async-start | bytes 524288 | tf_op jit(solution)/shard_map/all_to_all | solution.py:361
  102.5 2.0 %couple.1 = f32[2,256,256]{2,1,0:T(8,128)} custom-call(s32[64]{0:T(128)S(1)} %get-tuple-element.11.facts_ref, bf16[2,256,512]{2,1,0:T(8,128)(2,1)S(1)} %get-tuple-element.15.high_ref, bf16[2,256,512]{2,1,0:T(8,128)(2,1)S(1)} %get-tuple-element.16.low_ref, f32[8,2,64,256]{3,2,1,0:T(8,128)S(1)} %all-to-all-done.1.routed_ref), custom_call_target="tpu_custom_call" | custom-call | flops 400000000 | bytes 4000000 | tf_op jit(solution)/shard_map/couple/pallas_call | solution.py:362
  104.4 5.6 %all-to-all-done.2.parts_ref = f32[8,32,256]{2,1,0:T(8,128)S(1)} async-done(((f32[8,32,256]{2,1,0:T(8,128)}), f32[8,32,256]{2,1,0:T(8,128)S(1)}, u32[]{:S(2)}, u32[]{:S(2)}) %all-to-all-start.2) | async-done | bytes 262176 | tf_op jit(solution)/shard_map/all_to_all | solution.py:361
  110.0 1.2 %merge.1 = f32[32,512]{1,0:T(8,128)} custom-call(s32[64]{0:T(128)S(1)} %get-tuple-element.11.facts_ref, f32[8,32,256]{2,1,0:T(8,128)S(1)} %all-to-all-done.2.parts_ref, f32[32,256]{1,0:T(8,128)S(1)} %get-tuple-element.17.schur_ref), custom_call_target="tpu_custom_call" | custom-call | tf_op jit(solution)/shard_map/merge/pallas_call | solution.py:371
  (4 shorter events, 0.0 us)
Async XLA Ops:
  0.7 0.7 copy-start
  1.4 0.7 copy-start.1
  2.1 0.7 copy-start.2
  6.4 69.1 %all-to-all-start = ((f32[8,128,512]{2,1,0:T(8,128)}), f32[8,128,512]{2,1,0:T(8,128)S(1)}, u32[]{:S(2)}, u32[]{:S(2)}) async-start(f32[8,128,512]{2,1,0:T(8,128)} %get-tuple-element.12), calls=%async_computation | async-start | bytes 4194304 | tf_op jit(solution)/shard_map/all_to_all | solution.py:306
  11.5 14.7 %collective-permute-start = (f32[64,256]{1,0:T(8,128)S(1)}, f32[64,256]{1,0:T(8,128)S(1)}, u32[]{:S(2)}, u32[]{:S(2)}) collective-permute-start(f32[64,256]{1,0:T(8,128)S(1)} %skeleton.1), channel_id=1, source_target_pairs={{448,0},{456,8},{464,16},{472,24},{480,32},{488,40},{496,48},{504,... | collective-permute-start | bytes 196616 | tf_op jit(solution)/shard_map/ppermute | solution.py:282
  26.3 8.0 %collective-permute-start.1 = (f32[2,64,256]{2,1,0:T(8,128)S(1)}, f32[2,64,256]{2,1,0:T(8,128)S(1)}, u32[]{:S(2)}, u32[]{:S(2)}) collective-permute-start(f32[2,64,256]{2,1,0:T(8,128)S(1)} %pad_maximum_fusion.1), channel_id=1, source_target_pairs={{32,0},{40,8},{48,16},{56,24},{64,32},{72,40},{80,48},{88,56},{96,... | collective-permute-start | bytes 393224 | tf_op jit(solution)/shard_map/ppermute | solution.py:282
  34.3 13.2 %collective-permute-start.2 = (f32[4,64,256]{2,1,0:T(8,128)S(1)}, f32[4,64,256]{2,1,0:T(8,128)S(1)}, u32[]{:S(2)}, u32[]{:S(2)}) collective-permute-start(f32[4,64,256]{2,1,0:T(8,128)S(1)} %pad_maximum_fusion.near0), channel_id=1, source_target_pairs={{8,0},{16,8},{24,16},{32,24},{40,32},{48,40},{56,48},{64,56},{72,6... | collective-permute-start | bytes 786440 | tf_op jit(solution)/shard_map/ppermute | solution.py:282
  36.9 12.5 %collective-permute-start.3 = (f32[4,64,256]{2,1,0:T(8,128)S(1)}, f32[4,64,256]{2,1,0:T(8,128)S(1)}, u32[]{:S(2)}, u32[]{:S(2)}) collective-permute-start(f32[4,64,256]{2,1,0:T(8,128)S(1)} %pad_maximum_fusion.near0), channel_id=1, source_target_pairs={{24,0},{32,8},{40,16},{48,24},{56,32},{64,40},{72,48},{80,56},{88,... | collective-permute-start | bytes 786440 | tf_op jit(solution)/shard_map/ppermute | solution.py:282
  47.4 26.4 %collective-permute-start.4 = (f32[2,64,256]{2,1,0:T(8,128)S(1)}, f32[2,64,256]{2,1,0:T(8,128)S(1)}, u32[]{:S(2)}, u32[]{:S(2)}) collective-permute-start(f32[2,64,256]{2,1,0:T(8,128)S(1)} %slice.8), channel_id=1, source_target_pairs={{8,0},{16,8},{24,16},{32,24},{40,32},{48,40},{56,48},{64,56},{72,6... | collective-permute-start | bytes 393224 | tf_op jit(solution)/shard_map/ppermute | solution.py:282
  49.4 24.4 %collective-permute-start.5 = (f32[2,64,256]{2,1,0:T(8,128)S(1)}, f32[2,64,256]{2,1,0:T(8,128)S(1)}, u32[]{:S(2)}, u32[]{:S(2)}) collective-permute-start(f32[2,64,256]{2,1,0:T(8,128)S(1)} %slice.9), channel_id=1, source_target_pairs={{24,0},{32,8},{40,16},{48,24},{56,32},{64,40},{72,48},{80,56},{88,... | collective-permute-start | bytes 393224 | tf_op jit(solution)/shard_map/ppermute | solution.py:282
  58.9 14.9 %collective-permute-start.6 = (f32[64,256]{1,0:T(8,128)S(1)}, f32[64,256]{1,0:T(8,128)S(1)}, u32[]{:S(2)}, u32[]{:S(2)}) collective-permute-start(f32[64,256]{1,0:T(8,128)S(1)} %skeleton.1), channel_id=1, source_target_pairs={{256,0},{264,8},{272,16},{280,24},{288,32},{296,40},{304,48},{312,... | collective-permute-start | bytes 196616 | tf_op jit(solution)/shard_map/ppermute | solution.py:282
  75.5 20.7 %all-to-all-start.1 = ((f32[8,2,64,256]{3,2,1,0:T(8,128)}), f32[8,2,64,256]{3,2,1,0:T(8,128)S(1)}, u32[]{:S(2)}, u32[]{:S(2)}) async-start(f32[8,2,64,256]{3,2,1,0:T(8,128)} %order.1), calls=%async_computation.1 | async-start | bytes 2097152 | tf_op jit(solution)/shard_map/all_to_all | solution.py:321
  97.6 12.4 %all-to-all-start.2 = ((f32[8,32,256]{2,1,0:T(8,128)}), f32[8,32,256]{2,1,0:T(8,128)S(1)}, u32[]{:S(2)}, u32[]{:S(2)}) async-start(f32[8,32,256]{2,1,0:T(8,128)} %side.1), calls=%async_computation.2 | async-start | bytes 524288 | tf_op jit(solution)/shard_map/all_to_all | solution.py:361

commit v3 on v2

--- a/solution.py
+++ b/solution.py
@@ -133,54 +133,44 @@
 FIRST, LIVE = 32, 33
 
 
-def spread_kernel(
-    place_ref, index_ref, mask_ref, parent_ref, diag_ref, bases_ref, out_ref, facts_ref, both, sem
-):
+def spread_kernel(diag_ref, bases_ref, out_ref, both, sem):
     rows = diag_ref.shape[0]
     pair = (diag_ref, bases_ref)
-    loads = [pltpu.make_async_copy(ref, both.at[pl.ds(q * rows, rows)], sem.at[q]) for q, ref in enumerate(pair)]
-    for load in loads:
-        load.start()
-    own, column = place_ref[0], place_ref[1]
+    run_copies(
+        [pltpu.make_async_copy(ref, both.at[pl.ds(q * rows, rows)], sem.at[q]) for q, ref in enumerate(pair)]
+    )
+    run_copies([pltpu.make_async_copy(both, out_ref.at[p], sem.at[p]) for p in range(out_ref.shape[0])])
+
+
+def facts_kernel(index_ref, mask_ref, parent_ref, facts_ref):
+    own, column = lax.axis_index("clu"), lax.axis_index("col")
     slots, clusters = index_ref.shape
     half = slots // 2
     for k in range(slots):
         offset = (index_ref[k, own] - own + clusters + half) % clusters
         facts_ref[jnp.where(offset < slots, offset, half)] = k
-    for load in loads:
-        load.wait()
-    stores = [pltpu.make_async_copy(both, out_ref.at[p], sem.at[p]) for p in range(out_ref.shape[0])]
-    for store in stores:
-        store.start()
     sibling = find_sibling(own, parent_ref)
     facts_ref[FIRST] = (own < sibling).astype(jnp.int32)
-    count = slots // out_ref.shape[0]
+    count = slots // lax.axis_size("col")
     for k in range(count):
         slot = column * count + k
         live = mask_ref[0, slot]
         facts_ref[LIVE + 2 * k] = live
         facts_ref[LIVE + 2 * k + 1] = jnp.where(index_ref[slot, own] == sibling, live, 0)
-    for store in stores:
-        store.wait()
-
-
-def order_kernel(facts_ref, near0, near1, near3, relay1, relay3, far, out_ref, sem):
-    sources = (
-        [near0.at[0], near0.at[2], far, near0.at[3]],
-        [near1.at[0], near1.at[2], near1.at[1], near1.at[3]],
-        [relay1.at[0], relay3.at[0], relay1.at[1], relay3.at[1]],
-        [near3.at[0], near3.at[2], near3.at[1], near3.at[3]],
-    )
+
+
+def order_kernel(facts_ref, near0, near1, near2, near3, far, out_ref, sem):
+    stacks = (near0, near1, near2, near3)
     copies = []
     for d in range(16):
         slot = facts_ref[d]
-        target = out_ref.at[slot // 2, slot % 2]
-        copies.append(pltpu.make_async_copy(sources[d % 4][d // 4], target, sem.at[d]))
+        source = far if d == 8 else stacks[d % 4].at[d // 4]
+        copies.append(pltpu.make_async_copy(source, out_ref.at[slot // 2, slot % 2], sem.at[d]))
     run_copies(copies)
 
 
 def factor_kernel(
-    column_ref, db_ref, high_ref, low_ref, schur_ref, factor_ref, work, upper1, upper2, full, solve_ref
+    db_ref, high_ref, low_ref, schur_ref, factor_ref, work, upper1, upper2, full, solve_ref
 ):
     rows = db_ref.shape[1] // 2
     size = db_ref.shape[0] * rows
@@ -212,7 +202,7 @@
     solve_ref[HALF:, :] = dot_full(inv2, couple2, first)
     lift = basis[:, red:] - dot3(split2(basis[:, :red]), split2(solve_ref[...]))
     high_ref[...], low_ref[...] = split2(lift)
-    column = column_ref[0]
+    column = lax.axis_index("col")
     count = schur_ref.shape[0]
     start = pl.multiple_of(column * count, count)
     full[...] = corner - (
@@ -271,9 +261,6 @@
 def shards(near_blocks, diag_block, bases, near_index, near_mask, parent_map):
     columns = lax.axis_size("col")
     clusters = lax.axis_size("clu")
-    column = lax.axis_index("col").astype(jnp.int32)
-    own = lax.axis_index("clu").astype(jnp.int32)
-    place = jnp.stack([own, column])
     rows, size = bases.shape[1:]
     per_device = near_blocks.shape[1]
     shape = jax.ShapeDtypeStruct
@@ -290,34 +277,41 @@
         compiler_params=params(4),
         name="skeleton",
     )(keep_out(bases[0]))
+    far = shift(skeleton, clusters // 2)
     down8 = shift(skeleton, -8)
-    far = shift(skeleton, clusters // 2)
-    pair = jnp.stack([down8, skeleton])
-    up4 = shift(pair, 4)
-    spread, facts = pl.pallas_call(
+    down4 = shift(skeleton, -4)
+    up4 = shift(skeleton, 4)
+    spread = pl.pallas_call(
         spread_kernel,
-        out_shape=(pltpu.HBM((columns, 2 * rows, size), F32), shape((64,), jnp.int32)),
-        in_specs=[SMEM] * 4 + [HBM] * 2,
-        out_specs=(HBM, SMEM),
+        out_shape=pltpu.HBM((columns, 2 * rows, size), F32),
+        in_specs=[HBM] * 2,
+        out_specs=HBM,
         scratch_shapes=[pltpu.VMEM((2 * rows, size), F32), pltpu.SemaphoreType.DMA((columns,))],
         compiler_params=params(4),
         name="spread",
-    )(place, near_index.T, near_mask, parent_map, keep_out(diag_block[0]), keep_out(bases[0]))
+    )(keep_out(diag_block[0]), keep_out(bases[0]))
     db = lax.all_to_all(spread, "col", split_axis=0, concat_axis=0, tiled=False)
-    near0 = jnp.concatenate([pair, up4], axis=0)
+    near0 = jnp.stack([down8, down4, skeleton, up4])
+    near2 = shift(near0, 2)
     near1 = shift(near0, 1)
     near3 = shift(near0, 3)
-    relay1 = shift(near1[:2], 1)
-    relay3 = shift(near3[:2], 3)
+    facts = pl.pallas_call(
+        facts_kernel,
+        out_shape=shape((64,), jnp.int32),
+        in_specs=[SMEM] * 3,
+        out_specs=SMEM,
+        name="facts",
+    )(near_index.T, near_mask, parent_map)
+    facts = keep_out(facts)
     ordered = pl.pallas_call(
         order_kernel,
         out_shape=pltpu.HBM((columns, per_device, rows, RANK), F32),
-        in_specs=[SMEM] + [ANY] * 6,
+        in_specs=[SMEM] + [ANY] * 5,
         out_specs=HBM,
         compiler_params=params(2),
         scratch_shapes=[pltpu.SemaphoreType.DMA((near_index.shape[1],))],
         name="order",
-    )(facts, near0, near1, near3, relay1, relay3, far)
+    )(facts, near0, near1, near2, near3, far)
     routed = lax.all_to_all(ordered, "col", split_axis=0, concat_axis=0, tiled=False)
     count = RANK // columns
     high, low, schur, factor = pl.pallas_call(
@@ -328,13 +322,13 @@
             shape((count, RANK), F32),
             shape(((size - RANK) // columns, size - RANK), F32),
         ),
-        in_specs=[SMEM, VMEM],
+        in_specs=[VMEM],
         out_specs=(VMEM,) * 4,
         scratch_shapes=[pltpu.VMEM((HALF, 2 * HALF), F32)] * 3 + [pltpu.VMEM((RANK, RANK), F32)] * 2,
         cost_estimate=pl.CostEstimate(flops=6_000_000_000, bytes_accessed=4_000_000, transcendentals=0),
         compiler_params=params(24),
         name="factor",
-    )(column[None], db)
+    )(db)
     projected = (per_device, RANK, size)
     rows_high, rows_low = pl.pallas_call(
         project_kernel,

time: 113 us -> 104 us (0.920)
  the two profiles are of different devices: /device:TPU:24 before, /device:TPU:32 now
where the time goes in v3:
time: 104 us; the launch traced here: 103 us
  starting transfers between devices  43 us (41%)
  waiting for transfers between devices  31.8 us (31%)
  Pallas kernels  27.6 us (27%)
    ppermute x7, starting transfers between devices, shift(): lax.ppermute(x, 'clu', [((i + d) % clusters, i) for i in range(clusters)])  30.4 us
    ppermute x7, waiting for transfers between devices, shift(): lax.ppermute(x, 'clu', [((i + d) % clusters, i) for i in range(clusters)])  26.3 us
    pallas_call x1, Pallas kernels, shards(): pl.pallas_call(factor_kernel, out_shape=(shape((size, RANK), BF16), shape...  13.9 us
    all_to_all x1, waiting for transfers between devices, shards(): lax.all_to_all(side, 'col', split_axis=0, concat_axis=0, tiled=False)  5.46 us
    all_to_all x1, starting transfers between devices, shards(): lax.all_to_all(side, 'col', split_axis=0, concat_axis=0, tiled=False)  4.72 us
    all_to_all x1, starting transfers between devices, shards(): db = lax.all_to_all(spread, 'col', split_axis=0, concat_axis=0, tiled=False)  4.31 us
    all_to_all x1, starting transfers between devices, shards(): lax.all_to_all(ordered, 'col', split_axis=0, concat_axis=0, tiled=False)  3.57 us
    pallas_call x1, Pallas kernels, shards(): pl.pallas_call(project_kernel, out_shape=(shape(projected, BF16),) * 2, i...  2.45 us
  transfers between devices with their start and end apart: 10, of which 4 were waited for; matrix products, arithmetic and copies ran while one was open for 0% of the time, Pallas kernels for 22%

profile of v3, /device:TPU:32, one launch (start us, length us, event | category | flops | bytes accessed | tf_op | source)
XLA Modules:
  0.0 103.2 jit_solution(7192262167858157774)
XLA Ops:
  0.6 2.4 %spread.1 = f32[8,128,512]{2,1,0:T(8,128)} custom-call(f32[64,512]{1,0:T(8,128)} %bitcast.15, f32[64,512]{1,0:T(8,128)} %bitcast.12), custom_call_target="tpu_custom_call" | custom-call | tf_op jit(solution)/shard_map/spread/pallas_call | solution.py:284
  3.0 4.3 %all-to-all-start = ((f32[8,128,512]{2,1,0:T(8,128)}), f32[8,128,512]{2,1,0:T(8,128)S(1)}, u32[]{:S(2)}, u32[]{:S(2)}) async-start(f32[8,128,512]{2,1,0:T(8,128)} %spread.1), calls=%async_computation | async-start | bytes 4194304 | tf_op jit(solution)/shard_map/all_to_all | solution.py:293
  7.3 0.8 skeleton.1
  8.2 6.7 %collective-permute-start.2 = (f32[64,256]{1,0:T(8,128)S(1)}, f32[64,256]{1,0:T(8,128)S(1)}, u32[]{:S(2)}, u32[]{:S(2)}) collective-permute-start(f32[64,256]{1,0:T(8,128)S(1)} %skeleton.1), channel_id=1, source_target_pairs={{32,0},{40,8},{48,16},{56,24},{64,32},{72,40},{80,48},{88,56},{96,... | collective-permute-start | bytes 196616 | tf_op jit(solution)/shard_map/ppermute | solution.py:269
  14.9 1.9 %collective-permute-start.1 = (f32[64,256]{1,0:T(8,128)S(1)}, f32[64,256]{1,0:T(8,128)S(1)}, u32[]{:S(2)}, u32[]{:S(2)}) collective-permute-start(f32[64,256]{1,0:T(8,128)S(1)} %skeleton.1), channel_id=1, source_target_pairs={{480,0},{488,8},{496,16},{504,24},{0,32},{8,40},{16,48},{24,56},{3... | collective-permute-start | bytes 196616 | tf_op jit(solution)/shard_map/ppermute | solution.py:269
  16.8 3.6 %collective-permute-start = (f32[64,256]{1,0:T(8,128)S(1)}, f32[64,256]{1,0:T(8,128)S(1)}, u32[]{:S(2)}, u32[]{:S(2)}) collective-permute-start(f32[64,256]{1,0:T(8,128)S(1)} %skeleton.1), channel_id=1, source_target_pairs={{448,0},{456,8},{464,16},{472,24},{480,32},{488,40},{496,48},{504,... | collective-permute-start | bytes 196616 | tf_op jit(solution)/shard_map/ppermute | solution.py:269
  20.4 0.0 collective-permute-done.2
  20.4 3.6 %collective-permute-done.1 = f32[64,256]{1,0:T(8,128)S(1)} collective-permute-done((f32[64,256]{1,0:T(8,128)S(1)}, f32[64,256]{1,0:T(8,128)S(1)}, u32[]{:S(2)}, u32[]{:S(2)}) %collective-permute-start.1) | collective-permute-done | bytes 65568 | tf_op jit(solution)/shard_map/ppermute | solution.py:269
  24.1 5.8 %collective-permute-done = f32[64,256]{1,0:T(8,128)S(1)} collective-permute-done((f32[64,256]{1,0:T(8,128)S(1)}, f32[64,256]{1,0:T(8,128)S(1)}, u32[]{:S(2)}, u32[]{:S(2)}) %collective-permute-start) | collective-permute-done | bytes 65568 | tf_op jit(solution)/shard_map/ppermute | solution.py:269
  29.9 4.8 %collective-permute-start.3 = (f32[4,64,256]{2,1,0:T(8,128)S(1)}, f32[4,64,256]{2,1,0:T(8,128)S(1)}, u32[]{:S(2)}, u32[]{:S(2)}) collective-permute-start(f32[4,64,256]{2,1,0:T(8,128)S(1)} %pad_maximum_fusion.near0), channel_id=1, source_target_pairs={{8,0},{16,8},{24,16},{32,24},{40,32},{48,40},{56,48},{64,56},{72,6... | collective-permute-start | bytes 786440 | tf_op jit(solution)/shard_map/ppermute | solution.py:269
  34.7 2.5 %collective-permute-start.4 = (f32[4,64,256]{2,1,0:T(8,128)S(1)}, f32[4,64,256]{2,1,0:T(8,128)S(1)}, u32[]{:S(2)}, u32[]{:S(2)}) collective-permute-start(f32[4,64,256]{2,1,0:T(8,128)S(1)} %pad_maximum_fusion.near0), channel_id=1, source_target_pairs={{16,0},{24,8},{32,16},{40,24},{48,32},{56,40},{64,48},{72,56},{80,... | collective-permute-start | bytes 786440 | tf_op jit(solution)/shard_map/ppermute | solution.py:269
  37.2 4.3 %collective-permute-start.5 = (f32[4,64,256]{2,1,0:T(8,128)S(1)}, f32[4,64,256]{2,1,0:T(8,128)S(1)}, u32[]{:S(2)}, u32[]{:S(2)}) collective-permute-start(f32[4,64,256]{2,1,0:T(8,128)S(1)} %pad_maximum_fusion.near0), channel_id=1, source_target_pairs={{24,0},{32,8},{40,16},{48,24},{56,32},{64,40},{72,48},{80,56},{88,... | collective-permute-start | bytes 786440 | tf_op jit(solution)/shard_map/ppermute | solution.py:269
  41.5 6.5 %collective-permute-start.6 = (f32[64,256]{1,0:T(8,128)S(1)}, f32[64,256]{1,0:T(8,128)S(1)}, u32[]{:S(2)}, u32[]{:S(2)}) collective-permute-start(f32[64,256]{1,0:T(8,128)S(1)} %skeleton.1), channel_id=1, source_target_pairs={{256,0},{264,8},{272,16},{280,24},{288,32},{296,40},{304,48},{312,... | collective-permute-start | bytes 196616 | tf_op jit(solution)/shard_map/ppermute | solution.py:269
  48.1 1.5 %facts.1.facts_ref = s32[64]{0:T(128)} custom-call(s32[16,64]{1,0:T(8,128)} %bitcast.20, s32[1,16]{1,0:T(1,128)} %mask_ref.1, s32[64]{0:T(128)} %parent_ref.1), custom_call_target="tpu_custom_call" | custom-call | tf_op jit(solution)/shard_map/facts/pallas_call | solution.py:298
  49.6 16.9 %collective-permute-done.6.far = f32[64,256]{1,0:T(8,128)S(1)} collective-permute-done((f32[64,256]{1,0:T(8,128)S(1)}, f32[64,256]{1,0:T(8,128)S(1)}, u32[]{:S(2)}, u32[]{:S(2)}) %collective-permute-start.6) | collective-permute-done | bytes 65568 | tf_op jit(solution)/shard_map/ppermute | solution.py:269
  66.5 0.0 collective-permute-done.3.near1
  66.5 0.0 collective-permute-done.4.near2
  66.5 0.0 collective-permute-done.5.near3
  66.5 1.8 %order.1 = f32[8,2,64,256]{3,2,1,0:T(8,128)} custom-call(s32[64]{0:T(128)} %facts.1.facts_ref, f32[4,64,256]{2,1,0:T(8,128)S(1)} %pad_maximum_fusion.near0, f32[4,64,256]{2,1,0:T(8,128)S(1)} %collective-permute-done.3.near1, f32[4,64,256]{2,1,0:T(8,128)S(1)} %collective-permute-done.4.near2, f32[4,64,256]{2,1,0:T(8,128)S(1)} %collective-permute-done.5.near3, ...), custom_call_target="tpu_custom_call" | custom-call | tf_op jit(solution)/shard_map/order/pallas_call | solution.py:306
  68.3 0.0 all-to-all-done.db_ref
  68.3 3.6 %all-to-all-start.1 = ((f32[8,2,64,256]{3,2,1,0:T(8,128)}), f32[8,2,64,256]{3,2,1,0:T(8,128)S(1)}, u32[]{:S(2)}, u32[]{:S(2)}) async-start(f32[8,2,64,256]{3,2,1,0:T(8,128)} %order.1), calls=%async_computation.1 | async-start | bytes 2097152 | tf_op jit(solution)/shard_map/all_to_all | solution.py:315
  71.9 13.9 %factor.1 = (bf16[512,256]{1,0:T(8,128)(2,1)S(1)}, bf16[512,256]{1,0:T(8,128)(2,1)S(1)}, f32[32,256]{1,0:T(8,128)S(1)}, f32[32,256]{1,0:T(8,128)}) custom-call(f32[8,128,512]{2,1,0:T(8,128)S(1)} %all-to-all-done.db_ref), custom_call_target="tpu_custom_call" | custom-call | flops 6000000000 | bytes 4000000 | tf_op jit(solution)/shard_map/factor/pallas_call | solution.py:317
  85.8 2.4 %project.1 = (bf16[2,256,512]{2,1,0:T(8,128)(2,1)S(1)}, bf16[2,256,512]{2,1,0:T(8,128)(2,1)S(1)}) custom-call(f32[2,512,512]{2,1,0:T(8,128)} %bitcast.21, bf16[512,256]{1,0:T(8,128)(2,1)S(1)} %get-tuple-element.9.high_ref, bf16[512,256]{1,0:T(8,128)(2,1)S(1)} %get-tuple-element.10.low_ref), custom_call_target="tpu_custom_call" | custom-call | flops 1000000000 | bytes 4000000 | tf_op jit(solution)/shard_map/project/pallas_call | solution.py:333
  88.3 0.0 all-to-all-done.1.routed_ref
  88.3 1.4 %side.1 = f32[8,32,256]{2,1,0:T(8,128)} custom-call(s32[64]{0:T(128)} %facts.1.facts_ref, bf16[2,256,512]{2,1,0:T(8,128)(2,1)S(1)} %get-tuple-element.11.high_ref, bf16[2,256,512]{2,1,0:T(8,128)(2,1)S(1)} %get-tuple-element.12.low_ref, f32[8,2,64,256]{3,2,1,0:T(8,128)S(1)} %all-to-all-done.1.routed_ref), custom_call_target="tpu_custom_call" | custom-call | flops 200000000 | bytes 2000000 | tf_op jit(solution)/shard_map/side/pallas_call | solution.py:346
  89.7 4.7 %all-to-all-start.2 = ((f32[8,32,256]{2,1,0:T(8,128)}), f32[8,32,256]{2,1,0:T(8,128)S(1)}, u32[]{:S(2)}, u32[]{:S(2)}) async-start(f32[8,32,256]{2,1,0:T(8,128)} %side.1), calls=%async_computation.2 | async-start | bytes 524288 | tf_op jit(solution)/shard_map/all_to_all | solution.py:355
  94.4 2.0 %couple.1 = f32[2,256,256]{2,1,0:T(8,128)} custom-call(s32[64]{0:T(128)} %facts.1.facts_ref, bf16[2,256,512]{2,1,0:T(8,128)(2,1)S(1)} %get-tuple-element.11.high_ref, bf16[2,256,512]{2,1,0:T(8,128)(2,1)S(1)} %get-tuple-element.12.low_ref, f32[8,2,64,256]{3,2,1,0:T(8,128)S(1)} %all-to-all-done.1.routed_ref), custom_call_target="tpu_custom_call" | custom-call | flops 400000000 | bytes 4000000 | tf_op jit(solution)/shard_map/couple/pallas_call | solution.py:356
  96.4 5.5 %all-to-all-done.2.parts_ref = f32[8,32,256]{2,1,0:T(8,128)S(1)} async-done(((f32[8,32,256]{2,1,0:T(8,128)}), f32[8,32,256]{2,1,0:T(8,128)S(1)}, u32[]{:S(2)}, u32[]{:S(2)}) %all-to-all-start.2) | async-done | bytes 262176 | tf_op jit(solution)/shard_map/all_to_all | solution.py:355
  101.9 1.3 %merge.1 = f32[32,512]{1,0:T(8,128)} custom-call(s32[64]{0:T(128)} %facts.1.facts_ref, f32[8,32,256]{2,1,0:T(8,128)S(1)} %all-to-all-done.2.parts_ref, f32[32,256]{1,0:T(8,128)S(1)} %get-tuple-element.13.schur_ref), custom_call_target="tpu_custom_call" | custom-call | tf_op jit(solution)/shard_map/merge/pallas_call | solution.py:365
  (1 shorter events, 0.0 us)
Async XLA Ops:
  3.0 65.3 %all-to-all-start = ((f32[8,128,512]{2,1,0:T(8,128)}), f32[8,128,512]{2,1,0:T(8,128)S(1)}, u32[]{:S(2)}, u32[]{:S(2)}) async-start(f32[8,128,512]{2,1,0:T(8,128)} %spread.1), calls=%async_computation | async-start | bytes 4194304 | tf_op jit(solution)/shard_map/all_to_all | solution.py:293
  8.2 12.3 %collective-permute-start.2 = (f32[64,256]{1,0:T(8,128)S(1)}, f32[64,256]{1,0:T(8,128)S(1)}, u32[]{:S(2)}, u32[]{:S(2)}) collective-permute-start(f32[64,256]{1,0:T(8,128)S(1)} %skeleton.1), channel_id=1, source_target_pairs={{32,0},{40,8},{48,16},{56,24},{64,32},{72,40},{80,48},{88,56},{96,... | collective-permute-start | bytes 196616 | tf_op jit(solution)/shard_map/ppermute | solution.py:269
  14.9 9.2 %collective-permute-start.1 = (f32[64,256]{1,0:T(8,128)S(1)}, f32[64,256]{1,0:T(8,128)S(1)}, u32[]{:S(2)}, u32[]{:S(2)}) collective-permute-start(f32[64,256]{1,0:T(8,128)S(1)} %skeleton.1), channel_id=1, source_target_pairs={{480,0},{488,8},{496,16},{504,24},{0,32},{8,40},{16,48},{24,56},{3... | collective-permute-start | bytes 196616 | tf_op jit(solution)/shard_map/ppermute | solution.py:269
  16.8 13.0 %collective-permute-start = (f32[64,256]{1,0:T(8,128)S(1)}, f32[64,256]{1,0:T(8,128)S(1)}, u32[]{:S(2)}, u32[]{:S(2)}) collective-permute-start(f32[64,256]{1,0:T(8,128)S(1)} %skeleton.1), channel_id=1, source_target_pairs={{448,0},{456,8},{464,16},{472,24},{480,32},{488,40},{496,48},{504,... | collective-permute-start | bytes 196616 | tf_op jit(solution)/shard_map/ppermute | solution.py:269
  29.9 36.6 %collective-permute-start.3 = (f32[4,64,256]{2,1,0:T(8,128)S(1)}, f32[4,64,256]{2,1,0:T(8,128)S(1)}, u32[]{:S(2)}, u32[]{:S(2)}) collective-permute-start(f32[4,64,256]{2,1,0:T(8,128)S(1)} %pad_maximum_fusion.near0), channel_id=1, source_target_pairs={{8,0},{16,8},{24,16},{32,24},{40,32},{48,40},{56,48},{64,56},{72,6... | collective-permute-start | bytes 786440 | tf_op jit(solution)/shard_map/ppermute | solution.py:269
  34.7 31.8 %collective-permute-start.4 = (f32[4,64,256]{2,1,0:T(8,128)S(1)}, f32[4,64,256]{2,1,0:T(8,128)S(1)}, u32[]{:S(2)}, u32[]{:S(2)}) collective-permute-start(f32[4,64,256]{2,1,0:T(8,128)S(1)} %pad_maximum_fusion.near0), channel_id=1, source_target_pairs={{16,0},{24,8},{32,16},{40,24},{48,32},{56,40},{64,48},{72,56},{80,... | collective-permute-start | bytes 786440 | tf_op jit(solution)/shard_map/ppermute | solution.py:269
  37.2 29.3 %collective-permute-start.5 = (f32[4,64,256]{2,1,0:T(8,128)S(1)}, f32[4,64,256]{2,1,0:T(8,128)S(1)}, u32[]{:S(2)}, u32[]{:S(2)}) collective-permute-start(f32[4,64,256]{2,1,0:T(8,128)S(1)} %pad_maximum_fusion.near0), channel_id=1, source_target_pairs={{24,0},{32,8},{40,16},{48,24},{56,32},{64,40},{72,48},{80,56},{88,... | collective-permute-start | bytes 786440 | tf_op jit(solution)/shard_map/ppermute | solution.py:269
  41.5 24.9 %collective-permute-start.6 = (f32[64,256]{1,0:T(8,128)S(1)}, f32[64,256]{1,0:T(8,128)S(1)}, u32[]{:S(2)}, u32[]{:S(2)}) collective-permute-start(f32[64,256]{1,0:T(8,128)S(1)} %skeleton.1), channel_id=1, source_target_pairs={{256,0},{264,8},{272,16},{280,24},{288,32},{296,40},{304,48},{312,... | collective-permute-start | bytes 196616 | tf_op jit(solution)/shard_map/ppermute | solution.py:269
  68.3 19.9 %all-to-all-start.1 = ((f32[8,2,64,256]{3,2,1,0:T(8,128)}), f32[8,2,64,256]{3,2,1,0:T(8,128)S(1)}, u32[]{:S(2)}, u32[]{:S(2)}) async-start(f32[8,2,64,256]{3,2,1,0:T(8,128)} %order.1), calls=%async_computation.1 | async-start | bytes 2097152 | tf_op jit(solution)/shard_map/all_to_all | solution.py:315
  89.7 12.2 %all-to-all-start.2 = ((f32[8,32,256]{2,1,0:T(8,128)}), f32[8,32,256]{2,1,0:T(8,128)S(1)}, u32[]{:S(2)}, u32[]{:S(2)}) async-start(f32[8,32,256]{2,1,0:T(8,128)} %side.1), calls=%async_computation.2 | async-start | bytes 524288 | tf_op jit(solution)/shard_map/all_to_all | solution.py:355

commit v4 on v3

--- a/solution.py
+++ b/solution.py
@@ -159,19 +159,28 @@
         facts_ref[LIVE + 2 * k + 1] = jnp.where(index_ref[slot, own] == sibling, live, 0)
 
 
-def order_kernel(facts_ref, near0, near1, near2, near3, far, out_ref, sem):
+def order_kernel(facts_ref, near0, near1, near2, relay3, near3, far, out_ref, sem):
     stacks = (near0, near1, near2, near3)
     copies = []
     for d in range(16):
         slot = facts_ref[d]
-        source = far if d == 8 else stacks[d % 4].at[d // 4]
+        if d == 8:
+            source = far
+        elif d % 4 == 2 and d // 4 >= 2:
+            source = relay3.at[d // 4 - 2]
+        else:
+            source = stacks[d % 4].at[d // 4]
         copies.append(pltpu.make_async_copy(source, out_ref.at[slot // 2, slot % 2], sem.at[d]))
     run_copies(copies)
 
 
 def factor_kernel(
-    db_ref, high_ref, low_ref, schur_ref, factor_ref, work, upper1, upper2, full, solve_ref
+    mine_ref, theirs_ref, high_ref, low_ref, schur_ref, factor_ref, db_ref, work, upper1, upper2, full, solve_ref
 ):
+    core = lax.axis_index("col") % 2
+    for x in range(mine_ref.shape[0]):
+        db_ref[2 * x + core] = mine_ref[x]
+        db_ref[2 * x + 1 - core] = theirs_ref[x]
     rows = db_ref.shape[1] // 2
     size = db_ref.shape[0] * rows
     diag = db_ref[:, :rows, :].reshape(size, size)
@@ -281,20 +290,26 @@
     down8 = shift(skeleton, -8)
     down4 = shift(skeleton, -4)
     up4 = shift(skeleton, 4)
+    chips = columns // 2
     spread = pl.pallas_call(
         spread_kernel,
-        out_shape=pltpu.HBM((columns, 2 * rows, size), F32),
+        out_shape=pltpu.HBM((chips, 2 * rows, size), F32),
         in_specs=[HBM] * 2,
         out_specs=HBM,
-        scratch_shapes=[pltpu.VMEM((2 * rows, size), F32), pltpu.SemaphoreType.DMA((columns,))],
+        scratch_shapes=[pltpu.VMEM((2 * rows, size), F32), pltpu.SemaphoreType.DMA((chips,))],
         compiler_params=params(4),
         name="spread",
     )(keep_out(diag_block[0]), keep_out(bases[0]))
-    db = lax.all_to_all(spread, "col", split_axis=0, concat_axis=0, tiled=False)
+    same_core = [[2 * x + core for x in range(chips)] for core in range(2)]
+    mine = lax.all_to_all(
+        spread, "col", split_axis=0, concat_axis=0, axis_index_groups=same_core, tiled=False
+    )
+    theirs = lax.ppermute(mine, "col", [(c, c ^ 1) for c in range(columns)])
     near0 = jnp.stack([down8, down4, skeleton, up4])
-    near2 = shift(near0, 2)
+    near2 = shift(jnp.stack([down8, down4]), 2)
     near1 = shift(near0, 1)
     near3 = shift(near0, 3)
+    relay3 = shift(near3[1:3], 3)
     facts = pl.pallas_call(
         facts_kernel,
         out_shape=shape((64,), jnp.int32),
@@ -306,12 +321,12 @@
     ordered = pl.pallas_call(
         order_kernel,
         out_shape=pltpu.HBM((columns, per_device, rows, RANK), F32),
-        in_specs=[SMEM] + [ANY] * 5,
+        in_specs=[SMEM] + [ANY] * 6,
         out_specs=HBM,
         compiler_params=params(2),
         scratch_shapes=[pltpu.SemaphoreType.DMA((near_index.shape[1],))],
         name="order",
-    )(facts, near0, near1, near2, near3, far)
+    )(facts, near0, near1, near2, relay3, near3, far)
     routed = lax.all_to_all(ordered, "col", split_axis=0, concat_axis=0, tiled=False)
     count = RANK // columns
     high, low, schur, factor = pl.pallas_call(
@@ -322,13 +337,15 @@
             shape((count, RANK), F32),
             shape(((size - RANK) // columns, size - RANK), F32),
         ),
-        in_specs=[VMEM],
+        in_specs=[VMEM] * 2,
         out_specs=(VMEM,) * 4,
-        scratch_shapes=[pltpu.VMEM((HALF, 2 * HALF), F32)] * 3 + [pltpu.VMEM((RANK, RANK), F32)] * 2,
+        scratch_shapes=[pltpu.VMEM((columns, 2 * rows, size), F32)]
+        + [pltpu.VMEM((HALF, 2 * HALF), F32)] * 3
+        + [pltpu.VMEM((RANK, RANK), F32)] * 2,
         cost_estimate=pl.CostEstimate(flops=6_000_000_000, bytes_accessed=4_000_000, transcendentals=0),
         compiler_params=params(24),
         name="factor",
-    )(db)
+    )(mine, theirs)
     projected = (per_device, RANK, size)
     rows_high, rows_low = pl.pallas_call(
         project_kernel,

time: 104 us -> 120 us (1.15)
  blocking collectives: 0 us -> 19.4 us
  waiting for transfers between devices: 31.8 us -> 24.5 us
  starting transfers between devices: 43 us -> 46.6 us
    all_to_all x0 -> x1, blocking collectives: none -> 19.4 us  [shards(): lax.all_to_all(spread, 'col', split_axis=0, concat_axis=0, axis_index_gro...]
    ppermute x7 -> x8, waiting for transfers between devices: 26.3 us -> 19 us  [shift(): lax.ppermute(x, 'clu', [((i + d) % clusters, i) for i in range(clusters)])]
    ppermute x7 -> x8, starting transfers between devices: 30.4 us -> 36.4 us  [shift(): lax.ppermute(x, 'clu', [((i + d) % clusters, i) for i in range(clusters)])]
    all_to_all x1 -> x0, starting transfers between devices: 4.31 us -> none  [shards(): db = lax.all_to_all(spread, 'col', split_axis=0, concat_axis=0, tiled=False)]
    ppermute x0 -> x1, starting transfers between devices: none -> 1.91 us  [shards(): theirs = lax.ppermute(mine, 'col', [(c, c ^ 1) for c in range(columns)])]
  transfers between devices with their start and end apart: 10 -> 11, of which waited for: 4 -> 4; matrix products, arithmetic and copies ran while one was open for 0% -> 0% of each run, Pallas kernels for 22% -> 19%
where the time goes in v4:
time: 120 us; the launch traced here: 119 us
  starting transfers between devices  46.6 us (39%)
  Pallas kernels  27.5 us (23%)
  waiting for transfers between devices  24.5 us (20%)
  blocking collectives  19.4 us (16%)
    ppermute x8, starting transfers between devices, shift(): lax.ppermute(x, 'clu', [((i + d) % clusters, i) for i in range(clusters)])  36.4 us
    all_to_all x1, blocking collectives, shards(): lax.all_to_all(spread, 'col', split_axis=0, concat_axis=0, axis_index_gro...  19.4 us
    ppermute x8, waiting for transfers between devices, shift(): lax.ppermute(x, 'clu', [((i + d) % clusters, i) for i in range(clusters)])  19 us
    pallas_call x1, Pallas kernels, shards(): pl.pallas_call(factor_kernel, out_shape=(shape((size, RANK), BF16), shape...  14.2 us
    all_to_all x1, waiting for transfers between devices, shards(): lax.all_to_all(side, 'col', split_axis=0, concat_axis=0, tiled=False)  5.46 us
    all_to_all x1, starting transfers between devices, shards(): lax.all_to_all(side, 'col', split_axis=0, concat_axis=0, tiled=False)  4.71 us
    all_to_all x1, starting transfers between devices, shards(): lax.all_to_all(ordered, 'col', split_axis=0, concat_axis=0, tiled=False)  3.57 us
    pallas_call x1, Pallas kernels, shards(): pl.pallas_call(project_kernel, out_shape=(shape(projected, BF16),) * 2, i...  2.45 us
  transfers between devices with their start and end apart: 11, of which 4 were waited for; matrix products, arithmetic and copies ran while one was open for 0% of the time, Pallas kernels for 19%

profile of v4, /device:TPU:32, one launch (start us, length us, event | category | flops | bytes accessed | tf_op | source)
XLA Modules:
  0.0 118.9 jit_solution(308664474136709568)
XLA Ops:
  0.6 2.0 %spread.1 = f32[4,128,512]{2,1,0:T(8,128)} custom-call(f32[64,512]{1,0:T(8,128)} %bitcast.19, f32[64,512]{1,0:T(8,128)} %bitcast.12), custom_call_target="tpu_custom_call" | custom-call | tf_op jit(solution)/shard_map/spread/pallas_call | solution.py:294
  2.6 19.4 %all_to_all.15.mine_ref = f32[4,128,512]{2,1,0:T(8,128)S(1)} all-to-all(f32[4,128,512]{2,1,0:T(8,128)} %spread.1), channel_id=1, replica_groups={{0,2,4,6},{1,3,5,7},{8,10,12,14},{9,11,13,15},{16,18,20,22},{17,19,21,2..., dimensions={0} | all-to-all | bytes 2097152 | tf_op jit(solution)/shard_map/all_to_all | solution.py:304
  22.0 1.9 %collective-permute-start = (f32[4,128,512]{2,1,0:T(8,128)S(1)}, f32[4,128,512]{2,1,0:T(8,128)S(1)}, u32[]{:S(2)}, u32[]{:S(2)}) collective-permute-start(f32[4,128,512]{2,1,0:T(8,128)S(1)} %all_to_all.15.mine_ref), channel_id=1, source_target_pairs={{0,1},{1,0},{2,3},{3,2},{4,5},{5,4},{6,7},{7,6},{8,9},{9,8},{10,11... | collective-permute-start | bytes 3145736 | tf_op jit(solution)/shard_map/ppermute | solution.py:307
  23.9 0.9 skeleton.1
  24.8 2.3 %collective-permute-start.3 = (f32[64,256]{1,0:T(8,128)S(1)}, f32[64,256]{1,0:T(8,128)S(1)}, u32[]{:S(2)}, u32[]{:S(2)}) collective-permute-start(f32[64,256]{1,0:T(8,128)S(1)} %skeleton.1), channel_id=1, source_target_pairs={{32,0},{40,8},{48,16},{56,24},{64,32},{72,40},{80,48},{88,56},{96,... | collective-permute-start | bytes 196616 | tf_op jit(solution)/shard_map/ppermute | solution.py:278
  27.2 3.5 %collective-permute-start.2 = (f32[64,256]{1,0:T(8,128)S(1)}, f32[64,256]{1,0:T(8,128)S(1)}, u32[]{:S(2)}, u32[]{:S(2)}) collective-permute-start(f32[64,256]{1,0:T(8,128)S(1)} %skeleton.1), channel_id=1, source_target_pairs={{480,0},{488,8},{496,16},{504,24},{0,32},{8,40},{16,48},{24,56},{3... | collective-permute-start | bytes 196616 | tf_op jit(solution)/shard_map/ppermute | solution.py:278
  30.7 6.4 %collective-permute-start.1 = (f32[64,256]{1,0:T(8,128)S(1)}, f32[64,256]{1,0:T(8,128)S(1)}, u32[]{:S(2)}, u32[]{:S(2)}) collective-permute-start(f32[64,256]{1,0:T(8,128)S(1)} %skeleton.1), channel_id=1, source_target_pairs={{448,0},{456,8},{464,16},{472,24},{480,32},{488,40},{496,48},{504,... | collective-permute-start | bytes 196616 | tf_op jit(solution)/shard_map/ppermute | solution.py:278
  37.1 0.0 collective-permute-done.3
  37.1 3.6 %collective-permute-done.2 = f32[64,256]{1,0:T(8,128)S(1)} collective-permute-done((f32[64,256]{1,0:T(8,128)S(1)}, f32[64,256]{1,0:T(8,128)S(1)}, u32[]{:S(2)}, u32[]{:S(2)}) %collective-permute-start.2) | collective-permute-done | bytes 65568 | tf_op jit(solution)/shard_map/ppermute | solution.py:278
  40.7 5.8 %collective-permute-done.1 = f32[64,256]{1,0:T(8,128)S(1)} collective-permute-done((f32[64,256]{1,0:T(8,128)S(1)}, f32[64,256]{1,0:T(8,128)S(1)}, u32[]{:S(2)}, u32[]{:S(2)}) %collective-permute-start.1) | collective-permute-done | bytes 65568 | tf_op jit(solution)/shard_map/ppermute | solution.py:278
  46.5 3.3 %collective-permute-start.6 = (f32[4,64,256]{2,1,0:T(8,128)S(1)}, f32[4,64,256]{2,1,0:T(8,128)S(1)}, u32[]{:S(2)}, u32[]{:S(2)}) collective-permute-start(f32[4,64,256]{2,1,0:T(8,128)S(1)} %pad_maximum_fusion.near0), channel_id=1, source_target_pairs={{24,0},{32,8},{40,16},{48,24},{56,32},{64,40},{72,48},{80,56},{88,... | collective-permute-start | bytes 786440 | tf_op jit(solution)/shard_map/ppermute | solution.py:278
  49.8 3.6 %collective-permute-start.4 = (f32[4,64,256]{2,1,0:T(8,128)S(1)}, f32[4,64,256]{2,1,0:T(8,128)S(1)}, u32[]{:S(2)}, u32[]{:S(2)}) collective-permute-start(f32[4,64,256]{2,1,0:T(8,128)S(1)} %pad_maximum_fusion.near0), channel_id=1, source_target_pairs={{8,0},{16,8},{24,16},{32,24},{40,32},{48,40},{56,48},{64,56},{72,6... | collective-permute-start | bytes 786440 | tf_op jit(solution)/shard_map/ppermute | solution.py:278
  53.4 5.3 %collective-permute-start.5 = (f32[2,64,256]{2,1,0:T(8,128)S(1)}, f32[2,64,256]{2,1,0:T(8,128)S(1)}, u32[]{:S(2)}, u32[]{:S(2)}) collective-permute-start(f32[2,64,256]{2,1,0:T(8,128)S(1)} %pad_maximum_fusion.1), channel_id=1, source_target_pairs={{16,0},{24,8},{32,16},{40,24},{48,32},{56,40},{64,48},{72,56},{80,... | collective-permute-start | bytes 393224 | tf_op jit(solution)/shard_map/ppermute | solution.py:278
  58.8 0.0 collective-permute-done.6.near3
  58.8 3.0 %collective-permute-start.7 = (f32[2,64,256]{2,1,0:T(8,128)S(1)}, f32[2,64,256]{2,1,0:T(8,128)S(1)}, u32[]{:S(2)}, u32[]{:S(2)}) collective-permute-start(f32[2,64,256]{2,1,0:T(8,128)S(1)} %slice.4), channel_id=1, source_target_pairs={{24,0},{32,8},{40,16},{48,24},{56,32},{64,40},{72,48},{80,56},{88,... | collective-permute-start | bytes 393224 | tf_op jit(solution)/shard_map/ppermute | solution.py:278
  61.8 8.9 %collective-permute-start.8 = (f32[64,256]{1,0:T(8,128)S(1)}, f32[64,256]{1,0:T(8,128)S(1)}, u32[]{:S(2)}, u32[]{:S(2)}) collective-permute-start(f32[64,256]{1,0:T(8,128)S(1)} %skeleton.1), channel_id=1, source_target_pairs={{256,0},{264,8},{272,16},{280,24},{288,32},{296,40},{304,48},{312,... | collective-permute-start | bytes 196616 | tf_op jit(solution)/shard_map/ppermute | solution.py:278
  70.7 1.5 %facts.1.facts_ref = s32[64]{0:T(128)} custom-call(s32[16,64]{1,0:T(8,128)} %bitcast.22, s32[1,16]{1,0:T(1,128)} %mask_ref.1, s32[64]{0:T(128)} %parent_ref.1), custom_call_target="tpu_custom_call" | custom-call | tf_op jit(solution)/shard_map/facts/pallas_call | solution.py:313
  72.3 9.6 %collective-permute-done.8.far = f32[64,256]{1,0:T(8,128)S(1)} collective-permute-done((f32[64,256]{1,0:T(8,128)S(1)}, f32[64,256]{1,0:T(8,128)S(1)}, u32[]{:S(2)}, u32[]{:S(2)}) %collective-permute-start.8) | collective-permute-done | bytes 65568 | tf_op jit(solution)/shard_map/ppermute | solution.py:278
  81.9 0.0 collective-permute-done.5.near2
  81.9 0.0 collective-permute-done.4.near1
  81.9 0.0 collective-permute-done.7.relay3
  81.9 1.8 %order.1 = f32[8,2,64,256]{3,2,1,0:T(8,128)} custom-call(s32[64]{0:T(128)} %facts.1.facts_ref, f32[4,64,256]{2,1,0:T(8,128)S(1)} %pad_maximum_fusion.near0, f32[4,64,256]{2,1,0:T(8,128)S(1)} %collective-permute-done.4.near1, f32[2,64,256]{2,1,0:T(8,128)S(1)} %collective-permute-done.5.near2, f32[2,64,256]{2,1,0:T(8,128)S(1)} %collective-permute-done.7.relay3, ...), custom_call_target="tpu_custom_call" | custom-call | tf_op jit(solution)/shard_map/order/pallas_call | solution.py:321
  83.7 3.6 %all-to-all-start.1 = ((f32[8,2,64,256]{3,2,1,0:T(8,128)}), f32[8,2,64,256]{3,2,1,0:T(8,128)S(1)}, u32[]{:S(2)}, u32[]{:S(2)}) async-start(f32[8,2,64,256]{3,2,1,0:T(8,128)} %order.1), calls=%async_computation.1 | async-start | bytes 2097152 | tf_op jit(solution)/shard_map/all_to_all | solution.py:330
  87.3 0.0 collective-permute-done.theirs_ref
  87.3 14.2 %factor.1 = (bf16[512,256]{1,0:T(8,128)(2,1)S(1)}, bf16[512,256]{1,0:T(8,128)(2,1)S(1)}, f32[32,256]{1,0:T(8,128)S(1)}, f32[32,256]{1,0:T(8,128)}) custom-call(f32[4,128,512]{2,1,0:T(8,128)S(1)} %all_to_all.15.mine_ref, f32[4,128,512]{2,1,0:T(8,128)S(1)} %collective-permute-done.theirs_ref), custom_call_target="tpu_custom_call" | custom-call | flops 6000000000 | bytes 4000000 | tf_op jit(solution)/shard_map/factor/pallas_call | solution.py:332
  101.5 2.4 %project.1 = (bf16[2,256,512]{2,1,0:T(8,128)(2,1)S(1)}, bf16[2,256,512]{2,1,0:T(8,128)(2,1)S(1)}) custom-call(f32[2,512,512]{2,1,0:T(8,128)} %bitcast.23, bf16[512,256]{1,0:T(8,128)(2,1)S(1)} %get-tuple-element.9.high_ref, bf16[512,256]{1,0:T(8,128)(2,1)S(1)} %get-tuple-element.10.low_ref), custom_call_target="tpu_custom_call" | custom-call | flops 1000000000 | bytes 4000000 | tf_op jit(solution)/shard_map/project/pallas_call | solution.py:350
  104.0 0.0 all-to-all-done.1.routed_ref
  104.0 1.4 %side.1 = f32[8,32,256]{2,1,0:T(8,128)} custom-call(s32[64]{0:T(128)} %facts.1.facts_ref, bf16[2,256,512]{2,1,0:T(8,128)(2,1)S(1)} %get-tuple-element.11.high_ref, bf16[2,256,512]{2,1,0:T(8,128)(2,1)S(1)} %get-tuple-element.12.low_ref, f32[8,2,64,256]{3,2,1,0:T(8,128)S(1)} %all-to-all-done.1.routed_ref), custom_call_target="tpu_custom_call" | custom-call | flops 200000000 | bytes 2000000 | tf_op jit(solution)/shard_map/side/pallas_call | solution.py:363
  105.4 4.7 %all-to-all-start.2 = ((f32[8,32,256]{2,1,0:T(8,128)}), f32[8,32,256]{2,1,0:T(8,128)S(1)}, u32[]{:S(2)}, u32[]{:S(2)}) async-start(f32[8,32,256]{2,1,0:T(8,128)} %side.1), calls=%async_computation.2 | async-start | bytes 524288 | tf_op jit(solution)/shard_map/all_to_all | solution.py:372
  110.1 2.0 %couple.1 = f32[2,256,256]{2,1,0:T(8,128)} custom-call(s32[64]{0:T(128)} %facts.1.facts_ref, bf16[2,256,512]{2,1,0:T(8,128)(2,1)S(1)} %get-tuple-element.11.high_ref, bf16[2,256,512]{2,1,0:T(8,128)(2,1)S(1)} %get-tuple-element.12.low_ref, f32[8,2,64,256]{3,2,1,0:T(8,128)S(1)} %all-to-all-done.1.routed_ref), custom_call_target="tpu_custom_call" | custom-call | flops 400000000 | bytes 4000000 | tf_op jit(solution)/shard_map/couple/pallas_call | solution.py:373
  112.1 5.5 %all-to-all-done.2.parts_ref = f32[8,32,256]{2,1,0:T(8,128)S(1)} async-done(((f32[8,32,256]{2,1,0:T(8,128)}), f32[8,32,256]{2,1,0:T(8,128)S(1)}, u32[]{:S(2)}, u32[]{:S(2)}) %all-to-all-start.2) | async-done | bytes 262176 | tf_op jit(solution)/shard_map/all_to_all | solution.py:372
  117.6 1.3 %merge.1 = f32[32,512]{1,0:T(8,128)} custom-call(s32[64]{0:T(128)} %facts.1.facts_ref, f32[8,32,256]{2,1,0:T(8,128)S(1)} %all-to-all-done.2.parts_ref, f32[32,256]{1,0:T(8,128)S(1)} %get-tuple-element.13.schur_ref), custom_call_target="tpu_custom_call" | custom-call | tf_op jit(solution)/shard_map/merge/pallas_call | solution.py:382
  (3 shorter events, 0.0 us)
Async XLA Ops:
  22.0 65.3 %collective-permute-start = (f32[4,128,512]{2,1,0:T(8,128)S(1)}, f32[4,128,512]{2,1,0:T(8,128)S(1)}, u32[]{:S(2)}, u32[]{:S(2)}) collective-permute-start(f32[4,128,512]{2,1,0:T(8,128)S(1)} %all_to_all.15.mine_ref), channel_id=1, source_target_pairs={{0,1},{1,0},{2,3},{3,2},{4,5},{5,4},{6,7},{7,6},{8,9},{9,8},{10,11... | collective-permute-start | bytes 3145736 | tf_op jit(solution)/shard_map/ppermute | solution.py:307
  24.8 12.3 %collective-permute-start.3 = (f32[64,256]{1,0:T(8,128)S(1)}, f32[64,256]{1,0:T(8,128)S(1)}, u32[]{:S(2)}, u32[]{:S(2)}) collective-permute-start(f32[64,256]{1,0:T(8,128)S(1)} %skeleton.1), channel_id=1, source_target_pairs={{32,0},{40,8},{48,16},{56,24},{64,32},{72,40},{80,48},{88,56},{96,... | collective-permute-start | bytes 196616 | tf_op jit(solution)/shard_map/ppermute | solution.py:278
  27.2 13.5 %collective-permute-start.2 = (f32[64,256]{1,0:T(8,128)S(1)}, f32[64,256]{1,0:T(8,128)S(1)}, u32[]{:S(2)}, u32[]{:S(2)}) collective-permute-start(f32[64,256]{1,0:T(8,128)S(1)} %skeleton.1), channel_id=1, source_target_pairs={{480,0},{488,8},{496,16},{504,24},{0,32},{8,40},{16,48},{24,56},{3... | collective-permute-start | bytes 196616 | tf_op jit(solution)/shard_map/ppermute | solution.py:278
  30.7 15.8 %collective-permute-start.1 = (f32[64,256]{1,0:T(8,128)S(1)}, f32[64,256]{1,0:T(8,128)S(1)}, u32[]{:S(2)}, u32[]{:S(2)}) collective-permute-start(f32[64,256]{1,0:T(8,128)S(1)} %skeleton.1), channel_id=1, source_target_pairs={{448,0},{456,8},{464,16},{472,24},{480,32},{488,40},{496,48},{504,... | collective-permute-start | bytes 196616 | tf_op jit(solution)/shard_map/ppermute | solution.py:278
  46.5 12.3 %collective-permute-start.6 = (f32[4,64,256]{2,1,0:T(8,128)S(1)}, f32[4,64,256]{2,1,0:T(8,128)S(1)}, u32[]{:S(2)}, u32[]{:S(2)}) collective-permute-start(f32[4,64,256]{2,1,0:T(8,128)S(1)} %pad_maximum_fusion.near0), channel_id=1, source_target_pairs={{24,0},{32,8},{40,16},{48,24},{56,32},{64,40},{72,48},{80,56},{88,... | collective-permute-start | bytes 786440 | tf_op jit(solution)/shard_map/ppermute | solution.py:278
  49.8 32.1 %collective-permute-start.4 = (f32[4,64,256]{2,1,0:T(8,128)S(1)}, f32[4,64,256]{2,1,0:T(8,128)S(1)}, u32[]{:S(2)}, u32[]{:S(2)}) collective-permute-start(f32[4,64,256]{2,1,0:T(8,128)S(1)} %pad_maximum_fusion.near0), channel_id=1, source_target_pairs={{8,0},{16,8},{24,16},{32,24},{40,32},{48,40},{56,48},{64,56},{72,6... | collective-permute-start | bytes 786440 | tf_op jit(solution)/shard_map/ppermute | solution.py:278
  53.4 28.5 %collective-permute-start.5 = (f32[2,64,256]{2,1,0:T(8,128)S(1)}, f32[2,64,256]{2,1,0:T(8,128)S(1)}, u32[]{:S(2)}, u32[]{:S(2)}) collective-permute-start(f32[2,64,256]{2,1,0:T(8,128)S(1)} %pad_maximum_fusion.1), channel_id=1, source_target_pairs={{16,0},{24,8},{32,16},{40,24},{48,32},{56,40},{64,48},{72,56},{80,... | collective-permute-start | bytes 393224 | tf_op jit(solution)/shard_map/ppermute | solution.py:278
  58.8 23.1 %collective-permute-start.7 = (f32[2,64,256]{2,1,0:T(8,128)S(1)}, f32[2,64,256]{2,1,0:T(8,128)S(1)}, u32[]{:S(2)}, u32[]{:S(2)}) collective-permute-start(f32[2,64,256]{2,1,0:T(8,128)S(1)} %slice.4), channel_id=1, source_target_pairs={{24,0},{32,8},{40,16},{48,24},{56,32},{64,40},{72,48},{80,56},{88,... | collective-permute-start | bytes 393224 | tf_op jit(solution)/shard_map/ppermute | solution.py:278
  61.8 20.1 %collective-permute-start.8 = (f32[64,256]{1,0:T(8,128)S(1)}, f32[64,256]{1,0:T(8,128)S(1)}, u32[]{:S(2)}, u32[]{:S(2)}) collective-permute-start(f32[64,256]{1,0:T(8,128)S(1)} %skeleton.1), channel_id=1, source_target_pairs={{256,0},{264,8},{272,16},{280,24},{288,32},{296,40},{304,48},{312,... | collective-permute-start | bytes 196616 | tf_op jit(solution)/shard_map/ppermute | solution.py:278
  83.7 20.2 %all-to-all-start.1 = ((f32[8,2,64,256]{3,2,1,0:T(8,128)}), f32[8,2,64,256]{3,2,1,0:T(8,128)S(1)}, u32[]{:S(2)}, u32[]{:S(2)}) async-start(f32[8,2,64,256]{3,2,1,0:T(8,128)} %order.1), calls=%async_computation.1 | async-start | bytes 2097152 | tf_op jit(solution)/shard_map/all_to_all | solution.py:330
  105.4 12.2 %all-to-all-start.2 = ((f32[8,32,256]{2,1,0:T(8,128)}), f32[8,32,256]{2,1,0:T(8,128)S(1)}, u32[]{:S(2)}, u32[]{:S(2)}) async-start(f32[8,32,256]{2,1,0:T(8,128)} %side.1), calls=%async_computation.2 | async-start | bytes 524288 | tf_op jit(solution)/shard_map/all_to_all | solution.py:372

commit v5 on v4

--- a/solution.py
+++ b/solution.py
@@ -159,15 +159,34 @@
         facts_ref[LIVE + 2 * k + 1] = jnp.where(index_ref[slot, own] == sibling, live, 0)
 
 
-def order_kernel(facts_ref, near0, near1, near2, relay3, near3, far, out_ref, sem):
-    stacks = (near0, near1, near2, near3)
+RING = 4
+
+
+def fan_kernel(down8, down4, own, up4, up8, out1, out2, out3, sem):
+    place = lax.axis_index("clu") % RING
+    pieces = (down8, down4, own, up4, up8)
+    outs = (out1, out2, out3)
+    for r, out in enumerate(outs, 1):
+        for wraps in (0, 1):
+
+            @pl.when((place < r) if wraps else (place >= r))
+            def _():
+                for q in range(RING):
+                    pltpu.make_async_copy(pieces[q + wraps], out.at[q], sem.at[r - 1, q]).start()
+
+    for r, out in enumerate(outs, 1):
+        for q in range(RING):
+            pltpu.make_async_copy(pieces[q], out.at[q], sem.at[r - 1, q]).wait()
+
+
+def order_kernel(facts_ref, down8, down4, up4, near1, near2, near3, far, out_ref, sem):
+    own = (down8, down4, None, up4)
+    stacks = (None, near1, near2, near3)
     copies = []
     for d in range(16):
         slot = facts_ref[d]
-        if d == 8:
-            source = far
-        elif d % 4 == 2 and d // 4 >= 2:
-            source = relay3.at[d // 4 - 2]
+        if d % 4 == 0:
+            source = far if d == 8 else own[d // 4]
         else:
             source = stacks[d % 4].at[d // 4]
         copies.append(pltpu.make_async_copy(source, out_ref.at[slot // 2, slot % 2], sem.at[d]))
@@ -277,6 +296,10 @@
     def shift(x, d):
         return lax.ppermute(x, "clu", [((i + d) % clusters, i) for i in range(clusters)])
 
+    def shift_ring(x, r):
+        pairs = [(i - i % RING + (i + r) % RING, i) for i in range(clusters)]
+        return lax.ppermute(x, "clu", pairs)
+
     skeleton = pl.pallas_call(
         slice_kernel,
         out_shape=shape((rows, RANK), F32),
@@ -288,6 +311,7 @@
     )(keep_out(bases[0]))
     far = shift(skeleton, clusters // 2)
     down8 = shift(skeleton, -8)
+    up8 = shift(skeleton, 8)
     down4 = shift(skeleton, -4)
     up4 = shift(skeleton, 4)
     chips = columns // 2
@@ -305,11 +329,18 @@
         spread, "col", split_axis=0, concat_axis=0, axis_index_groups=same_core, tiled=False
     )
     theirs = lax.ppermute(mine, "col", [(c, c ^ 1) for c in range(columns)])
-    near0 = jnp.stack([down8, down4, skeleton, up4])
-    near2 = shift(jnp.stack([down8, down4]), 2)
-    near1 = shift(near0, 1)
-    near3 = shift(near0, 3)
-    relay3 = shift(near3[1:3], 3)
+    fan = pl.pallas_call(
+        fan_kernel,
+        out_shape=(shape((RING, rows, RANK), F32),) * 3,
+        in_specs=[ANY] * 5,
+        out_specs=(ANY,) * 3,
+        scratch_shapes=[pltpu.SemaphoreType.DMA((3, RING))],
+        compiler_params=params(2),
+        name="fan",
+    )(down8, down4, skeleton, up4, up8)
+    near2 = shift_ring(fan[1], 2)
+    near1 = shift_ring(fan[0], 1)
+    near3 = shift_ring(fan[2], 3)
     facts = pl.pallas_call(
         facts_kernel,
         out_shape=shape((64,), jnp.int32),
@@ -321,12 +352,12 @@
     ordered = pl.pallas_call(
         order_kernel,
         out_shape=pltpu.HBM((columns, per_device, rows, RANK), F32),
-        in_specs=[SMEM] + [ANY] * 6,
+        in_specs=[SMEM] + [ANY] * 7,
         out_specs=HBM,
         compiler_params=params(2),
         scratch_shapes=[pltpu.SemaphoreType.DMA((near_index.shape[1],))],
         name="order",
-    )(facts, near0, near1, near2, relay3, near3, far)
+    )(facts, down8, down4, up4, near1, near2, near3, far)
     routed = lax.all_to_all(ordered, "col", split_axis=0, concat_axis=0, tiled=False)
     count = RANK // columns
     high, low, schur, factor = pl.pallas_call(

time: 120 us -> 113 us (0.942)
  the two profiles are of different devices: /device:TPU:32 before, /device:TPU:24 now
where the time goes in v5:
time: 113 us; the launch traced here: 111 us
  starting transfers between devices  50.2 us (44%)
  Pallas kernels  28.4 us (25%)
  blocking collectives  19.4 us (17%)
  waiting for transfers between devices  12.3 us (11%)
    ppermute x5, starting transfers between devices, shift(): lax.ppermute(x, 'clu', [((i + d) % clusters, i) for i in range(clusters)])  30.4 us
    all_to_all x1, blocking collectives, shards(): lax.all_to_all(spread, 'col', split_axis=0, concat_axis=0, axis_index_gro...  19.4 us
    pallas_call x1, Pallas kernels, shards(): pl.pallas_call(factor_kernel, out_shape=(shape((size, RANK), BF16), shape...  14.2 us
    ppermute x3, starting transfers between devices, shift_ring(): return lax.ppermute(x, 'clu', pairs)  9.59 us
    ppermute x5, waiting for transfers between devices, shift(): lax.ppermute(x, 'clu', [((i + d) % clusters, i) for i in range(clusters)])  6.87 us
    all_to_all x1, waiting for transfers between devices, shards(): lax.all_to_all(side, 'col', split_axis=0, concat_axis=0, tiled=False)  5.46 us
    all_to_all x1, starting transfers between devices, shards(): lax.all_to_all(side, 'col', split_axis=0, concat_axis=0, tiled=False)  4.81 us
    all_to_all x1, starting transfers between devices, shards(): lax.all_to_all(ordered, 'col', split_axis=0, concat_axis=0, tiled=False)  3.57 us
  transfers between devices with their start and end apart: 11, of which 3 were waited for; matrix products, arithmetic and copies ran while one was open for 0% of the time, Pallas kernels for 21%

profile of v5, /device:TPU:24, one launch (start us, length us, event | category | flops | bytes accessed | tf_op | source)
XLA Modules:
  0.0 111.2 jit_solution(3184407423805399571)
XLA Ops:
  0.6 2.0 %spread.1 = f32[4,128,512]{2,1,0:T(8,128)} custom-call(f32[64,512]{1,0:T(8,128)} %bitcast.10, f32[64,512]{1,0:T(8,128)} %bitcast.7), custom_call_target="tpu_custom_call" | custom-call | tf_op jit(solution)/shard_map/spread/pallas_call | solution.py:318
  2.6 19.4 %all_to_all.15.mine_ref = f32[4,128,512]{2,1,0:T(8,128)S(1)} all-to-all(f32[4,128,512]{2,1,0:T(8,128)} %spread.1), channel_id=1, replica_groups={{0,2,4,6},{1,3,5,7},{8,10,12,14},{9,11,13,15},{16,18,20,22},{17,19,21,2..., dimensions={0} | all-to-all | bytes 2097152 | tf_op jit(solution)/shard_map/all_to_all | solution.py:328
  22.0 1.9 %collective-permute-start = (f32[4,128,512]{2,1,0:T(8,128)S(1)}, f32[4,128,512]{2,1,0:T(8,128)S(1)}, u32[]{:S(2)}, u32[]{:S(2)}) collective-permute-start(f32[4,128,512]{2,1,0:T(8,128)S(1)} %all_to_all.15.mine_ref), channel_id=1, source_target_pairs={{0,1},{1,0},{2,3},{3,2},{4,5},{5,4},{6,7},{7,6},{8,9},{9,8},{10,11... | collective-permute-start | bytes 3145736 | tf_op jit(solution)/shard_map/ppermute | solution.py:331
  23.9 0.9 skeleton.1.own
  24.8 5.2 %collective-permute-start.1 = (f32[64,256]{1,0:T(8,128)S(1)}, f32[64,256]{1,0:T(8,128)S(1)}, u32[]{:S(2)}, u32[]{:S(2)}) collective-permute-start(f32[64,256]{1,0:T(8,128)S(1)} %skeleton.1.own), channel_id=1, source_target_pairs={{448,0},{456,8},{464,16},{472,24},{480,32},{488,40},{496,48},{504,... | collective-permute-start | bytes 196616 | tf_op jit(solution)/shard_map/ppermute | solution.py:297
  30.0 3.8 %collective-permute-start.2 = (f32[64,256]{1,0:T(8,128)S(1)}, f32[64,256]{1,0:T(8,128)S(1)}, u32[]{:S(2)}, u32[]{:S(2)}) collective-permute-start(f32[64,256]{1,0:T(8,128)S(1)} %skeleton.1.own), channel_id=1, source_target_pairs={{480,0},{488,8},{496,16},{504,24},{0,32},{8,40},{16,48},{24,56},{3... | collective-permute-start | bytes 196616 | tf_op jit(solution)/shard_map/ppermute | solution.py:297
  33.8 6.2 %collective-permute-start.3 = (f32[64,256]{1,0:T(8,128)S(1)}, f32[64,256]{1,0:T(8,128)S(1)}, u32[]{:S(2)}, u32[]{:S(2)}) collective-permute-start(f32[64,256]{1,0:T(8,128)S(1)} %skeleton.1.own), channel_id=1, source_target_pairs={{32,0},{40,8},{48,16},{56,24},{64,32},{72,40},{80,48},{88,56},{96,... | collective-permute-start | bytes 196616 | tf_op jit(solution)/shard_map/ppermute | solution.py:297
  40.1 4.8 %collective-permute-start.4 = (f32[64,256]{1,0:T(8,128)S(1)}, f32[64,256]{1,0:T(8,128)S(1)}, u32[]{:S(2)}, u32[]{:S(2)}) collective-permute-start(f32[64,256]{1,0:T(8,128)S(1)} %skeleton.1.own), channel_id=1, source_target_pairs={{64,0},{72,8},{80,16},{88,24},{96,32},{104,40},{112,48},{120,56},{... | collective-permute-start | bytes 196616 | tf_op jit(solution)/shard_map/ppermute | solution.py:297
  44.9 0.0 collective-permute-done.1.down8
  44.9 0.0 collective-permute-done.2.down4
  44.9 0.0 collective-permute-done.3.up4
  44.9 3.1 %collective-permute-done.4.up8 = f32[64,256]{1,0:T(8,128)S(1)} collective-permute-done((f32[64,256]{1,0:T(8,128)S(1)}, f32[64,256]{1,0:T(8,128)S(1)}, u32[]{:S(2)}, u32[]{:S(2)}) %collective-permute-start.4) | collective-permute-done | bytes 65568 | tf_op jit(solution)/shard_map/ppermute | solution.py:297
  48.0 1.0 fan.1
  49.0 2.7 %collective-permute-start.5 = (f32[4,64,256]{2,1,0:T(8,128)}, f32[4,64,256]{2,1,0:T(8,128)S(1)}, u32[]{:S(2)}, u32[]{:S(2)}) collective-permute-start(f32[4,64,256]{2,1,0:T(8,128)} %get-tuple-element.16), channel_id=1, source_target_pairs={{8,0},{16,8},{24,16},{0,24},{40,32},{48,40},{56,48},{32,56},{72,64... | collective-permute-start | bytes 786440 | tf_op jit(solution)/shard_map/ppermute | solution.py:301
  51.6 2.8 %collective-permute-start.6 = (f32[4,64,256]{2,1,0:T(8,128)}, f32[4,64,256]{2,1,0:T(8,128)S(1)}, u32[]{:S(2)}, u32[]{:S(2)}) collective-permute-start(f32[4,64,256]{2,1,0:T(8,128)} %get-tuple-element.17), channel_id=1, source_target_pairs={{16,0},{24,8},{0,16},{8,24},{48,32},{56,40},{32,48},{40,56},{80,64... | collective-permute-start | bytes 786440 | tf_op jit(solution)/shard_map/ppermute | solution.py:301
  54.5 4.1 %collective-permute-start.7 = (f32[4,64,256]{2,1,0:T(8,128)}, f32[4,64,256]{2,1,0:T(8,128)S(1)}, u32[]{:S(2)}, u32[]{:S(2)}) collective-permute-start(f32[4,64,256]{2,1,0:T(8,128)} %get-tuple-element.18), channel_id=1, source_target_pairs={{24,0},{0,8},{8,16},{16,24},{56,32},{32,40},{40,48},{48,56},{88,64... | collective-permute-start | bytes 786440 | tf_op jit(solution)/shard_map/ppermute | solution.py:301
  58.6 10.3 %collective-permute-start.8 = (f32[64,256]{1,0:T(8,128)S(1)}, f32[64,256]{1,0:T(8,128)S(1)}, u32[]{:S(2)}, u32[]{:S(2)}) collective-permute-start(f32[64,256]{1,0:T(8,128)S(1)} %skeleton.1.own), channel_id=1, source_target_pairs={{256,0},{264,8},{272,16},{280,24},{288,32},{296,40},{304,48},{312,... | collective-permute-start | bytes 196616 | tf_op jit(solution)/shard_map/ppermute | solution.py:297
  68.9 1.5 %facts.1.facts_ref = s32[64]{0:T(128)} custom-call(s32[16,64]{1,0:T(8,128)} %bitcast.12, s32[1,16]{1,0:T(1,128)} %mask_ref.1, s32[64]{0:T(128)} %parent_ref.1), custom_call_target="tpu_custom_call" | custom-call | tf_op jit(solution)/shard_map/facts/pallas_call | solution.py:344
  70.4 3.8 %collective-permute-done.8.far = f32[64,256]{1,0:T(8,128)S(1)} collective-permute-done((f32[64,256]{1,0:T(8,128)S(1)}, f32[64,256]{1,0:T(8,128)S(1)}, u32[]{:S(2)}, u32[]{:S(2)}) %collective-permute-start.8) | collective-permute-done | bytes 65568 | tf_op jit(solution)/shard_map/ppermute | solution.py:297
  74.2 0.0 collective-permute-done.5.near1
  74.2 0.0 collective-permute-done.6.near2
  74.2 0.0 collective-permute-done.7.near3
  74.2 1.8 %order.1 = f32[8,2,64,256]{3,2,1,0:T(8,128)} custom-call(s32[64]{0:T(128)} %facts.1.facts_ref, f32[64,256]{1,0:T(8,128)S(1)} %collective-permute-done.1.down8, f32[64,256]{1,0:T(8,128)S(1)} %collective-permute-done.2.down4, f32[64,256]{1,0:T(8,128)S(1)} %collective-permute-done.3.up4, f32[4,64,256]{2,1,0:T(8,128)S(1)} %collective-permute-done.5.near1, ...), custom_call_target="tpu_custom_call" | custom-call | tf_op jit(solution)/shard_map/order/pallas_call | solution.py:352
  76.0 3.6 %all-to-all-start.1 = ((f32[8,2,64,256]{3,2,1,0:T(8,128)}), f32[8,2,64,256]{3,2,1,0:T(8,128)S(1)}, u32[]{:S(2)}, u32[]{:S(2)}) async-start(f32[8,2,64,256]{3,2,1,0:T(8,128)} %order.1), calls=%async_computation.1 | async-start | bytes 2097152 | tf_op jit(solution)/shard_map/all_to_all | solution.py:361
  79.5 0.0 collective-permute-done.theirs_ref
  79.6 14.2 %factor.1 = (bf16[512,256]{1,0:T(8,128)(2,1)S(1)}, bf16[512,256]{1,0:T(8,128)(2,1)S(1)}, f32[32,256]{1,0:T(8,128)S(1)}, f32[32,256]{1,0:T(8,128)}) custom-call(f32[4,128,512]{2,1,0:T(8,128)S(1)} %all_to_all.15.mine_ref, f32[4,128,512]{2,1,0:T(8,128)S(1)} %collective-permute-done.theirs_ref), custom_call_target="tpu_custom_call" | custom-call | flops 6000000000 | bytes 4000000 | tf_op jit(solution)/shard_map/factor/pallas_call | solution.py:363
  93.7 2.4 %project.1 = (bf16[2,256,512]{2,1,0:T(8,128)(2,1)S(1)}, bf16[2,256,512]{2,1,0:T(8,128)(2,1)S(1)}) custom-call(f32[2,512,512]{2,1,0:T(8,128)} %bitcast.13, bf16[512,256]{1,0:T(8,128)(2,1)S(1)} %get-tuple-element.12.high_ref, bf16[512,256]{1,0:T(8,128)(2,1)S(1)} %get-tuple-element.13.low_ref), custom_call_target="tpu_custom_call" | custom-call | flops 1000000000 | bytes 4000000 | tf_op jit(solution)/shard_map/project/pallas_call | solution.py:381
  96.2 0.0 all-to-all-done.1.routed_ref
  96.2 1.4 %side.1 = f32[8,32,256]{2,1,0:T(8,128)} custom-call(s32[64]{0:T(128)} %facts.1.facts_ref, bf16[2,256,512]{2,1,0:T(8,128)(2,1)S(1)} %get-tuple-element.14.high_ref, bf16[2,256,512]{2,1,0:T(8,128)(2,1)S(1)} %get-tuple-element.15.low_ref, f32[8,2,64,256]{3,2,1,0:T(8,128)S(1)} %all-to-all-done.1.routed_ref), custom_call_target="tpu_custom_call" | custom-call | flops 200000000 | bytes 2000000 | tf_op jit(solution)/shard_map/side/pallas_call | solution.py:394
  97.6 4.8 %all-to-all-start.2 = ((f32[8,32,256]{2,1,0:T(8,128)}), f32[8,32,256]{2,1,0:T(8,128)S(1)}, u32[]{:S(2)}, u32[]{:S(2)}) async-start(f32[8,32,256]{2,1,0:T(8,128)} %side.1), calls=%async_computation.2 | async-start | bytes 524288 | tf_op jit(solution)/shard_map/all_to_all | solution.py:403
  102.4 2.0 %couple.1 = f32[2,256,256]{2,1,0:T(8,128)} custom-call(s32[64]{0:T(128)} %facts.1.facts_ref, bf16[2,256,512]{2,1,0:T(8,128)(2,1)S(1)} %get-tuple-element.14.high_ref, bf16[2,256,512]{2,1,0:T(8,128)(2,1)S(1)} %get-tuple-element.15.low_ref, f32[8,2,64,256]{3,2,1,0:T(8,128)S(1)} %all-to-all-done.1.routed_ref), custom_call_target="tpu_custom_call" | custom-call | flops 400000000 | bytes 4000000 | tf_op jit(solution)/shard_map/couple/pallas_call | solution.py:404
  104.5 5.5 %all-to-all-done.2.parts_ref = f32[8,32,256]{2,1,0:T(8,128)S(1)} async-done(((f32[8,32,256]{2,1,0:T(8,128)}), f32[8,32,256]{2,1,0:T(8,128)S(1)}, u32[]{:S(2)}, u32[]{:S(2)}) %all-to-all-start.2) | async-done | bytes 262176 | tf_op jit(solution)/shard_map/all_to_all | solution.py:403
  109.9 1.3 %merge.1 = f32[32,512]{1,0:T(8,128)} custom-call(s32[64]{0:T(128)} %facts.1.facts_ref, f32[8,32,256]{2,1,0:T(8,128)S(1)} %all-to-all-done.2.parts_ref, f32[32,256]{1,0:T(8,128)S(1)} %get-tuple-element.19.schur_ref), custom_call_target="tpu_custom_call" | custom-call | tf_op jit(solution)/shard_map/merge/pallas_call | solution.py:413
Async XLA Ops:
  22.0 57.5 %collective-permute-start = (f32[4,128,512]{2,1,0:T(8,128)S(1)}, f32[4,128,512]{2,1,0:T(8,128)S(1)}, u32[]{:S(2)}, u32[]{:S(2)}) collective-permute-start(f32[4,128,512]{2,1,0:T(8,128)S(1)} %all_to_all.15.mine_ref), channel_id=1, source_target_pairs={{0,1},{1,0},{2,3},{3,2},{4,5},{5,4},{6,7},{7,6},{8,9},{9,8},{10,11... | collective-permute-start | bytes 3145736 | tf_op jit(solution)/shard_map/ppermute | solution.py:331
  24.8 20.1 %collective-permute-start.1 = (f32[64,256]{1,0:T(8,128)S(1)}, f32[64,256]{1,0:T(8,128)S(1)}, u32[]{:S(2)}, u32[]{:S(2)}) collective-permute-start(f32[64,256]{1,0:T(8,128)S(1)} %skeleton.1.own), channel_id=1, source_target_pairs={{448,0},{456,8},{464,16},{472,24},{480,32},{488,40},{496,48},{504,... | collective-permute-start | bytes 196616 | tf_op jit(solution)/shard_map/ppermute | solution.py:297
  30.0 14.9 %collective-permute-start.2 = (f32[64,256]{1,0:T(8,128)S(1)}, f32[64,256]{1,0:T(8,128)S(1)}, u32[]{:S(2)}, u32[]{:S(2)}) collective-permute-start(f32[64,256]{1,0:T(8,128)S(1)} %skeleton.1.own), channel_id=1, source_target_pairs={{480,0},{488,8},{496,16},{504,24},{0,32},{8,40},{16,48},{24,56},{3... | collective-permute-start | bytes 196616 | tf_op jit(solution)/shard_map/ppermute | solution.py:297
  33.8 11.1 %collective-permute-start.3 = (f32[64,256]{1,0:T(8,128)S(1)}, f32[64,256]{1,0:T(8,128)S(1)}, u32[]{:S(2)}, u32[]{:S(2)}) collective-permute-start(f32[64,256]{1,0:T(8,128)S(1)} %skeleton.1.own), channel_id=1, source_target_pairs={{32,0},{40,8},{48,16},{56,24},{64,32},{72,40},{80,48},{88,56},{96,... | collective-permute-start | bytes 196616 | tf_op jit(solution)/shard_map/ppermute | solution.py:297
  40.1 7.9 %collective-permute-start.4 = (f32[64,256]{1,0:T(8,128)S(1)}, f32[64,256]{1,0:T(8,128)S(1)}, u32[]{:S(2)}, u32[]{:S(2)}) collective-permute-start(f32[64,256]{1,0:T(8,128)S(1)} %skeleton.1.own), channel_id=1, source_target_pairs={{64,0},{72,8},{80,16},{88,24},{96,32},{104,40},{112,48},{120,56},{... | collective-permute-start | bytes 196616 | tf_op jit(solution)/shard_map/ppermute | solution.py:297
  49.0 25.2 %collective-permute-start.5 = (f32[4,64,256]{2,1,0:T(8,128)}, f32[4,64,256]{2,1,0:T(8,128)S(1)}, u32[]{:S(2)}, u32[]{:S(2)}) collective-permute-start(f32[4,64,256]{2,1,0:T(8,128)} %get-tuple-element.16), channel_id=1, source_target_pairs={{8,0},{16,8},{24,16},{0,24},{40,32},{48,40},{56,48},{32,56},{72,64... | collective-permute-start | bytes 786440 | tf_op jit(solution)/shard_map/ppermute | solution.py:301
  51.6 22.6 %collective-permute-start.6 = (f32[4,64,256]{2,1,0:T(8,128)}, f32[4,64,256]{2,1,0:T(8,128)S(1)}, u32[]{:S(2)}, u32[]{:S(2)}) collective-permute-start(f32[4,64,256]{2,1,0:T(8,128)} %get-tuple-element.17), channel_id=1, source_target_pairs={{16,0},{24,8},{0,16},{8,24},{48,32},{56,40},{32,48},{40,56},{80,64... | collective-permute-start | bytes 786440 | tf_op jit(solution)/shard_map/ppermute | solution.py:301
  54.5 19.7 %collective-permute-start.7 = (f32[4,64,256]{2,1,0:T(8,128)}, f32[4,64,256]{2,1,0:T(8,128)S(1)}, u32[]{:S(2)}, u32[]{:S(2)}) collective-permute-start(f32[4,64,256]{2,1,0:T(8,128)} %get-tuple-element.18), channel_id=1, source_target_pairs={{24,0},{0,8},{8,16},{16,24},{56,32},{32,40},{40,48},{48,56},{88,64... | collective-permute-start | bytes 786440 | tf_op jit(solution)/shard_map/ppermute | solution.py:301
  58.6 15.6 %collective-permute-start.8 = (f32[64,256]{1,0:T(8,128)S(1)}, f32[64,256]{1,0:T(8,128)S(1)}, u32[]{:S(2)}, u32[]{:S(2)}) collective-permute-start(f32[64,256]{1,0:T(8,128)S(1)} %skeleton.1.own), channel_id=1, source_target_pairs={{256,0},{264,8},{272,16},{280,24},{288,32},{296,40},{304,48},{312,... | collective-permute-start | bytes 196616 | tf_op jit(solution)/shard_map/ppermute | solution.py:297
  76.0 20.2 %all-to-all-start.1 = ((f32[8,2,64,256]{3,2,1,0:T(8,128)}), f32[8,2,64,256]{3,2,1,0:T(8,128)S(1)}, u32[]{:S(2)}, u32[]{:S(2)}) async-start(f32[8,2,64,256]{3,2,1,0:T(8,128)} %order.1), calls=%async_computation.1 | async-start | bytes 2097152 | tf_op jit(solution)/shard_map/all_to_all | solution.py:361
  97.6 12.3 %all-to-all-start.2 = ((f32[8,32,256]{2,1,0:T(8,128)}), f32[8,32,256]{2,1,0:T(8,128)S(1)}, u32[]{:S(2)}, u32[]{:S(2)}) async-start(f32[8,32,256]{2,1,0:T(8,128)} %side.1), calls=%async_computation.2 | async-start | bytes 524288 | tf_op jit(solution)/shard_map/all_to_all | solution.py:403

commit v6 on v4

--- a/solution.py
+++ b/solution.py
@@ -159,17 +159,12 @@
         facts_ref[LIVE + 2 * k + 1] = jnp.where(index_ref[slot, own] == sibling, live, 0)
 
 
-def order_kernel(facts_ref, near0, near1, near2, relay3, near3, far, out_ref, sem):
+def order_kernel(facts_ref, near0, near1, near2, near3, far, out_ref, sem):
     stacks = (near0, near1, near2, near3)
     copies = []
     for d in range(16):
         slot = facts_ref[d]
-        if d == 8:
-            source = far
-        elif d % 4 == 2 and d // 4 >= 2:
-            source = relay3.at[d // 4 - 2]
-        else:
-            source = stacks[d % 4].at[d // 4]
+        source = far if d == 8 else stacks[d % 4].at[d // 4]
         copies.append(pltpu.make_async_copy(source, out_ref.at[slot // 2, slot % 2], sem.at[d]))
     run_copies(copies)
 
@@ -306,10 +301,9 @@
     )
     theirs = lax.ppermute(mine, "col", [(c, c ^ 1) for c in range(columns)])
     near0 = jnp.stack([down8, down4, skeleton, up4])
-    near2 = shift(jnp.stack([down8, down4]), 2)
+    near2 = shift(near0, 2)
     near1 = shift(near0, 1)
     near3 = shift(near0, 3)
-    relay3 = shift(near3[1:3], 3)
     facts = pl.pallas_call(
         facts_kernel,
         out_shape=shape((64,), jnp.int32),
@@ -321,12 +315,12 @@
     ordered = pl.pallas_call(
         order_kernel,
         out_shape=pltpu.HBM((columns, per_device, rows, RANK), F32),
-        in_specs=[SMEM] + [ANY] * 6,
+        in_specs=[SMEM] + [ANY] * 5,
         out_specs=HBM,
         compiler_params=params(2),
         scratch_shapes=[pltpu.SemaphoreType.DMA((near_index.shape[1],))],
         name="order",
-    )(facts, near0, near1, near2, relay3, near3, far)
+    )(facts, near0, near1, near2, near3, far)
     routed = lax.all_to_all(ordered, "col", split_axis=0, concat_axis=0, tiled=False)
     count = RANK // columns
     high, low, schur, factor = pl.pallas_call(

time: 120 us -> 121 us (level)
  waiting for transfers between devices: 24.5 us -> 31.5 us
  starting transfers between devices: 46.6 us -> 40.6 us
    ppermute x8 -> x7, waiting for transfers between devices: 19 us -> 26.1 us  [shift(): lax.ppermute(x, 'clu', [((i + d) % clusters, i) for i in range(clusters)])]
    ppermute x8 -> x7, starting transfers between devices: 36.4 us -> 30.4 us  [shift(): lax.ppermute(x, 'clu', [((i + d) % clusters, i) for i in range(clusters)])]
  transfers between devices with their start and end apart: 11 -> 10, of which waited for: 4 -> 4; matrix products, arithmetic and copies ran while one was open for 0% -> 0% of each run, Pallas kernels for 19% -> 19%
where the time goes in v6:
time: 121 us; the launch traced here: 120 us
  starting transfers between devices  40.6 us (34%)
  waiting for transfers between devices  31.5 us (26%)
  Pallas kernels  27.5 us (23%)
  blocking collectives  19.4 us (16%)
    ppermute x7, starting transfers between devices, shift(): lax.ppermute(x, 'clu', [((i + d) % clusters, i) for i in range(clusters)])  30.4 us
    ppermute x7, waiting for transfers between devices, shift(): lax.ppermute(x, 'clu', [((i + d) % clusters, i) for i in range(clusters)])  26.1 us
    all_to_all x1, blocking collectives, shards(): lax.all_to_all(spread, 'col', split_axis=0, concat_axis=0, axis_index_gro...  19.4 us
    pallas_call x1, Pallas kernels, shards(): pl.pallas_call(factor_kernel, out_shape=(shape((size, RANK), BF16), shape...  14.2 us
    all_to_all x1, waiting for transfers between devices, shards(): lax.all_to_all(side, 'col', split_axis=0, concat_axis=0, tiled=False)  5.46 us
    all_to_all x1, starting transfers between devices, shards(): lax.all_to_all(side, 'col', split_axis=0, concat_axis=0, tiled=False)  4.72 us
    all_to_all x1, starting transfers between devices, shards(): lax.all_to_all(ordered, 'col', split_axis=0, concat_axis=0, tiled=False)  3.57 us
    pallas_call x1, Pallas kernels, shards(): pl.pallas_call(project_kernel, out_shape=(shape(projected, BF16),) * 2, i...  2.45 us
  transfers between devices with their start and end apart: 10, of which 4 were waited for; matrix products, arithmetic and copies ran while one was open for 0% of the time, Pallas kernels for 19%

profile of v6, /device:TPU:32, one launch (start us, length us, event | category | flops | bytes accessed | tf_op | source)
XLA Modules:
  0.0 119.8 jit_solution(5568067231211943011)
XLA Ops:
  0.6 2.0 %spread.1 = f32[4,128,512]{2,1,0:T(8,128)} custom-call(f32[64,512]{1,0:T(8,128)} %bitcast.15, f32[64,512]{1,0:T(8,128)} %bitcast.12), custom_call_target="tpu_custom_call" | custom-call | tf_op jit(solution)/shard_map/spread/pallas_call | solution.py:289
  2.6 19.4 %all_to_all.15.mine_ref = f32[4,128,512]{2,1,0:T(8,128)S(1)} all-to-all(f32[4,128,512]{2,1,0:T(8,128)} %spread.1), channel_id=1, replica_groups={{0,2,4,6},{1,3,5,7},{8,10,12,14},{9,11,13,15},{16,18,20,22},{17,19,21,2..., dimensions={0} | all-to-all | bytes 2097152 | tf_op jit(solution)/shard_map/all_to_all | solution.py:299
  22.0 1.9 %collective-permute-start = (f32[4,128,512]{2,1,0:T(8,128)S(1)}, f32[4,128,512]{2,1,0:T(8,128)S(1)}, u32[]{:S(2)}, u32[]{:S(2)}) collective-permute-start(f32[4,128,512]{2,1,0:T(8,128)S(1)} %all_to_all.15.mine_ref), channel_id=1, source_target_pairs={{0,1},{1,0},{2,3},{3,2},{4,5},{5,4},{6,7},{7,6},{8,9},{9,8},{10,11... | collective-permute-start | bytes 3145736 | tf_op jit(solution)/shard_map/ppermute | solution.py:302
  23.9 0.9 skeleton.1
  24.8 2.3 %collective-permute-start.3 = (f32[64,256]{1,0:T(8,128)S(1)}, f32[64,256]{1,0:T(8,128)S(1)}, u32[]{:S(2)}, u32[]{:S(2)}) collective-permute-start(f32[64,256]{1,0:T(8,128)S(1)} %skeleton.1), channel_id=1, source_target_pairs={{32,0},{40,8},{48,16},{56,24},{64,32},{72,40},{80,48},{88,56},{96,... | collective-permute-start | bytes 196616 | tf_op jit(solution)/shard_map/ppermute | solution.py:273
  27.1 3.5 %collective-permute-start.2 = (f32[64,256]{1,0:T(8,128)S(1)}, f32[64,256]{1,0:T(8,128)S(1)}, u32[]{:S(2)}, u32[]{:S(2)}) collective-permute-start(f32[64,256]{1,0:T(8,128)S(1)} %skeleton.1), channel_id=1, source_target_pairs={{480,0},{488,8},{496,16},{504,24},{0,32},{8,40},{16,48},{24,56},{3... | collective-permute-start | bytes 196616 | tf_op jit(solution)/shard_map/ppermute | solution.py:273
  30.6 6.4 %collective-permute-start.1 = (f32[64,256]{1,0:T(8,128)S(1)}, f32[64,256]{1,0:T(8,128)S(1)}, u32[]{:S(2)}, u32[]{:S(2)}) collective-permute-start(f32[64,256]{1,0:T(8,128)S(1)} %skeleton.1), channel_id=1, source_target_pairs={{448,0},{456,8},{464,16},{472,24},{480,32},{488,40},{496,48},{504,... | collective-permute-start | bytes 196616 | tf_op jit(solution)/shard_map/ppermute | solution.py:273
  37.0 0.0 collective-permute-done.3
  37.1 3.6 %collective-permute-done.2 = f32[64,256]{1,0:T(8,128)S(1)} collective-permute-done((f32[64,256]{1,0:T(8,128)S(1)}, f32[64,256]{1,0:T(8,128)S(1)}, u32[]{:S(2)}, u32[]{:S(2)}) %collective-permute-start.2) | collective-permute-done | bytes 65568 | tf_op jit(solution)/shard_map/ppermute | solution.py:273
  40.7 5.8 %collective-permute-done.1 = f32[64,256]{1,0:T(8,128)S(1)} collective-permute-done((f32[64,256]{1,0:T(8,128)S(1)}, f32[64,256]{1,0:T(8,128)S(1)}, u32[]{:S(2)}, u32[]{:S(2)}) %collective-permute-start.1) | collective-permute-done | bytes 65568 | tf_op jit(solution)/shard_map/ppermute | solution.py:273
  46.5 4.8 %collective-permute-start.4 = (f32[4,64,256]{2,1,0:T(8,128)S(1)}, f32[4,64,256]{2,1,0:T(8,128)S(1)}, u32[]{:S(2)}, u32[]{:S(2)}) collective-permute-start(f32[4,64,256]{2,1,0:T(8,128)S(1)} %pad_maximum_fusion.near0), channel_id=1, source_target_pairs={{8,0},{16,8},{24,16},{32,24},{40,32},{48,40},{56,48},{64,56},{72,6... | collective-permute-start | bytes 786440 | tf_op jit(solution)/shard_map/ppermute | solution.py:273
  51.3 2.5 %collective-permute-start.5 = (f32[4,64,256]{2,1,0:T(8,128)S(1)}, f32[4,64,256]{2,1,0:T(8,128)S(1)}, u32[]{:S(2)}, u32[]{:S(2)}) collective-permute-start(f32[4,64,256]{2,1,0:T(8,128)S(1)} %pad_maximum_fusion.near0), channel_id=1, source_target_pairs={{16,0},{24,8},{32,16},{40,24},{48,32},{56,40},{64,48},{72,56},{80,... | collective-permute-start | bytes 786440 | tf_op jit(solution)/shard_map/ppermute | solution.py:273
  53.8 4.3 %collective-permute-start.6 = (f32[4,64,256]{2,1,0:T(8,128)S(1)}, f32[4,64,256]{2,1,0:T(8,128)S(1)}, u32[]{:S(2)}, u32[]{:S(2)}) collective-permute-start(f32[4,64,256]{2,1,0:T(8,128)S(1)} %pad_maximum_fusion.near0), channel_id=1, source_target_pairs={{24,0},{32,8},{40,16},{48,24},{56,32},{64,40},{72,48},{80,56},{88,... | collective-permute-start | bytes 786440 | tf_op jit(solution)/shard_map/ppermute | solution.py:273
  58.1 6.5 %collective-permute-start.7 = (f32[64,256]{1,0:T(8,128)S(1)}, f32[64,256]{1,0:T(8,128)S(1)}, u32[]{:S(2)}, u32[]{:S(2)}) collective-permute-start(f32[64,256]{1,0:T(8,128)S(1)} %skeleton.1), channel_id=1, source_target_pairs={{256,0},{264,8},{272,16},{280,24},{288,32},{296,40},{304,48},{312,... | collective-permute-start | bytes 196616 | tf_op jit(solution)/shard_map/ppermute | solution.py:273
  64.7 1.5 %facts.1.facts_ref = s32[64]{0:T(128)} custom-call(s32[16,64]{1,0:T(8,128)} %bitcast.20, s32[1,16]{1,0:T(1,128)} %mask_ref.1, s32[64]{0:T(128)} %parent_ref.1), custom_call_target="tpu_custom_call" | custom-call | tf_op jit(solution)/shard_map/facts/pallas_call | solution.py:307
  66.2 16.7 %collective-permute-done.7.far = f32[64,256]{1,0:T(8,128)S(1)} collective-permute-done((f32[64,256]{1,0:T(8,128)S(1)}, f32[64,256]{1,0:T(8,128)S(1)}, u32[]{:S(2)}, u32[]{:S(2)}) %collective-permute-start.7) | collective-permute-done | bytes 65568 | tf_op jit(solution)/shard_map/ppermute | solution.py:273
  82.8 0.0 collective-permute-done.4.near1
  82.8 0.0 collective-permute-done.5.near2
  82.8 0.0 collective-permute-done.6.near3
  82.9 1.8 %order.1 = f32[8,2,64,256]{3,2,1,0:T(8,128)} custom-call(s32[64]{0:T(128)} %facts.1.facts_ref, f32[4,64,256]{2,1,0:T(8,128)S(1)} %pad_maximum_fusion.near0, f32[4,64,256]{2,1,0:T(8,128)S(1)} %collective-permute-done.4.near1, f32[4,64,256]{2,1,0:T(8,128)S(1)} %collective-permute-done.5.near2, f32[4,64,256]{2,1,0:T(8,128)S(1)} %collective-permute-done.6.near3, ...), custom_call_target="tpu_custom_call" | custom-call | tf_op jit(solution)/shard_map/order/pallas_call | solution.py:315
  84.7 3.6 %all-to-all-start.1 = ((f32[8,2,64,256]{3,2,1,0:T(8,128)}), f32[8,2,64,256]{3,2,1,0:T(8,128)S(1)}, u32[]{:S(2)}, u32[]{:S(2)}) async-start(f32[8,2,64,256]{3,2,1,0:T(8,128)} %order.1), calls=%async_computation.1 | async-start | bytes 2097152 | tf_op jit(solution)/shard_map/all_to_all | solution.py:324
  88.2 0.0 collective-permute-done.theirs_ref
  88.3 14.2 %factor.1 = (bf16[512,256]{1,0:T(8,128)(2,1)S(1)}, bf16[512,256]{1,0:T(8,128)(2,1)S(1)}, f32[32,256]{1,0:T(8,128)S(1)}, f32[32,256]{1,0:T(8,128)}) custom-call(f32[4,128,512]{2,1,0:T(8,128)S(1)} %all_to_all.15.mine_ref, f32[4,128,512]{2,1,0:T(8,128)S(1)} %collective-permute-done.theirs_ref), custom_call_target="tpu_custom_call" | custom-call | flops 6000000000 | bytes 4000000 | tf_op jit(solution)/shard_map/factor/pallas_call | solution.py:326
  102.4 2.4 %project.1 = (bf16[2,256,512]{2,1,0:T(8,128)(2,1)S(1)}, bf16[2,256,512]{2,1,0:T(8,128)(2,1)S(1)}) custom-call(f32[2,512,512]{2,1,0:T(8,128)} %bitcast.21, bf16[512,256]{1,0:T(8,128)(2,1)S(1)} %get-tuple-element.9.high_ref, bf16[512,256]{1,0:T(8,128)(2,1)S(1)} %get-tuple-element.10.low_ref), custom_call_target="tpu_custom_call" | custom-call | flops 1000000000 | bytes 4000000 | tf_op jit(solution)/shard_map/project/pallas_call | solution.py:344
  104.9 0.0 all-to-all-done.1.routed_ref
  104.9 1.4 %side.1 = f32[8,32,256]{2,1,0:T(8,128)} custom-call(s32[64]{0:T(128)} %facts.1.facts_ref, bf16[2,256,512]{2,1,0:T(8,128)(2,1)S(1)} %get-tuple-element.11.high_ref, bf16[2,256,512]{2,1,0:T(8,128)(2,1)S(1)} %get-tuple-element.12.low_ref, f32[8,2,64,256]{3,2,1,0:T(8,128)S(1)} %all-to-all-done.1.routed_ref), custom_call_target="tpu_custom_call" | custom-call | flops 200000000 | bytes 2000000 | tf_op jit(solution)/shard_map/side/pallas_call | solution.py:357
  106.3 4.7 %all-to-all-start.2 = ((f32[8,32,256]{2,1,0:T(8,128)}), f32[8,32,256]{2,1,0:T(8,128)S(1)}, u32[]{:S(2)}, u32[]{:S(2)}) async-start(f32[8,32,256]{2,1,0:T(8,128)} %side.1), calls=%async_computation.2 | async-start | bytes 524288 | tf_op jit(solution)/shard_map/all_to_all | solution.py:366
  111.0 2.0 %couple.1 = f32[2,256,256]{2,1,0:T(8,128)} custom-call(s32[64]{0:T(128)} %facts.1.facts_ref, bf16[2,256,512]{2,1,0:T(8,128)(2,1)S(1)} %get-tuple-element.11.high_ref, bf16[2,256,512]{2,1,0:T(8,128)(2,1)S(1)} %get-tuple-element.12.low_ref, f32[8,2,64,256]{3,2,1,0:T(8,128)S(1)} %all-to-all-done.1.routed_ref), custom_call_target="tpu_custom_call" | custom-call | flops 400000000 | bytes 4000000 | tf_op jit(solution)/shard_map/couple/pallas_call | solution.py:367
  113.1 5.5 %all-to-all-done.2.parts_ref = f32[8,32,256]{2,1,0:T(8,128)S(1)} async-done(((f32[8,32,256]{2,1,0:T(8,128)}), f32[8,32,256]{2,1,0:T(8,128)S(1)}, u32[]{:S(2)}, u32[]{:S(2)}) %all-to-all-start.2) | async-done | bytes 262176 | tf_op jit(solution)/shard_map/all_to_all | solution.py:366
  118.5 1.3 %merge.1 = f32[32,512]{1,0:T(8,128)} custom-call(s32[64]{0:T(128)} %facts.1.facts_ref, f32[8,32,256]{2,1,0:T(8,128)S(1)} %all-to-all-done.2.parts_ref, f32[32,256]{1,0:T(8,128)S(1)} %get-tuple-element.13.schur_ref), custom_call_target="tpu_custom_call" | custom-call | tf_op jit(solution)/shard_map/merge/pallas_call | solution.py:376
  (1 shorter events, 0.0 us)
Async XLA Ops:
  22.0 66.2 %collective-permute-start = (f32[4,128,512]{2,1,0:T(8,128)S(1)}, f32[4,128,512]{2,1,0:T(8,128)S(1)}, u32[]{:S(2)}, u32[]{:S(2)}) collective-permute-start(f32[4,128,512]{2,1,0:T(8,128)S(1)} %all_to_all.15.mine_ref), channel_id=1, source_target_pairs={{0,1},{1,0},{2,3},{3,2},{4,5},{5,4},{6,7},{7,6},{8,9},{9,8},{10,11... | collective-permute-start | bytes 3145736 | tf_op jit(solution)/shard_map/ppermute | solution.py:302
  24.8 12.3 %collective-permute-start.3 = (f32[64,256]{1,0:T(8,128)S(1)}, f32[64,256]{1,0:T(8,128)S(1)}, u32[]{:S(2)}, u32[]{:S(2)}) collective-permute-start(f32[64,256]{1,0:T(8,128)S(1)} %skeleton.1), channel_id=1, source_target_pairs={{32,0},{40,8},{48,16},{56,24},{64,32},{72,40},{80,48},{88,56},{96,... | collective-permute-start | bytes 196616 | tf_op jit(solution)/shard_map/ppermute | solution.py:273
  27.1 13.5 %collective-permute-start.2 = (f32[64,256]{1,0:T(8,128)S(1)}, f32[64,256]{1,0:T(8,128)S(1)}, u32[]{:S(2)}, u32[]{:S(2)}) collective-permute-start(f32[64,256]{1,0:T(8,128)S(1)} %skeleton.1), channel_id=1, source_target_pairs={{480,0},{488,8},{496,16},{504,24},{0,32},{8,40},{16,48},{24,56},{3... | collective-permute-start | bytes 196616 | tf_op jit(solution)/shard_map/ppermute | solution.py:273
  30.6 15.8 %collective-permute-start.1 = (f32[64,256]{1,0:T(8,128)S(1)}, f32[64,256]{1,0:T(8,128)S(1)}, u32[]{:S(2)}, u32[]{:S(2)}) collective-permute-start(f32[64,256]{1,0:T(8,128)S(1)} %skeleton.1), channel_id=1, source_target_pairs={{448,0},{456,8},{464,16},{472,24},{480,32},{488,40},{496,48},{504,... | collective-permute-start | bytes 196616 | tf_op jit(solution)/shard_map/ppermute | solution.py:273
  46.5 36.4 %collective-permute-start.4 = (f32[4,64,256]{2,1,0:T(8,128)S(1)}, f32[4,64,256]{2,1,0:T(8,128)S(1)}, u32[]{:S(2)}, u32[]{:S(2)}) collective-permute-start(f32[4,64,256]{2,1,0:T(8,128)S(1)} %pad_maximum_fusion.near0), channel_id=1, source_target_pairs={{8,0},{16,8},{24,16},{32,24},{40,32},{48,40},{56,48},{64,56},{72,6... | collective-permute-start | bytes 786440 | tf_op jit(solution)/shard_map/ppermute | solution.py:273
  51.3 31.6 %collective-permute-start.5 = (f32[4,64,256]{2,1,0:T(8,128)S(1)}, f32[4,64,256]{2,1,0:T(8,128)S(1)}, u32[]{:S(2)}, u32[]{:S(2)}) collective-permute-start(f32[4,64,256]{2,1,0:T(8,128)S(1)} %pad_maximum_fusion.near0), channel_id=1, source_target_pairs={{16,0},{24,8},{32,16},{40,24},{48,32},{56,40},{64,48},{72,56},{80,... | collective-permute-start | bytes 786440 | tf_op jit(solution)/shard_map/ppermute | solution.py:273
  53.8 29.0 %collective-permute-start.6 = (f32[4,64,256]{2,1,0:T(8,128)S(1)}, f32[4,64,256]{2,1,0:T(8,128)S(1)}, u32[]{:S(2)}, u32[]{:S(2)}) collective-permute-start(f32[4,64,256]{2,1,0:T(8,128)S(1)} %pad_maximum_fusion.near0), channel_id=1, source_target_pairs={{24,0},{32,8},{40,16},{48,24},{56,32},{64,40},{72,48},{80,56},{88,... | collective-permute-start | bytes 786440 | tf_op jit(solution)/shard_map/ppermute | solution.py:273
  58.1 24.7 %collective-permute-start.7 = (f32[64,256]{1,0:T(8,128)S(1)}, f32[64,256]{1,0:T(8,128)S(1)}, u32[]{:S(2)}, u32[]{:S(2)}) collective-permute-start(f32[64,256]{1,0:T(8,128)S(1)} %skeleton.1), channel_id=1, source_target_pairs={{256,0},{264,8},{272,16},{280,24},{288,32},{296,40},{304,48},{312,... | collective-permute-start | bytes 196616 | tf_op jit(solution)/shard_map/ppermute | solution.py:273
  84.7 20.2 %all-to-all-start.1 = ((f32[8,2,64,256]{3,2,1,0:T(8,128)}), f32[8,2,64,256]{3,2,1,0:T(8,128)S(1)}, u32[]{:S(2)}, u32[]{:S(2)}) async-start(f32[8,2,64,256]{3,2,1,0:T(8,128)} %order.1), calls=%async_computation.1 | async-start | bytes 2097152 | tf_op jit(solution)/shard_map/all_to_all | solution.py:324
  106.3 12.2 %all-to-all-start.2 = ((f32[8,32,256]{2,1,0:T(8,128)}), f32[8,32,256]{2,1,0:T(8,128)S(1)}, u32[]{:S(2)}, u32[]{:S(2)}) async-start(f32[8,32,256]{2,1,0:T(8,128)} %side.1), calls=%async_computation.2 | async-start | bytes 524288 | tf_op jit(solution)/shard_map/all_to_all | solution.py:366

commit v7 on v6

--- a/solution.py
+++ b/solution.py
@@ -272,6 +272,15 @@
     def shift(x, d):
         return lax.ppermute(x, "clu", [((i + d) % clusters, i) for i in range(clusters)])
 
+    def quarter_turn(x):
+        step = clusters // 4
+        pairs = [
+            ((i + (step if c % 2 == 0 else -step)) % clusters * columns + c, i * columns + c)
+            for i in range(clusters)
+            for c in range(columns)
+        ]
+        return lax.ppermute(x, ("clu", "col"), pairs)
+
     skeleton = pl.pallas_call(
         slice_kernel,
         out_shape=shape((rows, RANK), F32),
@@ -281,7 +290,8 @@
         compiler_params=params(4),
         name="skeleton",
     )(keep_out(bases[0]))
-    far = shift(skeleton, clusters // 2)
+    halfway = quarter_turn(skeleton)
+    far = quarter_turn(halfway)
     down8 = shift(skeleton, -8)
     down4 = shift(skeleton, -4)
     up4 = shift(skeleton, 4)

time: 121 us -> 123 us (1.017)
  the two profiles are of different devices: /device:TPU:32 before, /device:TPU:1 now
where the time goes in v7:
time: 123 us; the launch traced here: 122 us
  starting transfers between devices  55 us (45%)
  Pallas kernels  27.5 us (22%)
  waiting for transfers between devices  24 us (20%)
  blocking collectives  14.6 us (12%)
    ppermute x6, starting transfers between devices, shift(): lax.ppermute(x, 'clu', [((i + d) % clusters, i) for i in range(clusters)])  25.9 us
    all_to_all x1, blocking collectives, shards(): lax.all_to_all(spread, 'col', split_axis=0, concat_axis=0, axis_index_gro...  14.6 us
    ppermute x2, waiting for transfers between devices, quarter_turn(): return lax.ppermute(x, ('clu', 'col'), pairs)  14.3 us
    pallas_call x1, Pallas kernels, shards(): pl.pallas_call(factor_kernel, out_shape=(shape((size, RANK), BF16), shape...  14.2 us
    all_to_all x1, starting transfers between devices, shards(): lax.all_to_all(ordered, 'col', split_axis=0, concat_axis=0, tiled=False)  11.3 us
    ppermute x1, starting transfers between devices, shards(): theirs = lax.ppermute(mine, 'col', [(c, c ^ 1) for c in range(columns)])  8.54 us
    ppermute x6, waiting for transfers between devices, shift(): lax.ppermute(x, 'clu', [((i + d) % clusters, i) for i in range(clusters)])  5.29 us
    all_to_all x1, starting transfers between devices, shards(): lax.all_to_all(side, 'col', split_axis=0, concat_axis=0, tiled=False)  4.92 us
  transfers between devices with their start and end apart: 11, of which 5 were waited for; matrix products, arithmetic and copies ran while one was open for 0% of the time, Pallas kernels for 19%

profile of v7, /device:TPU:1, one launch (start us, length us, event | category | flops | bytes accessed | tf_op | source)
XLA Modules:
  0.0 121.8 jit_solution(12685172339375853251)
XLA Ops:
  0.6 2.0 %spread.1 = f32[4,128,512]{2,1,0:T(8,128)} custom-call(f32[64,512]{1,0:T(8,128)} %bitcast.15, f32[64,512]{1,0:T(8,128)} %bitcast.12), custom_call_target="tpu_custom_call" | custom-call | tf_op jit(solution)/shard_map/spread/pallas_call | solution.py:299
  2.6 14.6 %all_to_all.15.mine_ref = f32[4,128,512]{2,1,0:T(8,128)S(1)} all-to-all(f32[4,128,512]{2,1,0:T(8,128)} %spread.1), channel_id=1, replica_groups={{0,2,4,6},{1,3,5,7},{8,10,12,14},{9,11,13,15},{16,18,20,22},{17,19,21,2..., dimensions={0} | all-to-all | bytes 2097152 | tf_op jit(solution)/shard_map/all_to_all | solution.py:309
  17.2 8.5 %collective-permute-start = (f32[4,128,512]{2,1,0:T(8,128)S(1)}, f32[4,128,512]{2,1,0:T(8,128)S(1)}, u32[]{:S(2)}, u32[]{:S(2)}) collective-permute-start(f32[4,128,512]{2,1,0:T(8,128)S(1)} %all_to_all.15.mine_ref), channel_id=1, source_target_pairs={{0,1},{1,0},{2,3},{3,2},{4,5},{5,4},{6,7},{7,6},{8,9},{9,8},{10,11... | collective-permute-start | bytes 3145736 | tf_op jit(solution)/shard_map/ppermute | solution.py:312
  25.8 0.9 skeleton.1
  26.6 10.8 %collective-permute-start.3 = (f32[64,256]{1,0:T(8,128)S(1)}, f32[64,256]{1,0:T(8,128)S(1)}, u32[]{:S(2)}, u32[]{:S(2)}) collective-permute-start(f32[64,256]{1,0:T(8,128)S(1)} %skeleton.1), channel_id=1, source_target_pairs={{32,0},{40,8},{48,16},{56,24},{64,32},{72,40},{80,48},{88,56},{96,... | collective-permute-start | bytes 196616 | tf_op jit(solution)/shard_map/ppermute | solution.py:273
  37.4 1.9 %collective-permute-start.2 = (f32[64,256]{1,0:T(8,128)S(1)}, f32[64,256]{1,0:T(8,128)S(1)}, u32[]{:S(2)}, u32[]{:S(2)}) collective-permute-start(f32[64,256]{1,0:T(8,128)S(1)} %skeleton.1), channel_id=1, source_target_pairs={{480,0},{488,8},{496,16},{504,24},{0,32},{8,40},{16,48},{24,56},{3... | collective-permute-start | bytes 196616 | tf_op jit(solution)/shard_map/ppermute | solution.py:273
  39.3 1.9 %collective-permute-start.1 = (f32[64,256]{1,0:T(8,128)S(1)}, f32[64,256]{1,0:T(8,128)S(1)}, u32[]{:S(2)}, u32[]{:S(2)}) collective-permute-start(f32[64,256]{1,0:T(8,128)S(1)} %skeleton.1), channel_id=1, source_target_pairs={{448,0},{456,8},{464,16},{472,24},{480,32},{488,40},{496,48},{504,... | collective-permute-start | bytes 196616 | tf_op jit(solution)/shard_map/ppermute | solution.py:273
  41.3 0.0 collective-permute-done.3
  41.3 2.4 %collective-permute-done.2 = f32[64,256]{1,0:T(8,128)S(1)} collective-permute-done((f32[64,256]{1,0:T(8,128)S(1)}, f32[64,256]{1,0:T(8,128)S(1)}, u32[]{:S(2)}, u32[]{:S(2)}) %collective-permute-start.2) | collective-permute-done | bytes 65568 | tf_op jit(solution)/shard_map/ppermute | solution.py:273
  43.6 2.9 %collective-permute-done.1 = f32[64,256]{1,0:T(8,128)S(1)} collective-permute-done((f32[64,256]{1,0:T(8,128)S(1)}, f32[64,256]{1,0:T(8,128)S(1)}, u32[]{:S(2)}, u32[]{:S(2)}) %collective-permute-start.1) | collective-permute-done | bytes 65568 | tf_op jit(solution)/shard_map/ppermute | solution.py:273
  46.6 7.0 %collective-permute-start.4 = (f32[4,64,256]{2,1,0:T(8,128)S(1)}, f32[4,64,256]{2,1,0:T(8,128)S(1)}, u32[]{:S(2)}, u32[]{:S(2)}) collective-permute-start(f32[4,64,256]{2,1,0:T(8,128)S(1)} %pad_maximum_fusion.near0), channel_id=1, source_target_pairs={{8,0},{16,8},{24,16},{32,24},{40,32},{48,40},{56,48},{64,56},{72,6... | collective-permute-start | bytes 786440 | tf_op jit(solution)/shard_map/ppermute | solution.py:273
  53.6 2.3 %collective-permute-start.5 = (f32[4,64,256]{2,1,0:T(8,128)S(1)}, f32[4,64,256]{2,1,0:T(8,128)S(1)}, u32[]{:S(2)}, u32[]{:S(2)}) collective-permute-start(f32[4,64,256]{2,1,0:T(8,128)S(1)} %pad_maximum_fusion.near0), channel_id=1, source_target_pairs={{16,0},{24,8},{32,16},{40,24},{48,32},{56,40},{64,48},{72,56},{80,... | collective-permute-start | bytes 786440 | tf_op jit(solution)/shard_map/ppermute | solution.py:273
  55.9 1.9 %collective-permute-start.6 = (f32[4,64,256]{2,1,0:T(8,128)S(1)}, f32[4,64,256]{2,1,0:T(8,128)S(1)}, u32[]{:S(2)}, u32[]{:S(2)}) collective-permute-start(f32[4,64,256]{2,1,0:T(8,128)S(1)} %pad_maximum_fusion.near0), channel_id=1, source_target_pairs={{24,0},{32,8},{40,16},{48,24},{56,32},{64,40},{72,48},{80,56},{88,... | collective-permute-start | bytes 786440 | tf_op jit(solution)/shard_map/ppermute | solution.py:273
  57.8 2.4 %collective-permute-start.7 = (f32[64,256]{1,0:T(8,128)S(1)}, f32[64,256]{1,0:T(8,128)S(1)}, u32[]{:S(2)}, u32[]{:S(2)}) collective-permute-start(f32[64,256]{1,0:T(8,128)S(1)} %skeleton.1), channel_id=1, source_target_pairs={{128,0},{385,1},{130,2},{387,3},{132,4},{389,5},{134,6},{391,7},{1... | collective-permute-start | bytes 196616 | tf_op jit(solution)/shard_map/ppermute | solution.py:282
  60.2 8.0 %collective-permute-done.7 = f32[64,256]{1,0:T(8,128)S(1)} collective-permute-done((f32[64,256]{1,0:T(8,128)S(1)}, f32[64,256]{1,0:T(8,128)S(1)}, u32[]{:S(2)}, u32[]{:S(2)}) %collective-permute-start.7) | collective-permute-done | bytes 65568 | tf_op jit(solution)/shard_map/ppermute | solution.py:282
  68.2 1.9 %collective-permute-start.8 = (f32[64,256]{1,0:T(8,128)S(1)}, f32[64,256]{1,0:T(8,128)S(1)}, u32[]{:S(2)}, u32[]{:S(2)}) collective-permute-start(f32[64,256]{1,0:T(8,128)S(1)} %collective-permute-done.7), channel_id=1, source_target_pairs={{128,0},{385,1},{130,2},{387,3},{132,4},{389,5},{134,6},{391,7},{1... | collective-permute-start | bytes 196616 | tf_op jit(solution)/shard_map/ppermute | solution.py:282
  70.2 1.5 %facts.1.facts_ref = s32[64]{0:T(128)} custom-call(s32[16,64]{1,0:T(8,128)} %bitcast.20, s32[1,16]{1,0:T(1,128)} %mask_ref.1, s32[64]{0:T(128)} %parent_ref.1), custom_call_target="tpu_custom_call" | custom-call | tf_op jit(solution)/shard_map/facts/pallas_call | solution.py:317
  71.7 6.3 %collective-permute-done.8.far = f32[64,256]{1,0:T(8,128)S(1)} collective-permute-done((f32[64,256]{1,0:T(8,128)S(1)}, f32[64,256]{1,0:T(8,128)S(1)}, u32[]{:S(2)}, u32[]{:S(2)}) %collective-permute-start.8) | collective-permute-done | bytes 65568 | tf_op jit(solution)/shard_map/ppermute | solution.py:282
  77.9 0.0 collective-permute-done.4.near1
  77.9 0.0 collective-permute-done.5.near2
  77.9 0.0 collective-permute-done.6.near3
  78.0 1.8 %order.1 = f32[8,2,64,256]{3,2,1,0:T(8,128)} custom-call(s32[64]{0:T(128)} %facts.1.facts_ref, f32[4,64,256]{2,1,0:T(8,128)S(1)} %pad_maximum_fusion.near0, f32[4,64,256]{2,1,0:T(8,128)S(1)} %collective-permute-done.4.near1, f32[4,64,256]{2,1,0:T(8,128)S(1)} %collective-permute-done.5.near2, f32[4,64,256]{2,1,0:T(8,128)S(1)} %collective-permute-done.6.near3, ...), custom_call_target="tpu_custom_call" | custom-call | tf_op jit(solution)/shard_map/order/pallas_call | solution.py:325
  79.8 11.3 %all-to-all-start.1 = ((f32[8,2,64,256]{3,2,1,0:T(8,128)}), f32[8,2,64,256]{3,2,1,0:T(8,128)S(1)}, u32[]{:S(2)}, u32[]{:S(2)}) async-start(f32[8,2,64,256]{3,2,1,0:T(8,128)} %order.1), calls=%async_computation.1 | async-start | bytes 2097152 | tf_op jit(solution)/shard_map/all_to_all | solution.py:334
  91.1 0.0 collective-permute-done.theirs_ref
  91.1 14.2 %factor.1 = (bf16[512,256]{1,0:T(8,128)(2,1)S(1)}, bf16[512,256]{1,0:T(8,128)(2,1)S(1)}, f32[32,256]{1,0:T(8,128)S(1)}, f32[32,256]{1,0:T(8,128)}) custom-call(f32[4,128,512]{2,1,0:T(8,128)S(1)} %all_to_all.15.mine_ref, f32[4,128,512]{2,1,0:T(8,128)S(1)} %collective-permute-done.theirs_ref), custom_call_target="tpu_custom_call" | custom-call | flops 6000000000 | bytes 4000000 | tf_op jit(solution)/shard_map/factor/pallas_call | solution.py:336
  105.3 2.4 %project.1 = (bf16[2,256,512]{2,1,0:T(8,128)(2,1)S(1)}, bf16[2,256,512]{2,1,0:T(8,128)(2,1)S(1)}) custom-call(f32[2,512,512]{2,1,0:T(8,128)} %bitcast.21, bf16[512,256]{1,0:T(8,128)(2,1)S(1)} %get-tuple-element.9.high_ref, bf16[512,256]{1,0:T(8,128)(2,1)S(1)} %get-tuple-element.10.low_ref), custom_call_target="tpu_custom_call" | custom-call | flops 1000000000 | bytes 4000000 | tf_op jit(solution)/shard_map/project/pallas_call | solution.py:354
  107.7 0.0 all-to-all-done.1.routed_ref
  107.7 1.4 %side.1 = f32[8,32,256]{2,1,0:T(8,128)} custom-call(s32[64]{0:T(128)} %facts.1.facts_ref, bf16[2,256,512]{2,1,0:T(8,128)(2,1)S(1)} %get-tuple-element.11.high_ref, bf16[2,256,512]{2,1,0:T(8,128)(2,1)S(1)} %get-tuple-element.12.low_ref, f32[8,2,64,256]{3,2,1,0:T(8,128)S(1)} %all-to-all-done.1.routed_ref), custom_call_target="tpu_custom_call" | custom-call | flops 200000000 | bytes 2000000 | tf_op jit(solution)/shard_map/side/pallas_call | solution.py:367
  109.1 4.9 %all-to-all-start.2 = ((f32[8,32,256]{2,1,0:T(8,128)}), f32[8,32,256]{2,1,0:T(8,128)S(1)}, u32[]{:S(2)}, u32[]{:S(2)}) async-start(f32[8,32,256]{2,1,0:T(8,128)} %side.1), calls=%async_computation.2 | async-start | bytes 524288 | tf_op jit(solution)/shard_map/all_to_all | solution.py:376
  114.1 2.0 %couple.1 = f32[2,256,256]{2,1,0:T(8,128)} custom-call(s32[64]{0:T(128)} %facts.1.facts_ref, bf16[2,256,512]{2,1,0:T(8,128)(2,1)S(1)} %get-tuple-element.11.high_ref, bf16[2,256,512]{2,1,0:T(8,128)(2,1)S(1)} %get-tuple-element.12.low_ref, f32[8,2,64,256]{3,2,1,0:T(8,128)S(1)} %all-to-all-done.1.routed_ref), custom_call_target="tpu_custom_call" | custom-call | flops 400000000 | bytes 4000000 | tf_op jit(solution)/shard_map/couple/pallas_call | solution.py:377
  116.1 4.4 %all-to-all-done.2.parts_ref = f32[8,32,256]{2,1,0:T(8,128)S(1)} async-done(((f32[8,32,256]{2,1,0:T(8,128)}), f32[8,32,256]{2,1,0:T(8,128)S(1)}, u32[]{:S(2)}, u32[]{:S(2)}) %all-to-all-start.2) | async-done | bytes 262176 | tf_op jit(solution)/shard_map/all_to_all | solution.py:376
  120.5 1.3 %merge.1 = f32[32,512]{1,0:T(8,128)} custom-call(s32[64]{0:T(128)} %facts.1.facts_ref, f32[8,32,256]{2,1,0:T(8,128)S(1)} %all-to-all-done.2.parts_ref, f32[32,256]{1,0:T(8,128)S(1)} %get-tuple-element.13.schur_ref), custom_call_target="tpu_custom_call" | custom-call | tf_op jit(solution)/shard_map/merge/pallas_call | solution.py:386
  (1 shorter events, 0.0 us)
Async XLA Ops:
  17.2 73.9 %collective-permute-start = (f32[4,128,512]{2,1,0:T(8,128)S(1)}, f32[4,128,512]{2,1,0:T(8,128)S(1)}, u32[]{:S(2)}, u32[]{:S(2)}) collective-permute-start(f32[4,128,512]{2,1,0:T(8,128)S(1)} %all_to_all.15.mine_ref), channel_id=1, source_target_pairs={{0,1},{1,0},{2,3},{3,2},{4,5},{5,4},{6,7},{7,6},{8,9},{9,8},{10,11... | collective-permute-start | bytes 3145736 | tf_op jit(solution)/shard_map/ppermute | solution.py:312
  26.6 14.7 %collective-permute-start.3 = (f32[64,256]{1,0:T(8,128)S(1)}, f32[64,256]{1,0:T(8,128)S(1)}, u32[]{:S(2)}, u32[]{:S(2)}) collective-permute-start(f32[64,256]{1,0:T(8,128)S(1)} %skeleton.1), channel_id=1, source_target_pairs={{32,0},{40,8},{48,16},{56,24},{64,32},{72,40},{80,48},{88,56},{96,... | collective-permute-start | bytes 196616 | tf_op jit(solution)/shard_map/ppermute | solution.py:273
  37.4 6.2 %collective-permute-start.2 = (f32[64,256]{1,0:T(8,128)S(1)}, f32[64,256]{1,0:T(8,128)S(1)}, u32[]{:S(2)}, u32[]{:S(2)}) collective-permute-start(f32[64,256]{1,0:T(8,128)S(1)} %skeleton.1), channel_id=1, source_target_pairs={{480,0},{488,8},{496,16},{504,24},{0,32},{8,40},{16,48},{24,56},{3... | collective-permute-start | bytes 196616 | tf_op jit(solution)/shard_map/ppermute | solution.py:273
  39.3 7.2 %collective-permute-start.1 = (f32[64,256]{1,0:T(8,128)S(1)}, f32[64,256]{1,0:T(8,128)S(1)}, u32[]{:S(2)}, u32[]{:S(2)}) collective-permute-start(f32[64,256]{1,0:T(8,128)S(1)} %skeleton.1), channel_id=1, source_target_pairs={{448,0},{456,8},{464,16},{472,24},{480,32},{488,40},{496,48},{504,... | collective-permute-start | bytes 196616 | tf_op jit(solution)/shard_map/ppermute | solution.py:273
  46.6 31.4 %collective-permute-start.4 = (f32[4,64,256]{2,1,0:T(8,128)S(1)}, f32[4,64,256]{2,1,0:T(8,128)S(1)}, u32[]{:S(2)}, u32[]{:S(2)}) collective-permute-start(f32[4,64,256]{2,1,0:T(8,128)S(1)} %pad_maximum_fusion.near0), channel_id=1, source_target_pairs={{8,0},{16,8},{24,16},{32,24},{40,32},{48,40},{56,48},{64,56},{72,6... | collective-permute-start | bytes 786440 | tf_op jit(solution)/shard_map/ppermute | solution.py:273
  53.6 24.3 %collective-permute-start.5 = (f32[4,64,256]{2,1,0:T(8,128)S(1)}, f32[4,64,256]{2,1,0:T(8,128)S(1)}, u32[]{:S(2)}, u32[]{:S(2)}) collective-permute-start(f32[4,64,256]{2,1,0:T(8,128)S(1)} %pad_maximum_fusion.near0), channel_id=1, source_target_pairs={{16,0},{24,8},{32,16},{40,24},{48,32},{56,40},{64,48},{72,56},{80,... | collective-permute-start | bytes 786440 | tf_op jit(solution)/shard_map/ppermute | solution.py:273
  55.9 22.1 %collective-permute-start.6 = (f32[4,64,256]{2,1,0:T(8,128)S(1)}, f32[4,64,256]{2,1,0:T(8,128)S(1)}, u32[]{:S(2)}, u32[]{:S(2)}) collective-permute-start(f32[4,64,256]{2,1,0:T(8,128)S(1)} %pad_maximum_fusion.near0), channel_id=1, source_target_pairs={{24,0},{32,8},{40,16},{48,24},{56,32},{64,40},{72,48},{80,56},{88,... | collective-permute-start | bytes 786440 | tf_op jit(solution)/shard_map/ppermute | solution.py:273
  57.8 10.4 %collective-permute-start.7 = (f32[64,256]{1,0:T(8,128)S(1)}, f32[64,256]{1,0:T(8,128)S(1)}, u32[]{:S(2)}, u32[]{:S(2)}) collective-permute-start(f32[64,256]{1,0:T(8,128)S(1)} %skeleton.1), channel_id=1, source_target_pairs={{128,0},{385,1},{130,2},{387,3},{132,4},{389,5},{134,6},{391,7},{1... | collective-permute-start | bytes 196616 | tf_op jit(solution)/shard_map/ppermute | solution.py:282
  68.2 9.7 %collective-permute-start.8 = (f32[64,256]{1,0:T(8,128)S(1)}, f32[64,256]{1,0:T(8,128)S(1)}, u32[]{:S(2)}, u32[]{:S(2)}) collective-permute-start(f32[64,256]{1,0:T(8,128)S(1)} %collective-permute-done.7), channel_id=1, source_target_pairs={{128,0},{385,1},{130,2},{387,3},{132,4},{389,5},{134,6},{391,7},{1... | collective-permute-start | bytes 196616 | tf_op jit(solution)/shard_map/ppermute | solution.py:282
  79.8 28.0 %all-to-all-start.1 = ((f32[8,2,64,256]{3,2,1,0:T(8,128)}), f32[8,2,64,256]{3,2,1,0:T(8,128)S(1)}, u32[]{:S(2)}, u32[]{:S(2)}) async-start(f32[8,2,64,256]{3,2,1,0:T(8,128)} %order.1), calls=%async_computation.1 | async-start | bytes 2097152 | tf_op jit(solution)/shard_map/all_to_all | solution.py:334
  109.1 11.4 %all-to-all-start.2 = ((f32[8,32,256]{2,1,0:T(8,128)}), f32[8,32,256]{2,1,0:T(8,128)S(1)}, u32[]{:S(2)}, u32[]{:S(2)}) async-start(f32[8,32,256]{2,1,0:T(8,128)} %side.1), calls=%async_computation.2 | async-start | bytes 524288 | tf_op jit(solution)/shard_map/all_to_all | solution.py:376
